TPU v7x, 512 devices: a whole 4x8x8 slice. The times are simulated.
512 devices in a mesh: site: 16 (over z, core), col: 32 (over x, y).
Axes of the slice: x: 4, y: 8, z: 8, core: 2. Of those that a mesh axis runs over, the one named last changes fastest.
Arguments:
- state_prev: float32 [128, 128, 8192], P('site', None, 'col'), may hold values from -6 to 6
- state_cur: float32 [128, 128, 8192], P('site', None, 'col'), may hold values from -6 to 6
- occupancy: int32 [4, 128, 128], replicated, may hold values 0 or 1
- panel_order: int32 [32], replicated, may hold values from 0 to 31, each once
Outputs:
- ortho_states: float32 [128, 128, 8192], P('site', None, 'col')
- growth: float32 [2, 256], replicated
Inputs may be any that keep to these rules, and one draw needn't show every extreme that they name: panel_order holds each panel number once.
All inputs are finite; a program needn't handle non-finite values.
Results may differ from a plain program's by a relative error of at most 0.000075.
Values sent between devices are 32-bit elements; how exact they have to be, the bound alone decides.
No kernel may reach another device: no remote copies, remote signals or barrier semaphores. Data moves between devices by JAX's collectives and lax.ppermute only.
A program may use at most 64 MiB of HBM per device.

v0:
```python
import jax
import jax.numpy as jnp
from jax import lax
from jax.experimental import pallas as pl
from jax.experimental.pallas import tpu as pltpu
from jax.sharding import PartitionSpec as P

STEPS = 4
PANEL = 256
ENERGY = 0.5
RESCALE = 0.015625
BLOCK = 8

SITE = ("z", "core")
COL = ("x", "y")


def exchange(value, axis):
    size = lax.axis_size(axis)
    out = lax.all_to_all(value, axis, 0, 0, tiled=True)
    return out.reshape((size, value.shape[0] // size) + value.shape[1:])


def gather(value, axis):
    size = lax.axis_size(axis)
    copies = jnp.broadcast_to(value[None], (size,) + value.shape)
    return lax.all_to_all(copies.reshape((-1,) + value.shape[1:]), axis, 0, 0, tiled=True)


def padded_2(value):
    size, length = lax.axis_size(SITE), value.shape[0]
    up = [(i, (i + 1) % size) for i in range(size)]
    down = [(j, i) for i, j in up]
    before = lax.ppermute(value[length - 1 :], SITE, up)
    after = lax.ppermute(value[:1], SITE, down)
    return jnp.concatenate([before, value, after], axis=0)


def product(left, right):
    return jnp.dot(left, right, precision=lax.Precision.HIGHEST, preferred_element_type=jnp.float32)


def product_t(left, right):
    dims = (((0,), (0,)), ((), ()))
    return lax.dot_general(left, right, dims, precision=lax.Precision.HIGHEST, preferred_element_type=jnp.float32)


def fetch_panels(flat, panels):
    ny = lax.axis_size("y")
    received = exchange(flat, "x")
    quarters = [lax.dynamic_index_in_dim(received, panel // ny, 0, False) for panel in panels]
    rows = quarters[0].shape[0] // ny
    both = jnp.concatenate([q.reshape(ny, rows, PANEL) for q in quarters], axis=1)
    received = exchange(both.reshape(-1, PANEL), "y").reshape(ny, len(panels), rows, PANEL)
    mine = [lax.dynamic_index_in_dim(received[:, n], lax.rem(panel, ny), 0, False) for n, panel in enumerate(panels)]
    both = gather(gather(jnp.concatenate(mine, axis=0), "y"), "x")
    both = both.reshape(-1, len(panels), rows, PANEL)
    return [both[:, n].reshape(-1, PANEL) for n in range(len(panels))]


def sum_sites(value):
    value = exchange(value, "core").sum(axis=0)
    value = exchange(value, "z").sum(axis=0)
    return lax.all_gather(gather(value, "z"), "core", axis=0, tiled=True)


def split3(x):
    high = x.astype(jnp.bfloat16).astype(jnp.float32)
    rest = x - high
    mid = rest.astype(jnp.bfloat16).astype(jnp.float32)
    return high, mid, rest - mid


def outer(left, right):
    a, b, c = split3(left)
    d, e, f = split3(right)
    lhs = jnp.concatenate([a, a, b, a, c, b], axis=0).astype(jnp.bfloat16)
    rhs = jnp.concatenate([d, e, d, f, d, e], axis=0).astype(jnp.bfloat16)
    return lax.dot_general(lhs, rhs, (((0,), (0,)), ((), ())), preferred_element_type=jnp.float32)


def factor_kernel(gram_ref, out_ref):
    n = gram_ref.shape[0]
    lane = lax.broadcasted_iota(jnp.int32, (BLOCK, n), 1)
    sub = lax.broadcasted_iota(jnp.int32, (BLOCK, n), 0)
    sub1 = lax.broadcasted_iota(jnp.int32, (BLOCK, 128), 0)
    lane_all = lax.broadcasted_iota(jnp.int32, (n, n), 1)
    out_ref[...] = gram_ref[...]

    def step(j, _):
        r = pl.multiple_of(j * BLOCK, BLOCK)
        panel = out_ref[pl.ds(r, BLOCK), :]
        entry = {}
        for m in range(BLOCK):
            column = jnp.sum(jnp.where(lane == r + m, panel, 0.0), axis=1, keepdims=True)
            column = jnp.broadcast_to(column, (BLOCK, 128))
            for i in range(m, BLOCK):
                entry[i, m] = jnp.broadcast_to(column[i : i + 1], (BLOCK, 128))
        inv = {}
        for k in range(BLOCK):
            root = lax.rsqrt(entry[k, k])
            for i in range(k + 1, BLOCK):
                entry[i, k] = entry[i, k] * root
            for m in range(k + 1, BLOCK):
                for i in range(m, BLOCK):
                    entry[i, m] = entry[i, m] - entry[i, k] * entry[m, k]
            for c in range(k):
                acc = entry[k, c] * inv[c, c]
                for m in range(c + 1, k):
                    acc = acc + entry[k, m] * inv[m, c]
                inv[k, c] = -root * acc
            inv[k, k] = root
        inside = jnp.logical_and(lane >= r, lane < r + BLOCK)
        panel = jnp.where(inside, jnp.where(lane - r == sub, 1.0, 0.0), panel)
        new = None
        for k in range(BLOCK):
            column = jnp.zeros((BLOCK, 128), jnp.float32)
            for i in range(k, BLOCK):
                column = jnp.where(sub1 == i, inv[i, k], column)
            column = jnp.concatenate([column] * (n // 128), axis=1)
            term = column * jnp.broadcast_to(panel[k : k + 1], (BLOCK, n))
            new = term if new is None else new + term
        ahead = jnp.where(lane >= r + BLOCK, new, 0.0)
        inside = jnp.logical_and(lane_all >= r, lane_all < r + BLOCK)
        out_ref[...] = jnp.where(inside, 0.0, out_ref[...]) - outer(ahead, new)
        out_ref[pl.ds(r, BLOCK), :] = new
        return 0

    lax.fori_loop(0, n // BLOCK, step, 0)


def factor(gram):
    inverse = pl.pallas_call(
        factor_kernel,
        out_shape=jax.ShapeDtypeStruct(gram.shape, jnp.float32),
        in_specs=[pl.BlockSpec(memory_space=pltpu.VMEM)],
        out_specs=pl.BlockSpec(memory_space=pltpu.VMEM),
        cost_estimate=pl.CostEstimate(flops=16_000_000_000, bytes_accessed=524288, transcendentals=256),
    )(gram)
    eye = jnp.eye(gram.shape[0], dtype=bool)
    return inverse, -jnp.log(jnp.sum(jnp.where(eye, inverse, 0.0), axis=0))


def on_device(state_prev, state_cur, occupancy, panel_order):
    rows, side, width = state_cur.shape
    start = lax.axis_index(SITE) * rows
    local_mask = lax.dynamic_slice_in_dim(occupancy, start, rows, 1)
    previous, current = (state_prev, state_cur)
    for turn in range(STEPS):
        weights = local_mask[turn].astype(jnp.float32)[:, :, None]
        padded = padded_2(current)
        neighbours = padded[2:] + padded[:-2] + jnp.roll(current, 1, 1) + jnp.roll(current, -1, 1)
        previous, current = (current, weights * (ENERGY * current - neighbours - previous))
    flat = current.reshape(rows * side, width)
    first, second = panel_order[0], panel_order[1]
    a, b = fetch_panels(flat, (first, second))

    aa, ab, bb = product_t(a, a), product_t(a, b), product_t(b, b)
    gram = sum_sites(jnp.concatenate([aa, ab, bb], axis=0))
    aa, ab, bb = [gram[n * PANEL : (n + 1) * PANEL] for n in range(3)]
    a_late, b_late, gram = lax.optimization_barrier((a, b, gram))
    inner = sum_sites(jnp.concatenate([product_t(a_late, flat), product_t(b_late, flat)], axis=0))
    ax, bx = inner[:PANEL], inner[PANEL:]

    inverse_1, growth_1 = factor(aa)
    cross = product(inverse_1, ab)
    inverse_2, growth_2 = factor(bb - product_t(cross, cross))
    inner_1 = product(inverse_1, ax)
    inner_2 = product(inverse_2, bx - product_t(cross, inner_1))

    col = lax.axis_index(COL)
    is_first, is_second = col == first, col == second
    eye = jnp.eye(PANEL, dtype=jnp.float32) * (-float(side))
    zero = jnp.zeros_like(eye)
    inner_1 = jnp.where(is_first, eye, jnp.where(is_second, zero, inner_1 * RESCALE))
    inner_2 = jnp.where(is_first, zero, jnp.where(is_second, eye, inner_2 * RESCALE))
    weight_b = product_t(inverse_2, inner_2)
    weight_a = product_t(inverse_1, inner_1 - product(cross, weight_b))
    scale = jnp.where(jnp.logical_or(is_first, is_second), 0.0, RESCALE)
    both = jnp.concatenate([a, b], axis=1)
    weight = jnp.concatenate([weight_a, weight_b], axis=0)
    result = flat * scale - product(both, weight)
    return (result.reshape(rows, side, width), jnp.stack([growth_1, growth_2]))


def solution(mesh):
    mesh = jax.sharding.Mesh(mesh.devices.reshape(8, 2, 4, 8), SITE + COL)
    return jax.shard_map(
        on_device,
        mesh=mesh,
        in_specs=(P(SITE, None, COL), P(SITE, None, COL), P(), P()),
        out_specs=(P(SITE, None, COL), P()),
        check_vma=False,
    )
```

profile of v0, /device:TPU:1, one launch (start us, length us, event | category | flops | bytes accessed | tf_op | source)
XLA Modules:
  0.0 255.0 jit_solution(9396236657663776467)
XLA Ops:
  0.6 1.6 fusion.65
  2.3 3.5 %collective-permute-start.1 = (f32[1,128,256]{2,1,0:T(8,128)}, f32[1,128,256]{2,1,0:T(8,128)S(1)}, u32[]{:S(2)}, u32[]{:S(2)}) collective-permute-start(f32[1,128,256]{2,1,0:T(8,128)} %get-tuple-element.33), channel_id=1, source_target_pairs={{0,32},{32,64},{64,96},{96,128},{128,160},{160,192},{192,224},{224... | collective-permute-start | bytes 393224 | tf_op jit(solution)/shard_map/ppermute | solution.py:34
  5.8 3.4 %collective-permute-start = (f32[1,128,256]{2,1,0:T(8,128)S(1)}, f32[1,128,256]{2,1,0:T(8,128)S(1)}, u32[]{:S(2)}, u32[]{:S(2)}) collective-permute-start(f32[1,128,256]{2,1,0:T(8,128)S(1)} %get-tuple-element.32), channel_id=1, source_target_pairs={{32,0},{64,32},{96,64},{128,96},{160,128},{192,160},{224,192},{256... | collective-permute-start | bytes 393224 | tf_op jit(solution)/shard_map/ppermute | solution.py:35
  9.2 1.9 fusion.63
  13.7 3.2 %collective-permute-start.2 = (f32[1,128,256]{2,1,0:T(8,128)S(1)}, f32[1,128,256]{2,1,0:T(8,128)S(1)}, u32[]{:S(2)}, u32[]{:S(2)}) collective-permute-start(f32[1,128,256]{2,1,0:T(8,128)S(1)} %get-tuple-element.26), channel_id=1, source_target_pairs={{32,0},{64,32},{96,64},{128,96},{160,128},{192,160},{224,192},{256... | collective-permute-start | bytes 393224 | tf_op jit(solution)/shard_map/ppermute | solution.py:35
  18.8 4.4 %collective-permute-start.4 = (f32[1,128,256]{2,1,0:T(8,128)S(1)}, f32[1,128,256]{2,1,0:T(8,128)S(1)}, u32[]{:S(2)}, u32[]{:S(2)}) collective-permute-start(f32[1,128,256]{2,1,0:T(8,128)S(1)} %get-tuple-element.20), channel_id=1, source_target_pairs={{32,0},{64,32},{96,64},{128,96},{160,128},{192,160},{224,192},{256... | collective-permute-start | bytes 393224 | tf_op jit(solution)/shard_map/ppermute | solution.py:35
  24.9 4.6 %collective-permute-start.6 = (f32[1,128,256]{2,1,0:T(8,128)S(1)}, f32[1,128,256]{2,1,0:T(8,128)S(1)}, u32[]{:S(2)}, u32[]{:S(2)}) collective-permute-start(f32[1,128,256]{2,1,0:T(8,128)S(1)} %get-tuple-element.14), channel_id=1, source_target_pairs={{32,0},{64,32},{96,64},{128,96},{160,128},{192,160},{224,192},{256... | collective-permute-start | bytes 393224 | tf_op jit(solution)/shard_map/ppermute | solution.py:35
  33.0 4.1 %all-to-all-start = ((f32[4,256,256]{2,1,0:T(8,128)}), f32[4,256,256]{2,1,0:T(8,128)S(1)}, u32[]{:S(2)}, u32[]{:S(2)}) async-start(f32[4,256,256]{2,1,0:T(8,128)} %bitcast.7), calls=%async_computation | async-start | bytes 2097152 | tf_op jit(solution)/shard_map/all_to_all | solution.py:20
  43.1 5.2 %all-to-all-done = f32[4,256,256]{2,1,0:T(8,128)S(1)} async-done(((f32[4,256,256]{2,1,0:T(8,128)}), f32[4,256,256]{2,1,0:T(8,128)S(1)}, u32[]{:S(2)}, u32[]{:S(2)}) %all-to-all-start) | async-done | bytes 1048608 | tf_op jit(solution)/shard_map/all_to_all | solution.py:20
  49.2 6.8 %all-to-all-start.1 = ((f32[8,64,256]{2,1,0:T(8,128)}), f32[8,64,256]{2,1,0:T(8,128)S(1)}, u32[]{:S(2)}, u32[]{:S(2)}) async-start(f32[8,64,256]{2,1,0:T(8,128)} %pad_maximum_fusion.9), calls=%async_computation.1 | async-start | bytes 1048576 | tf_op jit(solution)/shard_map/all_to_all | solution.py:20
  56.0 12.1 %all-to-all-done.1 = f32[8,64,256]{2,1,0:T(8,128)S(1)} async-done(((f32[8,64,256]{2,1,0:T(8,128)}), f32[8,64,256]{2,1,0:T(8,128)S(1)}, u32[]{:S(2)}, u32[]{:S(2)}) %all-to-all-start.1) | async-done | bytes 524320 | tf_op jit(solution)/shard_map/all_to_all | solution.py:20
  68.2 14.7 %all_to_all.81 = f32[8,64,256]{2,1,0:T(8,128)S(1)} all-to-all(f32[8,64,256]{2,1,0:T(8,128)S(1)} %broadcast_in_dim.12), channel_id=1, replica_groups=mesh['z'=8,'core'=2,'x'=4,'y'=8] {'y'}, dimensions={0} | all-to-all | bytes 1048576 | tf_op jit(solution)/shard_map/all_to_all | solution.py:27
  83.1 21.3 %all_to_all.82 = f32[4,512,256]{2,1,0:T(8,128)S(1)} all-to-all(f32[4,512,256]{2,1,0:T(8,128)S(1)} %broadcast_in_dim.14), channel_id=1, replica_groups=mesh['z'=8,'core'=2,'x'=4,'y'=8] {'x'}, dimensions={0} | all-to-all | bytes 4194304 | tf_op jit(solution)/shard_map/all_to_all | solution.py:27
  104.4 1.8 convolution_bitcast_fusion
  106.3 1.8 convolution_bitcast_fusion.1
  108.1 1.8 convolution_bitcast_fusion.2
  110.0 12.4 %all_to_all.83 = f32[2,384,256]{2,1,0:T(8,128)S(1)} all-to-all(f32[2,384,256]{2,1,0:T(8,128)S(1)} %bitcast.80), channel_id=1, replica_groups=mesh['z'=8,'core'=2,'x'=4,'y'=8] {'core'}, dimensions={0} | all-to-all | bytes 1572864 | tf_op jit(solution)/shard_map/all_to_all | solution.py:20
  122.5 35.2 %all_to_all.84 = f32[8,48,256]{2,1,0:T(8,128)S(1)} all-to-all(f32[8,48,256]{2,1,0:T(8,128)S(1)} %bitcast.85), channel_id=1, replica_groups=mesh['z'=8,'core'=2,'x'=4,'y'=8] {'z'}, dimensions={0} | all-to-all | bytes 786432 | tf_op jit(solution)/shard_map/all_to_all | solution.py:20
  158.5 3.5 %all-to-all-start.6 = ((f32[8,48,256]{2,1,0:T(8,128)}), f32[8,48,256]{2,1,0:T(8,128)S(1)}, u32[]{:S(2)}, u32[]{:S(2)}) async-start(f32[8,48,256]{2,1,0:T(8,128)} %broadcast_in_dim.15), calls=%async_computation.6 | async-start | bytes 786432 | tf_op jit(solution)/shard_map/all_to_all | solution.py:27
  163.3 1.7 fusion.53
  165.0 9.2 %all-to-all-done.6 = f32[8,48,256]{2,1,0:T(8,128)S(1)} async-done(((f32[8,48,256]{2,1,0:T(8,128)}), f32[8,48,256]{2,1,0:T(8,128)S(1)}, u32[]{:S(2)}, u32[]{:S(2)}) %all-to-all-start.6) | async-done | bytes 393248 | tf_op jit(solution)/shard_map/all_to_all | solution.py:27
  174.2 5.5 %all_gather.6 = f32[768,256]{1,0:T(8,128)S(1)} all-gather(f32[384,256]{1,0:T(8,128)S(1)} %bitcast.84), channel_id=1, replica_groups=mesh['z'=8,'core'=2,'x'=4,'y'=8] {'core'}, dimensions={0}, use_global_device_ids=true | all-gather | bytes 1179648 | tf_op jit(solution)/shard_map/all_gather | solution.py:64
  180.4 13.8 %shard_map.59 = f32[256,256]{1,0:T(8,128)} custom-call(f32[256,256]{1,0:T(8,128)} %slice.222.gram_ref), custom_call_target="tpu_custom_call" | custom-call | flops 16000000000 | bytes 524288 | tf_op jit(solution)/shard_map/pallas_call | solution.py:133
  196.8 3.0 %fusion.69 = f32[256,256]{1,0:T(8,128)S(1)} fusion(f32[1024,256]{1,0:T(8,128)S(1)} %bitcast.74, f32[1024,256]{1,0:T(8,128)} %bitcast.4), kind=kOutput, calls=%fused_computation.101 | convolution fusion | flops 805306368 | bytes 2359296 | tf_op jit(solution)/shard_map/dot_general | solution.py:45
  199.8 3.0 %fusion.68 = f32[256,256]{1,0:T(8,128)S(1)} fusion(f32[1024,256]{1,0:T(8,128)S(1)} %bitcast.72, f32[1024,256]{1,0:T(8,128)} %bitcast.4), kind=kOutput, calls=%fused_computation.100 | convolution fusion | flops 805306368 | bytes 2359296 | tf_op jit(solution)/shard_map/dot_general | solution.py:45
  202.9 4.2 %all_to_all.85 = f32[2,256,256]{2,1,0:T(8,128)S(1)} all-to-all(f32[2,256,256]{2,1,0:T(8,128)S(1)} %bitcast.83), channel_id=1, replica_groups=mesh['z'=8,'core'=2,'x'=4,'y'=8] {'core'}, dimensions={0} | all-to-all | bytes 1048576 | tf_op jit(solution)/shard_map/all_to_all | solution.py:20
  207.8 3.4 %all-to-all-start.8 = ((f32[8,32,256]{2,1,0:T(8,128)}), f32[8,32,256]{2,1,0:T(8,128)S(1)}, u32[]{:S(2)}, u32[]{:S(2)}) async-start(f32[8,32,256]{2,1,0:T(8,128)} %bitcast.26), calls=%async_computation.8 | async-start | bytes 524288 | tf_op jit(solution)/shard_map/all_to_all | solution.py:20
  211.2 13.8 %shard_map.60 = f32[256,256]{1,0:T(8,128)} custom-call(f32[256,256]{1,0:T(8,128)} %convolution_subtract_fusion.2.gram_ref), custom_call_target="tpu_custom_call" | custom-call | flops 16000000000 | bytes 524288 | tf_op jit(solution)/shard_map/pallas_call | solution.py:133
  226.9 6.6 %all-to-all-start.9 = ((f32[8,32,256]{2,1,0:T(8,128)}), f32[8,32,256]{2,1,0:T(8,128)S(1)}, u32[]{:S(2)}, u32[]{:S(2)}) async-start(f32[8,32,256]{2,1,0:T(8,128)} %broadcast_in_dim.16), calls=%async_computation.9 | async-start | bytes 524288 | tf_op jit(solution)/shard_map/all_to_all | solution.py:27
  234.1 9.8 %all-to-all-done.9 = f32[8,32,256]{2,1,0:T(8,128)S(1)} async-done(((f32[8,32,256]{2,1,0:T(8,128)}), f32[8,32,256]{2,1,0:T(8,128)S(1)}, u32[]{:S(2)}, u32[]{:S(2)}) %all-to-all-start.9) | async-done | bytes 262176 | tf_op jit(solution)/shard_map/all_to_all | solution.py:27
  243.8 4.2 %all_gather.7 = f32[512,256]{1,0:T(8,128)S(1)} all-gather(f32[256,256]{1,0:T(8,128)S(1)} %bitcast.87), channel_id=1, replica_groups=mesh['z'=8,'core'=2,'x'=4,'y'=8] {'core'}, dimensions={0}, use_global_device_ids=true | all-gather | bytes 786432 | tf_op jit(solution)/shard_map/all_gather | solution.py:64
  251.0 4.0 %fusion.4 = f32[1024,256]{1,0:T(8,128)} fusion(f32[1024,256]{1,0:T(8,128)S(1)} %bitcast.75, f32[1024,256]{1,0:T(8,128)S(1)} %bitcast.73, f32[1024,256]{1,0:T(8,128)} %bitcast.4, f32[256,256]{1,0:T(8,128)S(1)} %fusion.70, f32[256,256]{1,0:T(8,128)S(1)} %fusion.71, f32[]{:T(128)S(6)} %select_n.59), kind=kOutput, calls=%fused_computation.4 | convolution fusion | flops 1611792384 | bytes 4718596 | tf_op jit(solution)/shard_map/dot_general | solution.py:40
  (67 shorter events, 21.7 us)
Async XLA Ops:
  2.3 9.6 %collective-permute-start.1 = (f32[1,128,256]{2,1,0:T(8,128)}, f32[1,128,256]{2,1,0:T(8,128)S(1)}, u32[]{:S(2)}, u32[]{:S(2)}) collective-permute-start(f32[1,128,256]{2,1,0:T(8,128)} %get-tuple-element.33), channel_id=1, source_target_pairs={{0,32},{32,64},{64,96},{96,128},{128,160},{160,192},{192,224},{224... | collective-permute-start | bytes 393224 | tf_op jit(solution)/shard_map/ppermute | solution.py:34
  5.8 5.3 %copy-start = (f32[8,128,256]{2,1,0:T(8,128)S(1)}, f32[8,128,256]{2,1,0:T(8,128)}, u32[]{:S(2)}) copy-start(f32[8,128,256]{2,1,0:T(8,128)} %param.5) | copy-start | bytes 3145732
  5.8 6.1 %collective-permute-start = (f32[1,128,256]{2,1,0:T(8,128)S(1)}, f32[1,128,256]{2,1,0:T(8,128)S(1)}, u32[]{:S(2)}, u32[]{:S(2)}) collective-permute-start(f32[1,128,256]{2,1,0:T(8,128)S(1)} %get-tuple-element.32), channel_id=1, source_target_pairs={{32,0},{64,32},{96,64},{128,96},{160,128},{192,160},{224,192},{256... | collective-permute-start | bytes 393224 | tf_op jit(solution)/shard_map/ppermute | solution.py:35
  13.7 4.1 %collective-permute-start.3 = (f32[1,128,256]{2,1,0:T(8,128)S(1)}, f32[1,128,256]{2,1,0:T(8,128)S(1)}, u32[]{:S(2)}, u32[]{:S(2)}) collective-permute-start(f32[1,128,256]{2,1,0:T(8,128)S(1)} %get-tuple-element.27), channel_id=1, source_target_pairs={{0,32},{32,64},{64,96},{96,128},{128,160},{160,192},{192,224},{224... | collective-permute-start | bytes 393224 | tf_op jit(solution)/shard_map/ppermute | solution.py:34
  13.7 4.4 %collective-permute-start.2 = (f32[1,128,256]{2,1,0:T(8,128)S(1)}, f32[1,128,256]{2,1,0:T(8,128)S(1)}, u32[]{:S(2)}, u32[]{:S(2)}) collective-permute-start(f32[1,128,256]{2,1,0:T(8,128)S(1)} %get-tuple-element.26), channel_id=1, source_target_pairs={{32,0},{64,32},{96,64},{128,96},{160,128},{192,160},{224,192},{256... | collective-permute-start | bytes 393224 | tf_op jit(solution)/shard_map/ppermute | solution.py:35
  18.8 5.3 %collective-permute-start.5 = (f32[1,128,256]{2,1,0:T(8,128)S(1)}, f32[1,128,256]{2,1,0:T(8,128)S(1)}, u32[]{:S(2)}, u32[]{:S(2)}) collective-permute-start(f32[1,128,256]{2,1,0:T(8,128)S(1)} %get-tuple-element.21), channel_id=1, source_target_pairs={{0,32},{32,64},{64,96},{96,128},{128,160},{160,192},{192,224},{224... | collective-permute-start | bytes 393224 | tf_op jit(solution)/shard_map/ppermute | solution.py:34
  18.8 5.4 %collective-permute-start.4 = (f32[1,128,256]{2,1,0:T(8,128)S(1)}, f32[1,128,256]{2,1,0:T(8,128)S(1)}, u32[]{:S(2)}, u32[]{:S(2)}) collective-permute-start(f32[1,128,256]{2,1,0:T(8,128)S(1)} %get-tuple-element.20), channel_id=1, source_target_pairs={{32,0},{64,32},{96,64},{128,96},{160,128},{192,160},{224,192},{256... | collective-permute-start | bytes 393224 | tf_op jit(solution)/shard_map/ppermute | solution.py:35
  24.9 5.5 %collective-permute-start.7 = (f32[1,128,256]{2,1,0:T(8,128)S(1)}, f32[1,128,256]{2,1,0:T(8,128)S(1)}, u32[]{:S(2)}, u32[]{:S(2)}) collective-permute-start(f32[1,128,256]{2,1,0:T(8,128)S(1)} %get-tuple-element.15), channel_id=1, source_target_pairs={{0,32},{32,64},{64,96},{96,128},{128,160},{160,192},{192,224},{224... | collective-permute-start | bytes 393224 | tf_op jit(solution)/shard_map/ppermute | solution.py:34
  24.9 6.8 %collective-permute-start.6 = (f32[1,128,256]{2,1,0:T(8,128)S(1)}, f32[1,128,256]{2,1,0:T(8,128)S(1)}, u32[]{:S(2)}, u32[]{:S(2)}) collective-permute-start(f32[1,128,256]{2,1,0:T(8,128)S(1)} %get-tuple-element.14), channel_id=1, source_target_pairs={{32,0},{64,32},{96,64},{128,96},{160,128},{192,160},{224,192},{256... | collective-permute-start | bytes 393224 | tf_op jit(solution)/shard_map/ppermute | solution.py:35
  33.0 4.1 %copy-start.4 = (s32[32]{0:T(128)S(1)}, s32[32]{0:T(128)}, u32[]{:S(2)}) copy-start(s32[32]{0:T(128)} %param.7) | copy-start | bytes 388
  33.0 15.3 %all-to-all-start = ((f32[4,256,256]{2,1,0:T(8,128)}), f32[4,256,256]{2,1,0:T(8,128)S(1)}, u32[]{:S(2)}, u32[]{:S(2)}) async-start(f32[4,256,256]{2,1,0:T(8,128)} %bitcast.7), calls=%async_computation | async-start | bytes 2097152 | tf_op jit(solution)/shard_map/all_to_all | solution.py:20
  49.2 18.9 %all-to-all-start.1 = ((f32[8,64,256]{2,1,0:T(8,128)}), f32[8,64,256]{2,1,0:T(8,128)S(1)}, u32[]{:S(2)}, u32[]{:S(2)}) async-start(f32[8,64,256]{2,1,0:T(8,128)} %pad_maximum_fusion.9), calls=%async_computation.1 | async-start | bytes 1048576 | tf_op jit(solution)/shard_map/all_to_all | solution.py:20
  104.4 3.7 %copy-start.1 = (f32[4,512,256]{2,1,0:T(8,128)}, f32[4,512,256]{2,1,0:T(8,128)S(1)}, u32[]{:S(2)}) copy-start(f32[4,512,256]{2,1,0:T(8,128)S(1)} %all_to_all.82) | copy-start | bytes 6291460
  158.5 15.7 %all-to-all-start.6 = ((f32[8,48,256]{2,1,0:T(8,128)}), f32[8,48,256]{2,1,0:T(8,128)S(1)}, u32[]{:S(2)}, u32[]{:S(2)}) async-start(f32[8,48,256]{2,1,0:T(8,128)} %broadcast_in_dim.15), calls=%async_computation.6 | async-start | bytes 786432 | tf_op jit(solution)/shard_map/all_to_all | solution.py:27
  207.8 18.3 %all-to-all-start.8 = ((f32[8,32,256]{2,1,0:T(8,128)}), f32[8,32,256]{2,1,0:T(8,128)S(1)}, u32[]{:S(2)}, u32[]{:S(2)}) async-start(f32[8,32,256]{2,1,0:T(8,128)} %bitcast.26), calls=%async_computation.8 | async-start | bytes 524288 | tf_op jit(solution)/shard_map/all_to_all | solution.py:20
  211.2 22.2 %copy-start.2 = (f32[256,256]{1,0:T(8,128)S(1)}, f32[256,256]{1,0:T(8,128)}, u32[]{:S(2)}) copy-start(f32[256,256]{1,0:T(8,128)} %shard_map.59) | copy-start | bytes 786436
  225.0 24.0 %copy-start.3 = (f32[256,256]{1,0:T(8,128)S(1)}, f32[256,256]{1,0:T(8,128)}, u32[]{:S(2)}) copy-start(f32[256,256]{1,0:T(8,128)} %shard_map.60) | copy-start | bytes 786436
  226.9 17.0 %all-to-all-start.9 = ((f32[8,32,256]{2,1,0:T(8,128)}), f32[8,32,256]{2,1,0:T(8,128)S(1)}, u32[]{:S(2)}, u32[]{:S(2)}) async-start(f32[8,32,256]{2,1,0:T(8,128)} %broadcast_in_dim.16), calls=%async_computation.9 | async-start | bytes 524288 | tf_op jit(solution)/shard_map/all_to_all | solution.py:27
where the time goes:
time: 256 us; the launch traced here: 255 us
  blocking collectives  97.5 us (38%)
  starting transfers between devices  43.6 us (17%)
  waiting for transfers between devices  40.5 us (16%)
  Pallas kernels  27.5 us (11%)
  matrix products  21.1 us (8%)
  local copies, waits for them, and re-layouts  9.09 us (4%)
  other arithmetic  7.99 us (3%)
  between operations  7.65 us (3%)
    all_to_all x3, blocking collectives, exchange(): out = lax.all_to_all(value, axis, 0, 0, tiled=True)  51.8 us
    all_to_all x2, blocking collectives, gather(): lax.all_to_all(copies.reshape((-1,) + value.shape[1:]), axis, 0, 0, tiled...  36 us
    pallas_call x2, Pallas kernels, factor(): pl.pallas_call(factor_kernel, out_shape=jax.ShapeDtypeStruct(gram.shape,...  27.5 us
    all_to_all x2, waiting for transfers between devices, gather(): lax.all_to_all(copies.reshape((-1,) + value.shape[1:]), axis, 0, 0, tiled...  19 us
    all_to_all x3, waiting for transfers between devices, exchange(): out = lax.all_to_all(value, axis, 0, 0, tiled=True)  17.3 us
    ppermute x4, starting transfers between devices, padded_2(): after = lax.ppermute(value[:1], SITE, down)  15.7 us
    dot_general x9, matrix products, product_t(): lax.dot_general(left, right, dims, precision=lax.Precision.HIGHEST, prefe...  14.7 us
    all_to_all x3, starting transfers between devices, exchange(): out = lax.all_to_all(value, axis, 0, 0, tiled=True)  14.4 us
  transfers between devices with their start and end apart: 13, of which 10 were waited for; matrix products, arithmetic and copies ran while one was open for 3% of the time, Pallas kernels for 5%

commit v1 on v0

--- a/solution.py
+++ b/solution.py
@@ -46,22 +46,11 @@
 
 
 def fetch_panels(flat, panels):
-    ny = lax.axis_size("y")
-    received = exchange(flat, "x")
-    quarters = [lax.dynamic_index_in_dim(received, panel // ny, 0, False) for panel in panels]
-    rows = quarters[0].shape[0] // ny
-    both = jnp.concatenate([q.reshape(ny, rows, PANEL) for q in quarters], axis=1)
-    received = exchange(both.reshape(-1, PANEL), "y").reshape(ny, len(panels), rows, PANEL)
-    mine = [lax.dynamic_index_in_dim(received[:, n], lax.rem(panel, ny), 0, False) for n, panel in enumerate(panels)]
-    both = gather(gather(jnp.concatenate(mine, axis=0), "y"), "x")
-    both = both.reshape(-1, len(panels), rows, PANEL)
+    received = exchange(flat, COL)
+    mine = jnp.concatenate([lax.dynamic_index_in_dim(received, panel, 0, False) for panel in panels], axis=0)
+    both = gather(gather(mine, "y"), "x")
+    both = both.reshape(-1, len(panels), received.shape[1], PANEL)
     return [both[:, n].reshape(-1, PANEL) for n in range(len(panels))]
-
-
-def sum_sites(value):
-    value = exchange(value, "core").sum(axis=0)
-    value = exchange(value, "z").sum(axis=0)
-    return lax.all_gather(gather(value, "z"), "core", axis=0, tiled=True)
 
 
 def split3(x):
@@ -130,15 +119,18 @@
 
 
 def factor(gram):
-    inverse = pl.pallas_call(
+    return pl.pallas_call(
         factor_kernel,
         out_shape=jax.ShapeDtypeStruct(gram.shape, jnp.float32),
         in_specs=[pl.BlockSpec(memory_space=pltpu.VMEM)],
         out_specs=pl.BlockSpec(memory_space=pltpu.VMEM),
         cost_estimate=pl.CostEstimate(flops=16_000_000_000, bytes_accessed=524288, transcendentals=256),
     )(gram)
-    eye = jnp.eye(gram.shape[0], dtype=bool)
-    return inverse, -jnp.log(jnp.sum(jnp.where(eye, inverse, 0.0), axis=0))
+
+
+def growth(inverse):
+    eye = jnp.eye(inverse.shape[0], dtype=bool)
+    return -jnp.log(jnp.sum(jnp.where(eye, inverse, 0.0), axis=0))
 
 
 def on_device(state_prev, state_cur, occupancy, panel_order):
@@ -155,16 +147,27 @@
     first, second = panel_order[0], panel_order[1]
     a, b = fetch_panels(flat, (first, second))
 
+    half = PANEL // 2
     aa, ab, bb = product_t(a, a), product_t(a, b), product_t(b, b)
-    gram = sum_sites(jnp.concatenate([aa, ab, bb], axis=0))
-    aa, ab, bb = [gram[n * PANEL : (n + 1) * PANEL] for n in range(3)]
+    corners = jnp.concatenate([aa[half:, half:], bb[half:, half:]], axis=1)
+    gram = jnp.concatenate([aa[:half], bb[:half], corners, ab], axis=0)
+    gram = exchange(gram, "core").sum(axis=0)
     a_late, b_late, gram = lax.optimization_barrier((a, b, gram))
-    inner = sum_sites(jnp.concatenate([product_t(a_late, flat), product_t(b_late, flat)], axis=0))
+    inner = jnp.concatenate([product_t(a_late, flat), product_t(b_late, flat)], axis=0)
+    gram = gather(exchange(gram, "z").sum(axis=0), "z")
+    inner = exchange(inner, "core").sum(axis=0)
+    inner, gram = lax.optimization_barrier((inner, lax.all_gather(gram, "core", axis=0, tiled=True)))
+    inner = exchange(inner, "z").sum(axis=0)
+    corners, ab = gram[PANEL : PANEL + half], gram[PANEL + half :]
+    unread = jnp.zeros((half, half), jnp.float32)
+    aa = jnp.concatenate([gram[:half], jnp.concatenate([unread, corners[:, :half]], axis=1)], axis=0)
+    bb = jnp.concatenate([gram[half:PANEL], jnp.concatenate([unread, corners[:, half:]], axis=1)], axis=0)
+
+    inner, inverse_1 = lax.optimization_barrier((inner, factor(aa)))
+    cross = product(inverse_1, ab)
+    inner, inverse_2 = lax.optimization_barrier((gather(inner, "z"), factor(bb - product_t(cross, cross))))
+    inner = lax.all_gather(inner, "core", axis=0, tiled=True)
     ax, bx = inner[:PANEL], inner[PANEL:]
-
-    inverse_1, growth_1 = factor(aa)
-    cross = product(inverse_1, ab)
-    inverse_2, growth_2 = factor(bb - product_t(cross, cross))
     inner_1 = product(inverse_1, ax)
     inner_2 = product(inverse_2, bx - product_t(cross, inner_1))
 
@@ -180,7 +183,7 @@
     both = jnp.concatenate([a, b], axis=1)
     weight = jnp.concatenate([weight_a, weight_b], axis=0)
     result = flat * scale - product(both, weight)
-    return (result.reshape(rows, side, width), jnp.stack([growth_1, growth_2]))
+    return (result.reshape(rows, side, width), jnp.stack([growth(inverse_1), growth(inverse_2)]))
 
 
 def solution(mesh):

time: 256 us -> 232 us (0.906)
  blocking collectives: 97.5 us -> 58.8 us
  starting transfers between devices: 43.6 us -> 57.4 us
    all_to_all x3 -> x1, blocking collectives: 51.8 us -> 11.4 us  [exchange(): out = lax.all_to_all(value, axis, 0, 0, tiled=True)]
    all_to_all x3 -> x4, starting transfers between devices: 14.4 us -> 28.2 us  [exchange(): out = lax.all_to_all(value, axis, 0, 0, tiled=True)]
    all_to_all x2, waiting for transfers between devices: 19 us -> 11.6 us  [gather(): lax.all_to_all(copies.reshape((-1,) + value.shape[1:]), axis, 0, 0, tiled...]
    all_to_all x3 -> x4, waiting for transfers between devices: 17.3 us -> 24.3 us  [exchange(): out = lax.all_to_all(value, axis, 0, 0, tiled=True)]
    all_to_all x2, blocking collectives: 36 us -> 42.3 us  [gather(): lax.all_to_all(copies.reshape((-1,) + value.shape[1:]), axis, 0, 0, tiled...]
    all_gather x2, blocking collectives: 9.68 us -> 5.1 us  [the longest x1 2.74 us: on_device(): inner = lax.all_gather(inner, 'core', axis=0, tiled=True)]
    ppermute x4, starting transfers between devices: 15.7 us -> 19.2 us  [padded_2(): after = lax.ppermute(value[:1], SITE, down)]
    ppermute x4, starting transfers between devices: 3.54 us -> 0.01 us  [padded_2(): before = lax.ppermute(value[length - 1:], SITE, up)]
  transfers between devices with their start and end apart: 13 -> 14, of which waited for: 10 -> 11; matrix products, arithmetic and copies ran while one was open for 3% -> 6% of each run, Pallas kernels for 5% -> 12%
where the time goes in v1:
time: 232 us; the launch traced here: 231 us
  blocking collectives  58.8 us (25%)
  starting transfers between devices  57.4 us (25%)
  waiting for transfers between devices  42.8 us (18%)
  Pallas kernels  27.5 us (12%)
  matrix products  21.4 us (9%)
  other arithmetic  9.37 us (4%)
  local copies, waits for them, and re-layouts  7.7 us (3%)
  between operations  6.1 us (3%)
    all_to_all x2, blocking collectives, gather(): lax.all_to_all(copies.reshape((-1,) + value.shape[1:]), axis, 0, 0, tiled...  42.3 us
    all_to_all x4, starting transfers between devices, exchange(): out = lax.all_to_all(value, axis, 0, 0, tiled=True)  28.2 us
    pallas_call x2, Pallas kernels, factor(): pl.pallas_call(factor_kernel, out_shape=jax.ShapeDtypeStruct(gram.shape,...  27.5 us
    all_to_all x4, waiting for transfers between devices, exchange(): out = lax.all_to_all(value, axis, 0, 0, tiled=True)  24.3 us
    ppermute x4, starting transfers between devices, padded_2(): after = lax.ppermute(value[:1], SITE, down)  19.2 us
    dot_general x9, matrix products, product_t(): lax.dot_general(left, right, dims, precision=lax.Precision.HIGHEST, prefe...  14.9 us
    all_to_all x2, waiting for transfers between devices, gather(): lax.all_to_all(copies.reshape((-1,) + value.shape[1:]), axis, 0, 0, tiled...  11.6 us
    all_to_all x1, blocking collectives, exchange(): out = lax.all_to_all(value, axis, 0, 0, tiled=True)  11.4 us
  transfers between devices with their start and end apart: 14, of which 11 were waited for; matrix products, arithmetic and copies ran while one was open for 6% of the time, Pallas kernels for 12%

profile of v1, /device:TPU:1, one launch (start us, length us, event | category | flops | bytes accessed | tf_op | source)
XLA Modules:
  0.0 231.1 jit_solution(15935609713133954353)
XLA Ops:
  0.6 1.6 fusion.65
  2.3 6.9 %collective-permute-start = (f32[1,128,256]{2,1,0:T(8,128)}, f32[1,128,256]{2,1,0:T(8,128)S(1)}, u32[]{:S(2)}, u32[]{:S(2)}) collective-permute-start(f32[1,128,256]{2,1,0:T(8,128)} %get-tuple-element.46), channel_id=1, source_target_pairs={{32,0},{64,32},{96,64},{128,96},{160,128},{192,160},{224,192},{256... | collective-permute-start | bytes 393224 | tf_op jit(solution)/shard_map/ppermute | solution.py:35
  9.2 2.1 fusion.63
  13.1 1.6 fusion.32
  14.9 4.8 %collective-permute-start.2 = (f32[1,128,256]{2,1,0:T(8,128)S(1)}, f32[1,128,256]{2,1,0:T(8,128)S(1)}, u32[]{:S(2)}, u32[]{:S(2)}) collective-permute-start(f32[1,128,256]{2,1,0:T(8,128)S(1)} %get-tuple-element.40), channel_id=1, source_target_pairs={{32,0},{64,32},{96,64},{128,96},{160,128},{192,160},{224,192},{256... | collective-permute-start | bytes 393224 | tf_op jit(solution)/shard_map/ppermute | solution.py:35
  22.3 3.9 %collective-permute-start.4 = (f32[1,128,256]{2,1,0:T(8,128)S(1)}, f32[1,128,256]{2,1,0:T(8,128)S(1)}, u32[]{:S(2)}, u32[]{:S(2)}) collective-permute-start(f32[1,128,256]{2,1,0:T(8,128)S(1)} %get-tuple-element.34), channel_id=1, source_target_pairs={{32,0},{64,32},{96,64},{128,96},{160,128},{192,160},{224,192},{256... | collective-permute-start | bytes 393224 | tf_op jit(solution)/shard_map/ppermute | solution.py:35
  28.8 3.7 %collective-permute-start.6 = (f32[1,128,256]{2,1,0:T(8,128)S(1)}, f32[1,128,256]{2,1,0:T(8,128)S(1)}, u32[]{:S(2)}, u32[]{:S(2)}) collective-permute-start(f32[1,128,256]{2,1,0:T(8,128)S(1)} %get-tuple-element.28), channel_id=1, source_target_pairs={{32,0},{64,32},{96,64},{128,96},{160,128},{192,160},{224,192},{256... | collective-permute-start | bytes 393224 | tf_op jit(solution)/shard_map/ppermute | solution.py:35
  32.5 1.4 collective-permute-done.6
  34.4 1.4 fusion.14
  35.8 9.8 %all-to-all-start = ((f32[32,32,256]{2,1,0:T(8,128)}), f32[32,32,256]{2,1,0:T(8,128)S(1)}, u32[]{:S(2)}, u32[]{:S(2)}) async-start(f32[32,32,256]{2,1,0:T(8,128)} %bitcast.7), calls=%async_computation | async-start | bytes 2097152 | tf_op jit(solution)/shard_map/all_to_all | solution.py:20
  50.0 16.3 %all-to-all-done = f32[32,32,256]{2,1,0:T(8,128)S(1)} async-done(((f32[32,32,256]{2,1,0:T(8,128)}), f32[32,32,256]{2,1,0:T(8,128)S(1)}, u32[]{:S(2)}, u32[]{:S(2)}) %all-to-all-start) | async-done | bytes 1048608 | tf_op jit(solution)/shard_map/all_to_all | solution.py:20
  66.4 18.7 %all_to_all.75 = f32[8,64,256]{2,1,0:T(8,128)S(1)} all-to-all(f32[8,64,256]{2,1,0:T(8,128)S(1)} %broadcast_in_dim.12), channel_id=1, replica_groups=mesh['z'=8,'core'=2,'x'=4,'y'=8] {'y'}, dimensions={0} | all-to-all | bytes 1048576 | tf_op jit(solution)/shard_map/all_to_all | solution.py:27
  85.3 23.6 %all_to_all.76 = f32[4,512,256]{2,1,0:T(8,128)S(1)} all-to-all(f32[4,512,256]{2,1,0:T(8,128)S(1)} %broadcast_in_dim.14), channel_id=1, replica_groups=mesh['z'=8,'core'=2,'x'=4,'y'=8] {'x'}, dimensions={0} | all-to-all | bytes 4194304 | tf_op jit(solution)/shard_map/all_to_all | solution.py:27
  108.8 1.9 convolution_bitcast_fusion.2
  110.8 1.9 convolution_bitcast_fusion.1
  112.8 1.9 convolution_bitcast_fusion
  115.6 11.4 %all_to_all.77 = f32[2,320,256]{2,1,0:T(8,128)S(1)} all-to-all(f32[2,320,256]{2,1,0:T(8,128)S(1)} %bitcast.77), channel_id=1, replica_groups=mesh['z'=8,'core'=2,'x'=4,'y'=8] {'core'}, dimensions={0} | all-to-all | bytes 1310720 | tf_op jit(solution)/shard_map/all_to_all | solution.py:20
  127.8 10.9 %all-to-all-start.5 = ((f32[8,40,256]{2,1,0:T(8,128)}), f32[8,40,256]{2,1,0:T(8,128)S(1)}, u32[]{:S(2)}, u32[]{:S(2)}) async-start(f32[8,40,256]{2,1,0:T(8,128)} %bitcast.21), calls=%async_computation.5 | async-start | bytes 655360 | tf_op jit(solution)/shard_map/all_to_all | solution.py:20
  138.7 3.0 %fusion.69 = f32[256,256]{1,0:T(8,128)S(1)} fusion(f32[1024,256]{1,0:T(8,128)S(1)} %bitcast.69, f32[1024,256]{1,0:T(8,128)} %bitcast.4), kind=kOutput, calls=%fused_computation.101 | convolution fusion | flops 805306368 | bytes 2359296 | tf_op jit(solution)/shard_map/dot_general | solution.py:45
  141.7 3.0 %fusion.70 = f32[256,256]{1,0:T(8,128)S(1)} fusion(f32[1024,256]{1,0:T(8,128)S(1)} %bitcast.71, f32[1024,256]{1,0:T(8,128)} %bitcast.4), kind=kOutput, calls=%fused_computation.102 | convolution fusion | flops 805306368 | bytes 2359296 | tf_op jit(solution)/shard_map/dot_general | solution.py:45
  145.6 6.7 %all-to-all-done.5 = f32[8,40,256]{2,1,0:T(8,128)S(1)} async-done(((f32[8,40,256]{2,1,0:T(8,128)}), f32[8,40,256]{2,1,0:T(8,128)S(1)}, u32[]{:S(2)}, u32[]{:S(2)}) %all-to-all-start.5) | async-done | bytes 327712 | tf_op jit(solution)/shard_map/all_to_all | solution.py:20
  152.3 4.1 %all-to-all-start.4 = ((f32[2,256,256]{2,1,0:T(8,128)}), f32[2,256,256]{2,1,0:T(8,128)S(1)}, u32[]{:S(2)}, u32[]{:S(2)}) async-start(f32[2,256,256]{2,1,0:T(8,128)} %bitcast.20), calls=%async_computation.4 | async-start | bytes 1048576 | tf_op jit(solution)/shard_map/all_to_all | solution.py:20
  156.4 1.3 all-to-all-done.4
  158.5 3.4 %all-to-all-start.6 = ((f32[8,40,256]{2,1,0:T(8,128)}), f32[8,40,256]{2,1,0:T(8,128)S(1)}, u32[]{:S(2)}, u32[]{:S(2)}) async-start(f32[8,40,256]{2,1,0:T(8,128)} %broadcast_in_dim.15), calls=%async_computation.6 | async-start | bytes 655360 | tf_op jit(solution)/shard_map/all_to_all | solution.py:27
  164.0 11.6 %all-to-all-done.6 = f32[8,40,256]{2,1,0:T(8,128)S(1)} async-done(((f32[8,40,256]{2,1,0:T(8,128)}), f32[8,40,256]{2,1,0:T(8,128)S(1)}, u32[]{:S(2)}, u32[]{:S(2)}) %all-to-all-start.6) | async-done | bytes 327712 | tf_op jit(solution)/shard_map/all_to_all | solution.py:27
  175.6 2.4 %all_gather.6 = f32[640,256]{1,0:T(8,128)S(1)} all-gather(f32[320,256]{1,0:T(8,128)S(1)} %bitcast.79), channel_id=1, replica_groups=mesh['z'=8,'core'=2,'x'=4,'y'=8] {'core'}, dimensions={0}, use_global_device_ids=true | all-gather | bytes 983040 | tf_op jit(solution)/shard_map/all_gather | solution.py:159
  178.0 3.4 %all-to-all-start.7 = ((f32[8,32,256]{2,1,0:T(8,128)}), f32[8,32,256]{2,1,0:T(8,128)S(1)}, u32[]{:S(2)}, u32[]{:S(2)}) async-start(f32[8,32,256]{2,1,0:T(8,128)} %bitcast.82), calls=%async_computation.7 | async-start | bytes 524288 | tf_op jit(solution)/shard_map/all_to_all | solution.py:20
  182.2 13.7 %shard_map.59 = f32[256,256]{1,0:T(8,128)} custom-call(f32[256,256]{1,0:T(8,128)} %select_maximum_fusion.1.gram_ref), custom_call_target="tpu_custom_call" | custom-call | flops 16000000000 | bytes 524288 | tf_op jit(solution)/shard_map/pallas_call | solution.py:122
  198.0 6.6 %all-to-all-start.8 = ((f32[8,32,256]{2,1,0:T(8,128)}), f32[8,32,256]{2,1,0:T(8,128)S(1)}, u32[]{:S(2)}, u32[]{:S(2)}) async-start(f32[8,32,256]{2,1,0:T(8,128)} %broadcast_in_dim.16), calls=%async_computation.8 | async-start | bytes 524288 | tf_op jit(solution)/shard_map/all_to_all | solution.py:27
  205.9 13.8 %shard_map.60 = f32[256,256]{1,0:T(8,128)} custom-call(f32[256,256]{1,0:T(8,128)} %convolution_subtract_fusion.2.gram_ref), custom_call_target="tpu_custom_call" | custom-call | flops 16000000000 | bytes 524288 | tf_op jit(solution)/shard_map/pallas_call | solution.py:122
  220.8 2.7 %all_gather.7 = f32[512,256]{1,0:T(8,128)S(1)} all-gather(f32[256,256]{1,0:T(8,128)S(1)} %bitcast.81), channel_id=1, replica_groups=mesh['z'=8,'core'=2,'x'=4,'y'=8] {'core'}, dimensions={0}, use_global_device_ids=true | all-gather | bytes 786432 | tf_op jit(solution)/shard_map/all_gather | solution.py:169
  227.1 4.0 %fusion.4 = f32[1024,256]{1,0:T(8,128)} fusion(f32[1024,256]{1,0:T(8,128)S(1)} %bitcast.72, f32[1024,256]{1,0:T(8,128)S(1)} %bitcast.70, f32[1024,256]{1,0:T(8,128)} %bitcast.4, f32[256,256]{1,0:T(8,128)S(1)} %fusion.71, f32[256,256]{1,0:T(8,128)S(1)} %fusion.72, f32[]{:T(128)S(6)} %select_n.44), kind=kOutput, calls=%fused_computation.4 | convolution fusion | flops 1611792384 | bytes 4718596 | tf_op jit(solution)/shard_map/dot_general | solution.py:40
  (71 shorter events, 21.3 us)
Async XLA Ops:
  2.3 9.8 %collective-permute-start = (f32[1,128,256]{2,1,0:T(8,128)}, f32[1,128,256]{2,1,0:T(8,128)S(1)}, u32[]{:S(2)}, u32[]{:S(2)}) collective-permute-start(f32[1,128,256]{2,1,0:T(8,128)} %get-tuple-element.46), channel_id=1, source_target_pairs={{32,0},{64,32},{96,64},{128,96},{160,128},{192,160},{224,192},{256... | collective-permute-start | bytes 393224 | tf_op jit(solution)/shard_map/ppermute | solution.py:35
  9.1 2.1 copy-start
  9.2 3.9 %collective-permute-start.1 = (f32[1,128,256]{2,1,0:T(8,128)S(1)}, f32[1,128,256]{2,1,0:T(8,128)S(1)}, u32[]{:S(2)}, u32[]{:S(2)}) collective-permute-start(f32[1,128,256]{2,1,0:T(8,128)S(1)} %get-tuple-element.47), channel_id=1, source_target_pairs={{0,32},{32,64},{64,96},{96,128},{128,160},{160,192},{192,224},{224... | collective-permute-start | bytes 393224 | tf_op jit(solution)/shard_map/ppermute | solution.py:34
  14.9 5.8 %collective-permute-start.2 = (f32[1,128,256]{2,1,0:T(8,128)S(1)}, f32[1,128,256]{2,1,0:T(8,128)S(1)}, u32[]{:S(2)}, u32[]{:S(2)}) collective-permute-start(f32[1,128,256]{2,1,0:T(8,128)S(1)} %get-tuple-element.40), channel_id=1, source_target_pairs={{32,0},{64,32},{96,64},{128,96},{160,128},{192,160},{224,192},{256... | collective-permute-start | bytes 393224 | tf_op jit(solution)/shard_map/ppermute | solution.py:35
  19.7 2.0 collective-permute-start.3
  22.3 5.1 %collective-permute-start.4 = (f32[1,128,256]{2,1,0:T(8,128)S(1)}, f32[1,128,256]{2,1,0:T(8,128)S(1)}, u32[]{:S(2)}, u32[]{:S(2)}) collective-permute-start(f32[1,128,256]{2,1,0:T(8,128)S(1)} %get-tuple-element.34), channel_id=1, source_target_pairs={{32,0},{64,32},{96,64},{128,96},{160,128},{192,160},{224,192},{256... | collective-permute-start | bytes 393224 | tf_op jit(solution)/shard_map/ppermute | solution.py:35
  26.2 2.0 collective-permute-start.5
  28.8 5.1 %collective-permute-start.6 = (f32[1,128,256]{2,1,0:T(8,128)S(1)}, f32[1,128,256]{2,1,0:T(8,128)S(1)}, u32[]{:S(2)}, u32[]{:S(2)}) collective-permute-start(f32[1,128,256]{2,1,0:T(8,128)S(1)} %get-tuple-element.28), channel_id=1, source_target_pairs={{32,0},{64,32},{96,64},{128,96},{160,128},{192,160},{224,192},{256... | collective-permute-start | bytes 393224 | tf_op jit(solution)/shard_map/ppermute | solution.py:35
  32.5 2.0 collective-permute-start.7
  35.8 9.8 %copy-start.4 = (s32[32]{0:T(128)S(1)}, s32[32]{0:T(128)}, u32[]{:S(2)}) copy-start(s32[32]{0:T(128)} %param.7) | copy-start | bytes 388
  35.8 30.6 %all-to-all-start = ((f32[32,32,256]{2,1,0:T(8,128)}), f32[32,32,256]{2,1,0:T(8,128)S(1)}, u32[]{:S(2)}, u32[]{:S(2)}) async-start(f32[32,32,256]{2,1,0:T(8,128)} %bitcast.7), calls=%async_computation | async-start | bytes 2097152 | tf_op jit(solution)/shard_map/all_to_all | solution.py:20
  110.8 2.0 copy-start.3
  114.7 0.9 slice-start
  127.8 24.5 %all-to-all-start.5 = ((f32[8,40,256]{2,1,0:T(8,128)}), f32[8,40,256]{2,1,0:T(8,128)S(1)}, u32[]{:S(2)}, u32[]{:S(2)}) async-start(f32[8,40,256]{2,1,0:T(8,128)} %bitcast.21), calls=%async_computation.5 | async-start | bytes 655360 | tf_op jit(solution)/shard_map/all_to_all | solution.py:20
  152.3 5.5 %all-to-all-start.4 = ((f32[2,256,256]{2,1,0:T(8,128)}), f32[2,256,256]{2,1,0:T(8,128)S(1)}, u32[]{:S(2)}, u32[]{:S(2)}) async-start(f32[2,256,256]{2,1,0:T(8,128)} %bitcast.20), calls=%async_computation.4 | async-start | bytes 1048576 | tf_op jit(solution)/shard_map/all_to_all | solution.py:20
  158.5 17.1 %all-to-all-start.6 = ((f32[8,40,256]{2,1,0:T(8,128)}), f32[8,40,256]{2,1,0:T(8,128)S(1)}, u32[]{:S(2)}, u32[]{:S(2)}) async-start(f32[8,40,256]{2,1,0:T(8,128)} %broadcast_in_dim.15), calls=%async_computation.6 | async-start | bytes 655360 | tf_op jit(solution)/shard_map/all_to_all | solution.py:27
  178.0 17.9 %all-to-all-start.7 = ((f32[8,32,256]{2,1,0:T(8,128)}), f32[8,32,256]{2,1,0:T(8,128)S(1)}, u32[]{:S(2)}, u32[]{:S(2)}) async-start(f32[8,32,256]{2,1,0:T(8,128)} %bitcast.82), calls=%async_computation.7 | async-start | bytes 524288 | tf_op jit(solution)/shard_map/all_to_all | solution.py:20
  198.0 21.7 %all-to-all-start.8 = ((f32[8,32,256]{2,1,0:T(8,128)}), f32[8,32,256]{2,1,0:T(8,128)S(1)}, u32[]{:S(2)}, u32[]{:S(2)}) async-start(f32[8,32,256]{2,1,0:T(8,128)} %broadcast_in_dim.16), calls=%async_computation.8 | async-start | bytes 524288 | tf_op jit(solution)/shard_map/all_to_all | solution.py:27
  205.9 13.8 %copy-start.1 = (f32[256,256]{1,0:T(8,128)S(1)}, f32[256,256]{1,0:T(8,128)}, u32[]{:S(2)}) copy-start(f32[256,256]{1,0:T(8,128)} %shard_map.59) | copy-start | bytes 786436
  219.7 4.8 %copy-start.2 = (f32[256,256]{1,0:T(8,128)S(1)}, f32[256,256]{1,0:T(8,128)}, u32[]{:S(2)}) copy-start(f32[256,256]{1,0:T(8,128)} %shard_map.60) | copy-start | bytes 786436

commit v2 on v1

--- a/solution.py
+++ b/solution.py
@@ -27,13 +27,61 @@
     return lax.all_to_all(copies.reshape((-1,) + value.shape[1:]), axis, 0, 0, tiled=True)
 
 
-def padded_2(value):
-    size, length = lax.axis_size(SITE), value.shape[0]
+def halos(previous, current):
+    size, length = lax.axis_size(SITE), current.shape[0]
     up = [(i, (i + 1) % size) for i in range(size)]
     down = [(j, i) for i, j in up]
-    before = lax.ppermute(value[length - 1 :], SITE, up)
-    after = lax.ppermute(value[:1], SITE, down)
-    return jnp.concatenate([before, value, after], axis=0)
+    last = jnp.concatenate([previous[length - STEPS + 1 :], current[length - STEPS :]], axis=0)
+    leading = jnp.concatenate([previous[: STEPS - 1], current[:STEPS]], axis=0)
+    return lax.ppermute(last, SITE, up), lax.ppermute(leading, SITE, down)
+
+
+def window_kernel(previous_ref, current_ref, before_ref, after_ref, weight_ref, out_ref, even, odd):
+    rows = current_ref.shape[0]
+    depth = STEPS
+    even[pl.ds(0, depth)] = before_ref[pl.ds(depth - 1, depth)]
+    even[pl.ds(depth, rows)] = current_ref[...]
+    even[pl.ds(depth + rows, depth)] = after_ref[pl.ds(depth - 1, depth)]
+    odd[pl.ds(1, depth - 1)] = before_ref[pl.ds(0, depth - 1)]
+    odd[pl.ds(depth, rows)] = previous_ref[...]
+    odd[pl.ds(depth + rows, depth - 1)] = after_ref[pl.ds(0, depth - 1)]
+    for turn in range(STEPS):
+        current, previous = (even, odd) if turn % 2 == 0 else (odd, even)
+        last = turn == STEPS - 1
+
+        for row in range(turn + 1, rows + 2 * depth - 1 - turn):
+            here = current[row]
+            neighbours = current[row + 1] + current[row - 1] + pltpu.roll(here, 1, 0) + pltpu.roll(here, here.shape[0] - 1, 0)
+            value = weight_ref[turn, :, row : row + 1] * (ENERGY * here - neighbours - previous[row])
+            if last:
+                out_ref[row - depth] = value
+            else:
+                previous[row] = value
+
+
+def window(previous, current, occupancy):
+    rows, side, width = current.shape
+    before, after = halos(previous, current)
+    start = lax.axis_index(SITE) * rows
+    around = jnp.concatenate([occupancy[:, side - STEPS :], occupancy, occupancy[:, :STEPS]], axis=1)
+    weights = lax.dynamic_slice_in_dim(around, start, rows + 2 * STEPS, 1).astype(jnp.float32).transpose(0, 2, 1)
+    slab = pltpu.VMEM((rows + 2 * STEPS, side, width), jnp.float32)
+    return pl.pallas_call(
+        window_kernel,
+        out_shape=jax.ShapeDtypeStruct(current.shape, jnp.float32),
+        in_specs=[pl.BlockSpec(memory_space=pltpu.VMEM)] * 5,
+        out_specs=pl.BlockSpec(memory_space=pltpu.VMEM),
+        scratch_shapes=[slab, slab],
+        compiler_params=pltpu.CompilerParams(vmem_limit_bytes=32 * 1024 * 1024),
+        cost_estimate=pl.CostEstimate(flops=12_000_000, bytes_accessed=6_000_000, transcendentals=0),
+    )(previous, current, before, after, weights)
+
+
+def core_sum(value):
+    core, half = lax.axis_index("core"), value.shape[0] // 2
+    give = lax.dynamic_slice_in_dim(value, (1 - core) * half, half, 0)
+    keep = lax.dynamic_slice_in_dim(value, core * half, half, 0)
+    return keep + lax.ppermute(give, "core", [(0, 1), (1, 0)])
 
 
 def product(left, right):
@@ -135,14 +183,7 @@
 
 def on_device(state_prev, state_cur, occupancy, panel_order):
     rows, side, width = state_cur.shape
-    start = lax.axis_index(SITE) * rows
-    local_mask = lax.dynamic_slice_in_dim(occupancy, start, rows, 1)
-    previous, current = (state_prev, state_cur)
-    for turn in range(STEPS):
-        weights = local_mask[turn].astype(jnp.float32)[:, :, None]
-        padded = padded_2(current)
-        neighbours = padded[2:] + padded[:-2] + jnp.roll(current, 1, 1) + jnp.roll(current, -1, 1)
-        previous, current = (current, weights * (ENERGY * current - neighbours - previous))
+    current = window(state_prev, state_cur, occupancy)
     flat = current.reshape(rows * side, width)
     first, second = panel_order[0], panel_order[1]
     a, b = fetch_panels(flat, (first, second))
@@ -155,7 +196,7 @@
     a_late, b_late, gram = lax.optimization_barrier((a, b, gram))
     inner = jnp.concatenate([product_t(a_late, flat), product_t(b_late, flat)], axis=0)
     gram = gather(exchange(gram, "z").sum(axis=0), "z")
-    inner = exchange(inner, "core").sum(axis=0)
+    inner = core_sum(inner)
     inner, gram = lax.optimization_barrier((inner, lax.all_gather(gram, "core", axis=0, tiled=True)))
     inner = exchange(inner, "z").sum(axis=0)
     corners, ab = gram[PANEL : PANEL + half], gram[PANEL + half :]

time: 232 us -> 222 us (0.957)
  starting transfers between devices: 57.4 us -> 50.2 us
  Pallas kernels: 27.5 us -> 32.1 us
  waiting for transfers between devices: 42.8 us -> 38.5 us
    ppermute x8 -> x3, starting transfers between devices: 19.2 us -> 9.39 us  [the longest x2 6.88 us: halos(): return (lax.ppermute(last, SITE, up), lax.ppermute(leading, SITE, down))]
    pallas_call x0 -> x1, Pallas kernels: none -> 4.54 us  [window(): pl.pallas_call(window_kernel, out_shape=jax.ShapeDtypeStruct(current.shap...]
    mul x4 -> x0, other arithmetic: 3.76 us -> none  [on_device(): weights * (ENERGY * current - neighbours - previous)]
    all_to_all x2, waiting for transfers between devices: 11.6 us -> 8.18 us  [gather(): lax.all_to_all(copies.reshape((-1,) + value.shape[1:]), axis, 0, 0, tiled...]
    all_to_all x4 -> x3, starting transfers between devices: 28.2 us -> 30.8 us  [exchange(): out = lax.all_to_all(value, axis, 0, 0, tiled=True)]
    all_to_all x4 -> x3, waiting for transfers between devices: 24.3 us -> 22.8 us  [exchange(): out = lax.all_to_all(value, axis, 0, 0, tiled=True)]
    ppermute x8 -> x3, waiting for transfers between devices: 6.82 us -> 7.55 us  [the longest x2 7.5 us: halos(): return (lax.ppermute(last, SITE, up), lax.ppermute(leading, SITE, down))]
  transfers between devices with their start and end apart: 14 -> 8, of which waited for: 11 -> 6; matrix products, arithmetic and copies ran while one was open for 6% -> 6% of each run, Pallas kernels for 12% -> 12%
where the time goes in v2:
time: 222 us; the launch traced here: 221 us
  blocking collectives  59 us (27%)
  starting transfers between devices  50.2 us (23%)
  waiting for transfers between devices  38.5 us (17%)
  Pallas kernels  32.1 us (14%)
  matrix products  21.4 us (10%)
  other arithmetic  8.02 us (4%)
  between operations  6.1 us (3%)
  local copies, waits for them, and re-layouts  5.98 us (3%)
    all_to_all x2, blocking collectives, gather(): lax.all_to_all(copies.reshape((-1,) + value.shape[1:]), axis, 0, 0, tiled...  42.3 us
    all_to_all x3, starting transfers between devices, exchange(): out = lax.all_to_all(value, axis, 0, 0, tiled=True)  30.8 us
    pallas_call x2, Pallas kernels, factor(): pl.pallas_call(factor_kernel, out_shape=jax.ShapeDtypeStruct(gram.shape,...  27.6 us
    all_to_all x3, waiting for transfers between devices, exchange(): out = lax.all_to_all(value, axis, 0, 0, tiled=True)  22.8 us
    dot_general x9, matrix products, product_t(): lax.dot_general(left, right, dims, precision=lax.Precision.HIGHEST, prefe...  14.9 us
    all_to_all x1, blocking collectives, exchange(): out = lax.all_to_all(value, axis, 0, 0, tiled=True)  11.5 us
    all_to_all x2, starting transfers between devices, gather(): lax.all_to_all(copies.reshape((-1,) + value.shape[1:]), axis, 0, 0, tiled...  9.99 us
    all_to_all x2, waiting for transfers between devices, gather(): lax.all_to_all(copies.reshape((-1,) + value.shape[1:]), axis, 0, 0, tiled...  8.18 us
  transfers between devices with their start and end apart: 8, of which 6 were waited for; matrix products, arithmetic and copies ran while one was open for 6% of the time, Pallas kernels for 12%

profile of v2, /device:TPU:1, one launch (start us, length us, event | category | flops | bytes accessed | tf_op | source)
XLA Modules:
  0.0 221.3 jit_solution(6756124309990892677)
XLA Ops:
  0.6 1.4 fusion.35
  3.2 3.5 %collective-permute-start = (f32[7,128,256]{2,1,0:T(8,128)}, f32[7,128,256]{2,1,0:T(8,128)S(1)}, u32[]{:S(2)}, u32[]{:S(2)}) collective-permute-start(f32[7,128,256]{2,1,0:T(8,128)} %pad_maximum_fusion), channel_id=1, source_target_pairs={{0,32},{32,64},{64,96},{96,128},{128,160},{160,192},{192,224},{224... | collective-permute-start | bytes 2752520 | tf_op jit(solution)/shard_map/ppermute | solution.py:36
  7.7 3.4 %collective-permute-start.1 = (f32[7,128,256]{2,1,0:T(8,128)}, f32[7,128,256]{2,1,0:T(8,128)}, u32[]{:S(2)}, u32[]{:S(2)}) collective-permute-start(f32[7,128,256]{2,1,0:T(8,128)} %pad_maximum_fusion.1), channel_id=1, source_target_pairs={{32,0},{64,32},{96,64},{128,96},{160,128},{192,160},{224,192},{256... | collective-permute-start | bytes 2752520 | tf_op jit(solution)/shard_map/ppermute | solution.py:36
  12.3 1.2 fusion.20.weight_ref
  13.6 3.8 %collective-permute-done.before_ref = f32[7,128,256]{2,1,0:T(8,128)S(1)} collective-permute-done((f32[7,128,256]{2,1,0:T(8,128)}, f32[7,128,256]{2,1,0:T(8,128)S(1)}, u32[]{:S(2)}, u32[]{:S(2)}) %collective-permute-start) | collective-permute-done | bytes 917536 | tf_op jit(solution)/shard_map/ppermute | solution.py:36
  17.4 3.7 %collective-permute-done.1.after_ref = f32[7,128,256]{2,1,0:T(8,128)} collective-permute-done((f32[7,128,256]{2,1,0:T(8,128)}, f32[7,128,256]{2,1,0:T(8,128)}, u32[]{:S(2)}, u32[]{:S(2)}) %collective-permute-start.1) | collective-permute-done | bytes 917536 | tf_op jit(solution)/shard_map/ppermute | solution.py:36
  21.1 4.5 %shard_map.59 = f32[8,128,256]{2,1,0:T(8,128)} custom-call(f32[8,128,256]{2,1,0:T(8,128)S(1)} %copy-done.1, f32[8,128,256]{2,1,0:T(8,128)S(1)} %copy-done, f32[7,128,256]{2,1,0:T(8,128)S(1)} %collective-permute-done.before_ref, f32[7,128,256]{2,1,0:T(8,128)} %collective-permute-done.1.after_ref, f32[4,128,16]{2,1,0:T(8,128)S(1)} %fusion.20.weight_ref), custom_call_target="tpu_custom_call" | custom-call | flops 12000000 | bytes 6000000 | tf_op jit(solution)/shard_map/pallas_call | solution.py:69
  25.6 9.8 %all-to-all-start = ((f32[32,32,256]{2,1,0:T(8,128)}), f32[32,32,256]{2,1,0:T(8,128)S(1)}, u32[]{:S(2)}, u32[]{:S(2)}) async-start(f32[32,32,256]{2,1,0:T(8,128)} %bitcast.4), calls=%async_computation | async-start | bytes 2097152 | tf_op jit(solution)/shard_map/all_to_all | solution.py:20
  39.9 15.3 %all-to-all-done = f32[32,32,256]{2,1,0:T(8,128)S(1)} async-done(((f32[32,32,256]{2,1,0:T(8,128)}), f32[32,32,256]{2,1,0:T(8,128)S(1)}, u32[]{:S(2)}, u32[]{:S(2)}) %all-to-all-start) | async-done | bytes 1048608 | tf_op jit(solution)/shard_map/all_to_all | solution.py:20
  55.2 19.2 %all_to_all.66 = f32[8,64,256]{2,1,0:T(8,128)S(1)} all-to-all(f32[8,64,256]{2,1,0:T(8,128)S(1)} %broadcast_in_dim.12), channel_id=1, replica_groups=mesh['z'=8,'core'=2,'x'=4,'y'=8] {'y'}, dimensions={0} | all-to-all | bytes 1048576 | tf_op jit(solution)/shard_map/all_to_all | solution.py:27
  74.6 23.1 %all_to_all.67 = f32[4,512,256]{2,1,0:T(8,128)S(1)} all-to-all(f32[4,512,256]{2,1,0:T(8,128)S(1)} %broadcast_in_dim.14), channel_id=1, replica_groups=mesh['z'=8,'core'=2,'x'=4,'y'=8] {'x'}, dimensions={0} | all-to-all | bytes 4194304 | tf_op jit(solution)/shard_map/all_to_all | solution.py:27
  97.7 1.9 convolution_bitcast_fusion.2
  99.6 1.9 convolution_bitcast_fusion.1
  101.6 1.9 convolution_bitcast_fusion
  104.4 11.5 %all_to_all.68 = f32[2,320,256]{2,1,0:T(8,128)S(1)} all-to-all(f32[2,320,256]{2,1,0:T(8,128)S(1)} %bitcast.70), channel_id=1, replica_groups=mesh['z'=8,'core'=2,'x'=4,'y'=8] {'core'}, dimensions={0} | all-to-all | bytes 1310720 | tf_op jit(solution)/shard_map/all_to_all | solution.py:20
  116.7 17.6 %all-to-all-start.4 = ((f32[8,40,256]{2,1,0:T(8,128)}), f32[8,40,256]{2,1,0:T(8,128)S(1)}, u32[]{:S(2)}, u32[]{:S(2)}) async-start(f32[8,40,256]{2,1,0:T(8,128)} %bitcast.17), calls=%async_computation.4 | async-start | bytes 655360 | tf_op jit(solution)/shard_map/all_to_all | solution.py:20
  134.3 3.0 %fusion.41 = f32[256,256]{1,0:T(8,128)S(1)} fusion(f32[1024,256]{1,0:T(8,128)S(1)} %bitcast.64, f32[1024,256]{1,0:T(8,128)} %bitcast.1), kind=kOutput, calls=%fused_computation.68 | convolution fusion | flops 805306368 | bytes 2359296 | tf_op jit(solution)/shard_map/dot_general | solution.py:93
  137.3 3.0 %fusion.40 = f32[256,256]{1,0:T(8,128)S(1)} fusion(f32[1024,256]{1,0:T(8,128)S(1)} %bitcast.62, f32[1024,256]{1,0:T(8,128)} %bitcast.1), kind=kOutput, calls=%fused_computation.67 | convolution fusion | flops 805306368 | bytes 2359296 | tf_op jit(solution)/shard_map/dot_general | solution.py:93
  140.4 7.5 %all-to-all-done.4 = f32[8,40,256]{2,1,0:T(8,128)S(1)} async-done(((f32[8,40,256]{2,1,0:T(8,128)}), f32[8,40,256]{2,1,0:T(8,128)S(1)}, u32[]{:S(2)}, u32[]{:S(2)}) %all-to-all-start.4) | async-done | bytes 327712 | tf_op jit(solution)/shard_map/all_to_all | solution.py:20
  148.7 3.4 %all-to-all-start.5 = ((f32[8,40,256]{2,1,0:T(8,128)}), f32[8,40,256]{2,1,0:T(8,128)S(1)}, u32[]{:S(2)}, u32[]{:S(2)}) async-start(f32[8,40,256]{2,1,0:T(8,128)} %broadcast_in_dim.15), calls=%async_computation.5 | async-start | bytes 655360 | tf_op jit(solution)/shard_map/all_to_all | solution.py:27
  152.9 2.5 %collective-permute-start.2 = (f32[256,256]{1,0:T(8,128)}, f32[256,256]{1,0:T(8,128)S(1)}, u32[]{:S(2)}, u32[]{:S(2)}) collective-permute-start(f32[256,256]{1,0:T(8,128)} %fusion.21), channel_id=1, source_target_pairs={{0,32},{32,0},{1,33},{33,1},{2,34},{34,2},{3,35},{35,3},{4,36},{36... | collective-permute-start | bytes 786440 | tf_op jit(solution)/shard_map/ppermute | solution.py:84
  157.5 8.2 %all-to-all-done.5 = f32[8,40,256]{2,1,0:T(8,128)S(1)} async-done(((f32[8,40,256]{2,1,0:T(8,128)}), f32[8,40,256]{2,1,0:T(8,128)S(1)}, u32[]{:S(2)}, u32[]{:S(2)}) %all-to-all-start.5) | async-done | bytes 327712 | tf_op jit(solution)/shard_map/all_to_all | solution.py:27
  165.7 2.4 %all_gather.6 = f32[640,256]{1,0:T(8,128)S(1)} all-gather(f32[320,256]{1,0:T(8,128)S(1)} %bitcast.72), channel_id=1, replica_groups=mesh['z'=8,'core'=2,'x'=4,'y'=8] {'core'}, dimensions={0}, use_global_device_ids=true | all-gather | bytes 983040 | tf_op jit(solution)/shard_map/all_gather | solution.py:200
  168.2 3.4 %all-to-all-start.6 = ((f32[8,32,256]{2,1,0:T(8,128)}), f32[8,32,256]{2,1,0:T(8,128)S(1)}, u32[]{:S(2)}, u32[]{:S(2)}) async-start(f32[8,32,256]{2,1,0:T(8,128)} %bitcast.75), calls=%async_computation.6 | async-start | bytes 524288 | tf_op jit(solution)/shard_map/all_to_all | solution.py:20
  172.3 13.8 %shard_map.60 = f32[256,256]{1,0:T(8,128)} custom-call(f32[256,256]{1,0:T(8,128)} %select_maximum_fusion.1.gram_ref), custom_call_target="tpu_custom_call" | custom-call | flops 16000000000 | bytes 524288 | tf_op jit(solution)/shard_map/pallas_call | solution.py:170
  186.1 1.3 fusion.26
  188.2 6.6 %all-to-all-start.7 = ((f32[8,32,256]{2,1,0:T(8,128)}), f32[8,32,256]{2,1,0:T(8,128)S(1)}, u32[]{:S(2)}, u32[]{:S(2)}) async-start(f32[8,32,256]{2,1,0:T(8,128)} %broadcast_in_dim.16), calls=%async_computation.7 | async-start | bytes 524288 | tf_op jit(solution)/shard_map/all_to_all | solution.py:27
  194.7 1.3 convolution_subtract_fusion.2.gram_ref
  196.1 13.8 %shard_map.61 = f32[256,256]{1,0:T(8,128)} custom-call(f32[256,256]{1,0:T(8,128)} %convolution_subtract_fusion.2.gram_ref), custom_call_target="tpu_custom_call" | custom-call | flops 16000000000 | bytes 524288 | tf_op jit(solution)/shard_map/pallas_call | solution.py:170
  209.9 1.0 select_reduce_fusion
  211.0 2.7 %all_gather.7 = f32[512,256]{1,0:T(8,128)S(1)} all-gather(f32[256,256]{1,0:T(8,128)S(1)} %bitcast.74), channel_id=1, replica_groups=mesh['z'=8,'core'=2,'x'=4,'y'=8] {'core'}, dimensions={0}, use_global_device_ids=true | all-gather | bytes 786432 | tf_op jit(solution)/shard_map/all_gather | solution.py:210
  217.3 4.0 %multiply_subtract_fusion = f32[1024,256]{1,0:T(8,128)} fusion(f32[1024,256]{1,0:T(8,128)} %bitcast.1, f32[1024,256]{1,0:T(8,128)S(1)} %bitcast.65, f32[1024,256]{1,0:T(8,128)S(1)} %bitcast.63, f32[256,256]{1,0:T(8,128)S(1)} %fusion.42, f32[256,256]{1,0:T(8,128)S(1)} %fusion.43, f32[]{:T(128)S(6)} %select_n.50), kind=kOutput, calls=%fused_computation.17 | convolution fusion | flops 1611792384 | bytes 4718596 | tf_op jit(solution)/shard_map/dot_general | solution.py:88
  (56 shorter events, 13.4 us)
Async XLA Ops:
  0.6 1.5 copy-start.1
  2.2 8.9 %copy-start.5 = (s32[4,128,128]{2,1,0:T(8,128)S(1)}, s32[4,128,128]{2,1,0:T(8,128)}, u32[]{:S(2)}) copy-start(s32[4,128,128]{2,1,0:T(8,128)} %param.6) | copy-start | bytes 786436
  3.2 17.8 %copy-start = (f32[8,128,256]{2,1,0:T(8,128)S(1)}, f32[8,128,256]{2,1,0:T(8,128)}, u32[]{:S(2)}) copy-start(f32[8,128,256]{2,1,0:T(8,128)} %current_ref.1) | copy-start | bytes 3145732
  3.2 14.1 %collective-permute-start = (f32[7,128,256]{2,1,0:T(8,128)}, f32[7,128,256]{2,1,0:T(8,128)S(1)}, u32[]{:S(2)}, u32[]{:S(2)}) collective-permute-start(f32[7,128,256]{2,1,0:T(8,128)} %pad_maximum_fusion), channel_id=1, source_target_pairs={{0,32},{32,64},{64,96},{96,128},{128,160},{160,192},{192,224},{224... | collective-permute-start | bytes 2752520 | tf_op jit(solution)/shard_map/ppermute | solution.py:36
  7.7 13.3 %collective-permute-start.1 = (f32[7,128,256]{2,1,0:T(8,128)}, f32[7,128,256]{2,1,0:T(8,128)}, u32[]{:S(2)}, u32[]{:S(2)}) collective-permute-start(f32[7,128,256]{2,1,0:T(8,128)} %pad_maximum_fusion.1), channel_id=1, source_target_pairs={{32,0},{64,32},{96,64},{128,96},{160,128},{192,160},{224,192},{256... | collective-permute-start | bytes 2752520 | tf_op jit(solution)/shard_map/ppermute | solution.py:36
  25.6 9.8 %copy-start.6 = (s32[32]{0:T(128)S(1)}, s32[32]{0:T(128)}, u32[]{:S(2)}) copy-start(s32[32]{0:T(128)} %param.7) | copy-start | bytes 388
  25.6 29.5 %all-to-all-start = ((f32[32,32,256]{2,1,0:T(8,128)}), f32[32,32,256]{2,1,0:T(8,128)S(1)}, u32[]{:S(2)}, u32[]{:S(2)}) async-start(f32[32,32,256]{2,1,0:T(8,128)} %bitcast.4), calls=%async_computation | async-start | bytes 2097152 | tf_op jit(solution)/shard_map/all_to_all | solution.py:20
  99.6 2.0 copy-start.4
  103.5 0.9 slice-start
  116.7 31.2 %all-to-all-start.4 = ((f32[8,40,256]{2,1,0:T(8,128)}), f32[8,40,256]{2,1,0:T(8,128)S(1)}, u32[]{:S(2)}, u32[]{:S(2)}) async-start(f32[8,40,256]{2,1,0:T(8,128)} %bitcast.17), calls=%async_computation.4 | async-start | bytes 655360 | tf_op jit(solution)/shard_map/all_to_all | solution.py:20
  148.7 17.0 %all-to-all-start.5 = ((f32[8,40,256]{2,1,0:T(8,128)}), f32[8,40,256]{2,1,0:T(8,128)S(1)}, u32[]{:S(2)}, u32[]{:S(2)}) async-start(f32[8,40,256]{2,1,0:T(8,128)} %broadcast_in_dim.15), calls=%async_computation.5 | async-start | bytes 655360 | tf_op jit(solution)/shard_map/all_to_all | solution.py:27
  152.9 3.9 %collective-permute-start.2 = (f32[256,256]{1,0:T(8,128)}, f32[256,256]{1,0:T(8,128)S(1)}, u32[]{:S(2)}, u32[]{:S(2)}) collective-permute-start(f32[256,256]{1,0:T(8,128)} %fusion.21), channel_id=1, source_target_pairs={{0,32},{32,0},{1,33},{33,1},{2,34},{34,2},{3,35},{35,3},{4,36},{36... | collective-permute-start | bytes 786440 | tf_op jit(solution)/shard_map/ppermute | solution.py:84
  168.2 17.9 %all-to-all-start.6 = ((f32[8,32,256]{2,1,0:T(8,128)}), f32[8,32,256]{2,1,0:T(8,128)S(1)}, u32[]{:S(2)}, u32[]{:S(2)}) async-start(f32[8,32,256]{2,1,0:T(8,128)} %bitcast.75), calls=%async_computation.6 | async-start | bytes 524288 | tf_op jit(solution)/shard_map/all_to_all | solution.py:20
  188.2 21.7 %all-to-all-start.7 = ((f32[8,32,256]{2,1,0:T(8,128)}), f32[8,32,256]{2,1,0:T(8,128)S(1)}, u32[]{:S(2)}, u32[]{:S(2)}) async-start(f32[8,32,256]{2,1,0:T(8,128)} %broadcast_in_dim.16), calls=%async_computation.7 | async-start | bytes 524288 | tf_op jit(solution)/shard_map/all_to_all | solution.py:27
  196.1 13.8 %copy-start.2 = (f32[256,256]{1,0:T(8,128)S(1)}, f32[256,256]{1,0:T(8,128)}, u32[]{:S(2)}) copy-start(f32[256,256]{1,0:T(8,128)} %shard_map.60) | copy-start | bytes 786436
  209.9 4.8 %copy-start.3 = (f32[256,256]{1,0:T(8,128)S(1)}, f32[256,256]{1,0:T(8,128)}, u32[]{:S(2)}) copy-start(f32[256,256]{1,0:T(8,128)} %shard_map.61) | copy-start | bytes 786436

commit v3 on v2

--- a/solution.py
+++ b/solution.py
@@ -10,6 +10,7 @@
 ENERGY = 0.5
 RESCALE = 0.015625
 BLOCK = 8
+GROUP = 4
 
 SITE = ("z", "core")
 COL = ("x", "y")
@@ -97,8 +98,7 @@
     received = exchange(flat, COL)
     mine = jnp.concatenate([lax.dynamic_index_in_dim(received, panel, 0, False) for panel in panels], axis=0)
     both = gather(gather(mine, "y"), "x")
-    both = both.reshape(-1, len(panels), received.shape[1], PANEL)
-    return [both[:, n].reshape(-1, PANEL) for n in range(len(panels))]
+    return both.reshape(-1, len(panels), received.shape[1], PANEL)
 
 
 def split3(x):
@@ -116,69 +116,136 @@
     return lax.dot_general(lhs, rhs, (((0,), (0,)), ((), ())), preferred_element_type=jnp.float32)
 
 
-def factor_kernel(gram_ref, out_ref):
-    n = gram_ref.shape[0]
+def columns_of(rows, lane, first):
+    out = []
+    for m in range(BLOCK):
+        column = jnp.sum(jnp.where(lane == first + m, rows, 0.0), axis=1, keepdims=True)
+        out.append(jnp.broadcast_to(column, (BLOCK, 128)))
+    return out
+
+
+def invert_block(columns):
+    entry = {}
+    for m in range(BLOCK):
+        for i in range(m, BLOCK):
+            entry[i, m] = jnp.broadcast_to(columns[m][i : i + 1], (BLOCK, 128))
+    inv = {}
+    for k in range(BLOCK):
+        root = lax.rsqrt(entry[k, k])
+        for i in range(k + 1, BLOCK):
+            entry[i, k] = entry[i, k] * root
+        for m in range(k + 1, BLOCK):
+            for i in range(m, BLOCK):
+                entry[i, m] = entry[i, m] - entry[i, k] * entry[m, k]
+        for c in range(k):
+            acc = entry[k, c] * inv[c, c]
+            for m in range(c + 1, k):
+                acc = acc + entry[k, m] * inv[m, c]
+            inv[k, c] = -root * acc
+        inv[k, k] = root
+    return inv
+
+
+def combine(columns, rows):
+    n = rows.shape[1]
+    out = None
+    for k in range(BLOCK):
+        wide = jnp.concatenate([columns[k]] * (n // 128), axis=1)
+        term = wide * jnp.broadcast_to(rows[k : k + 1], (BLOCK, n))
+        out = term if out is None else out + term
+    return out
+
+
+def eliminate(out_ref, growth_ref):
+    n = out_ref.shape[0]
     lane = lax.broadcasted_iota(jnp.int32, (BLOCK, n), 1)
     sub = lax.broadcasted_iota(jnp.int32, (BLOCK, n), 0)
     sub1 = lax.broadcasted_iota(jnp.int32, (BLOCK, 128), 0)
     lane_all = lax.broadcasted_iota(jnp.int32, (n, n), 1)
-    out_ref[...] = gram_ref[...]
+    width = GROUP * BLOCK
 
     def step(j, _):
-        r = pl.multiple_of(j * BLOCK, BLOCK)
-        panel = out_ref[pl.ds(r, BLOCK), :]
-        entry = {}
-        for m in range(BLOCK):
-            column = jnp.sum(jnp.where(lane == r + m, panel, 0.0), axis=1, keepdims=True)
-            column = jnp.broadcast_to(column, (BLOCK, 128))
-            for i in range(m, BLOCK):
-                entry[i, m] = jnp.broadcast_to(column[i : i + 1], (BLOCK, 128))
-        inv = {}
-        for k in range(BLOCK):
-            root = lax.rsqrt(entry[k, k])
-            for i in range(k + 1, BLOCK):
-                entry[i, k] = entry[i, k] * root
-            for m in range(k + 1, BLOCK):
-                for i in range(m, BLOCK):
-                    entry[i, m] = entry[i, m] - entry[i, k] * entry[m, k]
-            for c in range(k):
-                acc = entry[k, c] * inv[c, c]
-                for m in range(c + 1, k):
-                    acc = acc + entry[k, m] * inv[m, c]
-                inv[k, c] = -root * acc
-            inv[k, k] = root
-        inside = jnp.logical_and(lane >= r, lane < r + BLOCK)
-        panel = jnp.where(inside, jnp.where(lane - r == sub, 1.0, 0.0), panel)
-        new = None
-        for k in range(BLOCK):
-            column = jnp.zeros((BLOCK, 128), jnp.float32)
-            for i in range(k, BLOCK):
-                column = jnp.where(sub1 == i, inv[i, k], column)
-            column = jnp.concatenate([column] * (n // 128), axis=1)
-            term = column * jnp.broadcast_to(panel[k : k + 1], (BLOCK, n))
-            new = term if new is None else new + term
-        ahead = jnp.where(lane >= r + BLOCK, new, 0.0)
-        inside = jnp.logical_and(lane_all >= r, lane_all < r + BLOCK)
-        out_ref[...] = jnp.where(inside, 0.0, out_ref[...]) - outer(ahead, new)
-        out_ref[pl.ds(r, BLOCK), :] = new
+        first = pl.multiple_of(j * width, width)
+        end = first + width
+        panels = [out_ref[pl.ds(first + g * BLOCK, BLOCK), :] for g in range(GROUP)]
+        done, ahead, rest = [], [], []
+        for g in range(GROUP):
+            r = first + g * BLOCK
+            panel = panels[g]
+            inside = jnp.logical_and(lane >= r, lane < r + BLOCK)
+            inv = invert_block(columns_of(panel, lane, r))
+            below = [columns_of(panels[h], lane, r) for h in range(g + 1, GROUP)]
+            panel = jnp.where(inside, jnp.where(lane - r == sub, 1.0, 0.0), panel)
+            factor_columns = []
+            for k in range(BLOCK):
+                column = jnp.zeros((BLOCK, 128), jnp.float32)
+                for i in range(k, BLOCK):
+                    column = jnp.where(sub1 == i, inv[i, k], column)
+                factor_columns.append(column)
+            new = combine(factor_columns, panel)
+            for h in range(g + 1, GROUP):
+                source = below[h - g - 1]
+                weights = []
+                for k in range(BLOCK):
+                    acc = inv[k, 0] * source[0]
+                    for m in range(1, k + 1):
+                        acc = acc + inv[k, m] * source[m]
+                    weights.append(acc)
+                panels[h] = jnp.where(inside, 0.0, panels[h]) - combine(weights, new)
+            done.append(jnp.where(lane < r + BLOCK, new, 0.0))
+            ahead.append(jnp.where(lane >= end, new, 0.0))
+            rest.append(jnp.where(jnp.logical_and(lane >= r + BLOCK, lane < end), 0.0, new))
+        inside = jnp.logical_and(lane_all >= first, lane_all < end)
+        update = outer(jnp.concatenate(ahead, axis=0), jnp.concatenate(rest, axis=0))
+        out_ref[...] = jnp.where(inside, 0.0, out_ref[...]) - update
+        for g in range(GROUP):
+            out_ref[pl.ds(first + g * BLOCK, BLOCK), :] = done[g]
         return 0
 
-    lax.fori_loop(0, n // BLOCK, step, 0)
-
-
-def factor(gram):
-    return pl.pallas_call(
-        factor_kernel,
-        out_shape=jax.ShapeDtypeStruct(gram.shape, jnp.float32),
-        in_specs=[pl.BlockSpec(memory_space=pltpu.VMEM)],
-        out_specs=pl.BlockSpec(memory_space=pltpu.VMEM),
-        cost_estimate=pl.CostEstimate(flops=16_000_000_000, bytes_accessed=524288, transcendentals=256),
-    )(gram)
-
-
-def growth(inverse):
-    eye = jnp.eye(inverse.shape[0], dtype=bool)
-    return -jnp.log(jnp.sum(jnp.where(eye, inverse, 0.0), axis=0))
+    lax.fori_loop(0, n // width, step, 0)
+    row = lax.broadcasted_iota(jnp.int32, (n, n), 0)
+    growth_ref[...] = -jnp.log(jnp.sum(jnp.where(row == lane_all, out_ref[...], 0.0), axis=0, keepdims=True))
+
+
+def gram_kernel(both_ref, out_ref):
+    half = PANEL // 2
+    a, b = [both_ref[:, n].reshape(-1, PANEL) for n in range(2)]
+    out_ref[pl.ds(0, half), :] = product_t(a[:, :half], a)
+    out_ref[pl.ds(half, half), :] = product_t(b[:, :half], b)
+    out_ref[pl.ds(PANEL, half), pl.ds(0, half)] = product_t(a[:, half:], a[:, half:])
+    out_ref[pl.ds(PANEL, half), pl.ds(half, half)] = product_t(b[:, half:], b[:, half:])
+    out_ref[pl.ds(PANEL + half, PANEL), :] = product_t(a, b)
+
+
+def first_kernel(gram_ref, out_ref, growth_ref):
+    half = PANEL // 2
+    out_ref[pl.ds(0, half), :] = gram_ref[pl.ds(0, half), :]
+    out_ref[pl.ds(half, half), pl.ds(0, half)] = jnp.zeros((half, half), jnp.float32)
+    out_ref[pl.ds(half, half), pl.ds(half, half)] = gram_ref[pl.ds(PANEL, half), pl.ds(0, half)]
+    eliminate(out_ref, growth_ref)
+
+
+def second_kernel(gram_ref, inverse_ref, out_ref, growth_ref, cross_ref):
+    half = PANEL // 2
+    cross = product(inverse_ref[...], gram_ref[pl.ds(PANEL + half, PANEL), :])
+    cross_ref[...] = cross
+    inner = product_t(cross, cross)
+    out_ref[pl.ds(0, half), :] = gram_ref[pl.ds(half, half), :] - inner[:half]
+    out_ref[pl.ds(half, half), pl.ds(0, half)] = jnp.zeros((half, half), jnp.float32)
+    out_ref[pl.ds(half, half), pl.ds(half, half)] = gram_ref[pl.ds(PANEL, half), pl.ds(half, half)] - inner[half:, half:]
+    eliminate(out_ref, growth_ref)
+
+
+def on_chip(kernel, flops, *shapes):
+    vmem = pl.BlockSpec(memory_space=pltpu.VMEM)
+    return lambda *args: pl.pallas_call(
+        kernel,
+        out_shape=[jax.ShapeDtypeStruct(shape, jnp.float32) for shape in shapes],
+        in_specs=[vmem] * len(args),
+        out_specs=[vmem] * len(shapes),
+        compiler_params=pltpu.CompilerParams(vmem_limit_bytes=32 * 1024 * 1024),
+        cost_estimate=pl.CostEstimate(flops=flops, bytes_accessed=524288, transcendentals=PANEL),
+    )(*args)
 
 
 def on_device(state_prev, state_cur, occupancy, panel_order):
@@ -186,12 +253,9 @@
     current = window(state_prev, state_cur, occupancy)
     flat = current.reshape(rows * side, width)
     first, second = panel_order[0], panel_order[1]
-    a, b = fetch_panels(flat, (first, second))
-
-    half = PANEL // 2
-    aa, ab, bb = product_t(a, a), product_t(a, b), product_t(b, b)
-    corners = jnp.concatenate([aa[half:, half:], bb[half:, half:]], axis=1)
-    gram = jnp.concatenate([aa[:half], bb[:half], corners, ab], axis=0)
+    both = fetch_panels(flat, (first, second))
+    (gram,) = on_chip(gram_kernel, 4_000_000_000, (PANEL * 5 // 2, PANEL))(both)
+    a, b = [both[:, n].reshape(-1, PANEL) for n in range(2)]
     gram = exchange(gram, "core").sum(axis=0)
     a_late, b_late, gram = lax.optimization_barrier((a, b, gram))
     inner = jnp.concatenate([product_t(a_late, flat), product_t(b_late, flat)], axis=0)
@@ -199,14 +263,11 @@
     inner = core_sum(inner)
     inner, gram = lax.optimization_barrier((inner, lax.all_gather(gram, "core", axis=0, tiled=True)))
     inner = exchange(inner, "z").sum(axis=0)
-    corners, ab = gram[PANEL : PANEL + half], gram[PANEL + half :]
-    unread = jnp.zeros((half, half), jnp.float32)
-    aa = jnp.concatenate([gram[:half], jnp.concatenate([unread, corners[:, :half]], axis=1)], axis=0)
-    bb = jnp.concatenate([gram[half:PANEL], jnp.concatenate([unread, corners[:, half:]], axis=1)], axis=0)
-
-    inner, inverse_1 = lax.optimization_barrier((inner, factor(aa)))
-    cross = product(inverse_1, ab)
-    inner, inverse_2 = lax.optimization_barrier((gather(inner, "z"), factor(bb - product_t(cross, cross))))
+    square, row = (PANEL, PANEL), (1, PANEL)
+    inverse_1, growth_1 = on_chip(first_kernel, 10_000_000_000, square, row)(gram)
+    inner, inverse_1 = lax.optimization_barrier((inner, inverse_1))
+    inverse_2, growth_2, cross = on_chip(second_kernel, 11_000_000_000, square, row, square)(gram, inverse_1)
+    inner, inverse_2 = lax.optimization_barrier((gather(inner, "z"), inverse_2))
     inner = lax.all_gather(inner, "core", axis=0, tiled=True)
     ax, bx = inner[:PANEL], inner[PANEL:]
     inner_1 = product(inverse_1, ax)
@@ -224,7 +285,7 @@
     both = jnp.concatenate([a, b], axis=1)
     weight = jnp.concatenate([weight_a, weight_b], axis=0)
     result = flat * scale - product(both, weight)
-    return (result.reshape(rows, side, width), jnp.stack([growth(inverse_1), growth(inverse_2)]))
+    return (result.reshape(rows, side, width), jnp.concatenate([growth_1, growth_2], axis=0))
 
 
 def solution(mesh):

time: 222 us -> 208 us (0.937)
  matrix products: 21.4 us -> 13 us
  Pallas kernels: 32.1 us -> 25.3 us
  waiting for transfers between devices: 38.5 us -> 44.4 us
  starting transfers between devices: 50.2 us -> 47.9 us
    dot_general x9 -> x5, matrix products: 14.9 us -> 7.88 us  [product_t(): lax.dot_general(left, right, dims, precision=lax.Precision.HIGHEST, prefe...]
    pallas_call x2 -> x3, Pallas kernels: 27.6 us -> 20.8 us  [on_chip(): pl.pallas_call(kernel, out_shape=[jax.ShapeDtypeStruct(shape, jnp.float32...]
    all_to_all x3, waiting for transfers between devices: 22.8 us -> 26.7 us  [exchange(): out = lax.all_to_all(value, axis, 0, 0, tiled=True)]
    all_to_all x2, starting transfers between devices: 9.99 us -> 7.48 us  [gather(): lax.all_to_all(copies.reshape((-1,) + value.shape[1:]), axis, 0, 0, tiled...]
    dot_general x5 -> x4, matrix products: 6.46 us -> 5.14 us  [product(): jnp.dot(left, right, precision=lax.Precision.HIGHEST, preferred_element_t...]
  transfers between devices with their start and end apart: 8 -> 8, of which waited for: 6 -> 7; matrix products, arithmetic and copies ran while one was open for 6% -> 6% of each run, Pallas kernels for 12% -> 9%
where the time goes in v3:
time: 208 us; the launch traced here: 207 us
  blocking collectives  58.8 us (28%)
  starting transfers between devices  47.9 us (23%)
  waiting for transfers between devices  44.4 us (21%)
  Pallas kernels  25.3 us (12%)
  matrix products  13 us (6%)
  other arithmetic  6.21 us (3%)
  between operations  5.96 us (3%)
  local copies, waits for them, and re-layouts  5.21 us (3%)
    all_to_all x2, blocking collectives, gather(): lax.all_to_all(copies.reshape((-1,) + value.shape[1:]), axis, 0, 0, tiled...  42.3 us
    all_to_all x3, starting transfers between devices, exchange(): out = lax.all_to_all(value, axis, 0, 0, tiled=True)  30.8 us
    all_to_all x3, waiting for transfers between devices, exchange(): out = lax.all_to_all(value, axis, 0, 0, tiled=True)  26.7 us
    pallas_call x3, Pallas kernels, on_chip(): pl.pallas_call(kernel, out_shape=[jax.ShapeDtypeStruct(shape, jnp.float32...  20.8 us
    all_to_all x1, blocking collectives, exchange(): out = lax.all_to_all(value, axis, 0, 0, tiled=True)  11.5 us
    all_to_all x2, waiting for transfers between devices, gather(): lax.all_to_all(copies.reshape((-1,) + value.shape[1:]), axis, 0, 0, tiled...  10.2 us
    dot_general x5, matrix products, product_t(): lax.dot_general(left, right, dims, precision=lax.Precision.HIGHEST, prefe...  7.88 us
    ppermute x2, waiting for transfers between devices, halos(): return (lax.ppermute(last, SITE, up), lax.ppermute(leading, SITE, down))  7.49 us
  transfers between devices with their start and end apart: 8, of which 7 were waited for; matrix products, arithmetic and copies ran while one was open for 6% of the time, Pallas kernels for 9%

profile of v3, /device:TPU:1, one launch (start us, length us, event | category | flops | bytes accessed | tf_op | source)
XLA Modules:
  0.0 206.8 jit_solution(3628308070720948090)
XLA Ops:
  0.6 1.4 fusion.25
  2.2 1.0 pad_maximum_fusion
  3.2 3.5 %collective-permute-start = (f32[7,128,256]{2,1,0:T(8,128)}, f32[7,128,256]{2,1,0:T(8,128)S(1)}, u32[]{:S(2)}, u32[]{:S(2)}) collective-permute-start(f32[7,128,256]{2,1,0:T(8,128)} %pad_maximum_fusion), channel_id=1, source_target_pairs={{0,32},{32,64},{64,96},{96,128},{128,160},{160,192},{192,224},{224... | collective-permute-start | bytes 2752520 | tf_op jit(solution)/shard_map/ppermute | solution.py:37
  6.7 1.0 pad_maximum_fusion.1
  7.7 3.4 %collective-permute-start.1 = (f32[7,128,256]{2,1,0:T(8,128)}, f32[7,128,256]{2,1,0:T(8,128)}, u32[]{:S(2)}, u32[]{:S(2)}) collective-permute-start(f32[7,128,256]{2,1,0:T(8,128)} %pad_maximum_fusion.1), channel_id=1, source_target_pairs={{32,0},{64,32},{96,64},{128,96},{160,128},{192,160},{224,192},{256... | collective-permute-start | bytes 2752520 | tf_op jit(solution)/shard_map/ppermute | solution.py:37
  11.4 0.9 copy.9
  12.3 1.2 fusion.16.weight_ref
  13.6 3.8 %collective-permute-done.before_ref = f32[7,128,256]{2,1,0:T(8,128)S(1)} collective-permute-done((f32[7,128,256]{2,1,0:T(8,128)}, f32[7,128,256]{2,1,0:T(8,128)S(1)}, u32[]{:S(2)}, u32[]{:S(2)}) %collective-permute-start) | collective-permute-done | bytes 917536 | tf_op jit(solution)/shard_map/ppermute | solution.py:37
  17.4 3.7 %collective-permute-done.1.after_ref = f32[7,128,256]{2,1,0:T(8,128)} collective-permute-done((f32[7,128,256]{2,1,0:T(8,128)}, f32[7,128,256]{2,1,0:T(8,128)}, u32[]{:S(2)}, u32[]{:S(2)}) %collective-permute-start.1) | collective-permute-done | bytes 917536 | tf_op jit(solution)/shard_map/ppermute | solution.py:37
  21.1 4.5 %shard_map.59 = f32[8,128,256]{2,1,0:T(8,128)} custom-call(f32[8,128,256]{2,1,0:T(8,128)S(1)} %copy-done.1, f32[8,128,256]{2,1,0:T(8,128)S(1)} %copy-done, f32[7,128,256]{2,1,0:T(8,128)S(1)} %collective-permute-done.before_ref, f32[7,128,256]{2,1,0:T(8,128)} %collective-permute-done.1.after_ref, f32[4,128,16]{2,1,0:T(8,128)S(1)} %fusion.16.weight_ref), custom_call_target="tpu_custom_call" | custom-call | flops 12000000 | bytes 6000000 | tf_op jit(solution)/shard_map/pallas_call | solution.py:70
  25.6 9.8 %all-to-all-start = ((f32[32,32,256]{2,1,0:T(8,128)}), f32[32,32,256]{2,1,0:T(8,128)S(1)}, u32[]{:S(2)}, u32[]{:S(2)}) async-start(f32[32,32,256]{2,1,0:T(8,128)} %bitcast.4), calls=%async_computation | async-start | bytes 2097152 | tf_op jit(solution)/shard_map/all_to_all | solution.py:21
  39.9 15.3 %all-to-all-done = f32[32,32,256]{2,1,0:T(8,128)S(1)} async-done(((f32[32,32,256]{2,1,0:T(8,128)}), f32[32,32,256]{2,1,0:T(8,128)S(1)}, u32[]{:S(2)}, u32[]{:S(2)}) %all-to-all-start) | async-done | bytes 1048608 | tf_op jit(solution)/shard_map/all_to_all | solution.py:21
  55.2 19.2 %all_to_all.66 = f32[8,64,256]{2,1,0:T(8,128)S(1)} all-to-all(f32[8,64,256]{2,1,0:T(8,128)S(1)} %broadcast_in_dim.10), channel_id=1, replica_groups=mesh['z'=8,'core'=2,'x'=4,'y'=8] {'y'}, dimensions={0} | all-to-all | bytes 1048576 | tf_op jit(solution)/shard_map/all_to_all | solution.py:28
  74.6 23.1 %all_to_all.67 = f32[4,512,256]{2,1,0:T(8,128)S(1)} all-to-all(f32[4,512,256]{2,1,0:T(8,128)S(1)} %broadcast_in_dim.12), channel_id=1, replica_groups=mesh['z'=8,'core'=2,'x'=4,'y'=8] {'x'}, dimensions={0} | all-to-all | bytes 4194304 | tf_op jit(solution)/shard_map/all_to_all | solution.py:28
  97.8 3.0 %shard_map.60 = f32[640,256]{1,0:T(8,128)S(1)} custom-call(f32[32,2,32,256]{3,2,1,0:T(8,128)S(1)} %bitcast.36), custom_call_target="tpu_custom_call" | custom-call | flops 4000000000 | bytes 524288 | tf_op jit(solution)/shard_map/pallas_call | solution.py:241
  100.8 11.5 %all_to_all.68 = f32[2,320,256]{2,1,0:T(8,128)S(1)} all-to-all(f32[2,320,256]{2,1,0:T(8,128)S(1)} %bitcast.37), channel_id=1, replica_groups=mesh['z'=8,'core'=2,'x'=4,'y'=8] {'core'}, dimensions={0} | all-to-all | bytes 1310720 | tf_op jit(solution)/shard_map/all_to_all | solution.py:21
  113.1 17.6 %all-to-all-start.4 = ((f32[8,40,256]{2,1,0:T(8,128)}), f32[8,40,256]{2,1,0:T(8,128)S(1)}, u32[]{:S(2)}, u32[]{:S(2)}) async-start(f32[8,40,256]{2,1,0:T(8,128)} %bitcast.12), calls=%async_computation.4 | async-start | bytes 655360 | tf_op jit(solution)/shard_map/all_to_all | solution.py:21
  130.7 3.0 %fusion.29 = f32[256,256]{1,0:T(8,128)S(1)} fusion(f32[1024,256]{1,0:T(8,128)S(1)} %bitcast.40, f32[1024,256]{1,0:T(8,128)} %bitcast.1), kind=kOutput, calls=%fused_computation.44 | convolution fusion | flops 805306368 | bytes 2359296 | tf_op jit(solution)/shard_map/dot_general | solution.py:94
  133.7 3.0 %fusion.28 = f32[256,256]{1,0:T(8,128)S(1)} fusion(f32[1024,256]{1,0:T(8,128)S(1)} %bitcast.38, f32[1024,256]{1,0:T(8,128)} %bitcast.1), kind=kOutput, calls=%fused_computation.43 | convolution fusion | flops 805306368 | bytes 2359296 | tf_op jit(solution)/shard_map/dot_general | solution.py:94
  136.8 7.5 %all-to-all-done.4 = f32[8,40,256]{2,1,0:T(8,128)S(1)} async-done(((f32[8,40,256]{2,1,0:T(8,128)}), f32[8,40,256]{2,1,0:T(8,128)S(1)}, u32[]{:S(2)}, u32[]{:S(2)}) %all-to-all-start.4) | async-done | bytes 327712 | tf_op jit(solution)/shard_map/all_to_all | solution.py:21
  145.1 3.4 %all-to-all-start.5 = ((f32[8,40,256]{2,1,0:T(8,128)}), f32[8,40,256]{2,1,0:T(8,128)S(1)}, u32[]{:S(2)}, u32[]{:S(2)}) async-start(f32[8,40,256]{2,1,0:T(8,128)} %broadcast_in_dim.13), calls=%async_computation.5 | async-start | bytes 655360 | tf_op jit(solution)/shard_map/all_to_all | solution.py:28
  149.3 2.7 %collective-permute-start.2 = (f32[256,256]{1,0:T(8,128)}, f32[256,256]{1,0:T(8,128)S(1)}, u32[]{:S(2)}, u32[]{:S(2)}) collective-permute-start(f32[256,256]{1,0:T(8,128)} %fusion.17), channel_id=1, source_target_pairs={{0,32},{32,0},{1,33},{33,1},{2,34},{34,2},{3,35},{35,3},{4,36},{36... | collective-permute-start | bytes 786440 | tf_op jit(solution)/shard_map/ppermute | solution.py:85
  154.1 8.0 %all-to-all-done.5 = f32[8,40,256]{2,1,0:T(8,128)S(1)} async-done(((f32[8,40,256]{2,1,0:T(8,128)}), f32[8,40,256]{2,1,0:T(8,128)S(1)}, u32[]{:S(2)}, u32[]{:S(2)}) %all-to-all-start.5) | async-done | bytes 327712 | tf_op jit(solution)/shard_map/all_to_all | solution.py:28
  162.1 2.4 %all_gather.6.gram_ref = f32[640,256]{1,0:T(8,128)S(1)} all-gather(f32[320,256]{1,0:T(8,128)S(1)} %bitcast.43), channel_id=1, replica_groups=mesh['z'=8,'core'=2,'x'=4,'y'=8] {'core'}, dimensions={0}, use_global_device_ids=true | all-gather | bytes 983040 | tf_op jit(solution)/shard_map/all_gather | solution.py:264
  164.6 3.4 %all-to-all-start.6 = ((f32[8,32,256]{2,1,0:T(8,128)}), f32[8,32,256]{2,1,0:T(8,128)S(1)}, u32[]{:S(2)}, u32[]{:S(2)}) async-start(f32[8,32,256]{2,1,0:T(8,128)} %bitcast.45), calls=%async_computation.6 | async-start | bytes 524288 | tf_op jit(solution)/shard_map/all_to_all | solution.py:21
  168.0 8.3 %shard_map.61 = (f32[256,256]{1,0:T(8,128)S(1)}, f32[1,256]{1,0:T(1,128)S(1)}) custom-call(f32[640,256]{1,0:T(8,128)S(1)} %all_gather.6.gram_ref), custom_call_target="tpu_custom_call" | custom-call | flops 10000000000 | bytes 524288 | tf_op jit(solution)/shard_map/pallas_call | solution.py:241
  176.3 3.9 %all-to-all-done.6 = f32[8,32,256]{2,1,0:T(8,128)S(1)} async-done(((f32[8,32,256]{2,1,0:T(8,128)}), f32[8,32,256]{2,1,0:T(8,128)S(1)}, u32[]{:S(2)}, u32[]{:S(2)}) %all-to-all-start.6) | async-done | bytes 262176 | tf_op jit(solution)/shard_map/all_to_all | solution.py:21
  181.0 4.0 %all-to-all-start.7 = ((f32[8,32,256]{2,1,0:T(8,128)}), f32[8,32,256]{2,1,0:T(8,128)}, u32[]{:S(2)}, u32[]{:S(2)}) async-start(f32[8,32,256]{2,1,0:T(8,128)} %broadcast_in_dim.14), calls=%async_computation.7 | async-start | bytes 524288 | tf_op jit(solution)/shard_map/all_to_all | solution.py:28
  185.0 9.4 %shard_map.62 = (f32[256,256]{1,0:T(8,128)S(1)}, f32[1,256]{1,0:T(1,128)S(1)}, f32[256,256]{1,0:T(8,128)S(1)}) custom-call(f32[640,256]{1,0:T(8,128)S(1)} %all_gather.6.gram_ref, f32[256,256]{1,0:T(8,128)S(1)} %get-tuple-element.22.inverse_ref), custom_call_target="tpu_custom_call" | custom-call | flops 11000000512 | bytes 524288 | tf_op jit(solution)/shard_map/pallas_call | solution.py:241
  195.1 2.2 %all-to-all-done.7 = f32[8,32,256]{2,1,0:T(8,128)} async-done(((f32[8,32,256]{2,1,0:T(8,128)}), f32[8,32,256]{2,1,0:T(8,128)}, u32[]{:S(2)}, u32[]{:S(2)}) %all-to-all-start.7) | async-done | bytes 262176 | tf_op jit(solution)/shard_map/all_to_all | solution.py:28
  197.2 2.6 %all_gather.7 = f32[512,256]{1,0:T(8,128)S(1)} all-gather(f32[256,256]{1,0:T(8,128)} %bitcast.15), channel_id=1, replica_groups=mesh['z'=8,'core'=2,'x'=4,'y'=8] {'core'}, dimensions={0}, use_global_device_ids=true | all-gather | bytes 786432 | tf_op jit(solution)/shard_map/all_gather | solution.py:271
  202.8 4.0 %multiply_subtract_fusion = f32[1024,256]{1,0:T(8,128)} fusion(f32[1024,256]{1,0:T(8,128)} %bitcast.1, f32[1024,256]{1,0:T(8,128)S(1)} %bitcast.41, f32[1024,256]{1,0:T(8,128)S(1)} %bitcast.39, f32[256,256]{1,0:T(8,128)S(1)} %fusion.30, f32[256,256]{1,0:T(8,128)S(1)} %fusion.31, f32[]{:T(128)S(6)} %select_n.43), kind=kOutput, calls=%fused_computation.9 | convolution fusion | flops 1611792384 | bytes 4718596 | tf_op jit(solution)/shard_map/dot_general | solution.py:89
  (33 shorter events, 8.9 us)
Async XLA Ops:
  0.6 1.5 copy-start.1
  2.2 8.9 %copy-start.2 = (s32[4,128,128]{2,1,0:T(8,128)S(1)}, s32[4,128,128]{2,1,0:T(8,128)}, u32[]{:S(2)}) copy-start(s32[4,128,128]{2,1,0:T(8,128)} %param.6) | copy-start | bytes 786436
  3.2 17.8 %copy-start = (f32[8,128,256]{2,1,0:T(8,128)S(1)}, f32[8,128,256]{2,1,0:T(8,128)}, u32[]{:S(2)}) copy-start(f32[8,128,256]{2,1,0:T(8,128)} %current_ref.1) | copy-start | bytes 3145732
  3.2 14.1 %collective-permute-start = (f32[7,128,256]{2,1,0:T(8,128)}, f32[7,128,256]{2,1,0:T(8,128)S(1)}, u32[]{:S(2)}, u32[]{:S(2)}) collective-permute-start(f32[7,128,256]{2,1,0:T(8,128)} %pad_maximum_fusion), channel_id=1, source_target_pairs={{0,32},{32,64},{64,96},{96,128},{128,160},{160,192},{192,224},{224... | collective-permute-start | bytes 2752520 | tf_op jit(solution)/shard_map/ppermute | solution.py:37
  7.7 13.3 %collective-permute-start.1 = (f32[7,128,256]{2,1,0:T(8,128)}, f32[7,128,256]{2,1,0:T(8,128)}, u32[]{:S(2)}, u32[]{:S(2)}) collective-permute-start(f32[7,128,256]{2,1,0:T(8,128)} %pad_maximum_fusion.1), channel_id=1, source_target_pairs={{32,0},{64,32},{96,64},{128,96},{160,128},{192,160},{224,192},{256... | collective-permute-start | bytes 2752520 | tf_op jit(solution)/shard_map/ppermute | solution.py:37
  25.6 9.8 %copy-start.3 = (s32[32]{0:T(128)S(1)}, s32[32]{0:T(128)}, u32[]{:S(2)}) copy-start(s32[32]{0:T(128)} %param.7) | copy-start | bytes 388
  25.6 29.5 %all-to-all-start = ((f32[32,32,256]{2,1,0:T(8,128)}), f32[32,32,256]{2,1,0:T(8,128)S(1)}, u32[]{:S(2)}, u32[]{:S(2)}) async-start(f32[32,32,256]{2,1,0:T(8,128)} %bitcast.4), calls=%async_computation | async-start | bytes 2097152 | tf_op jit(solution)/shard_map/all_to_all | solution.py:21
  113.1 31.2 %all-to-all-start.4 = ((f32[8,40,256]{2,1,0:T(8,128)}), f32[8,40,256]{2,1,0:T(8,128)S(1)}, u32[]{:S(2)}, u32[]{:S(2)}) async-start(f32[8,40,256]{2,1,0:T(8,128)} %bitcast.12), calls=%async_computation.4 | async-start | bytes 655360 | tf_op jit(solution)/shard_map/all_to_all | solution.py:21
  145.1 17.0 %all-to-all-start.5 = ((f32[8,40,256]{2,1,0:T(8,128)}), f32[8,40,256]{2,1,0:T(8,128)S(1)}, u32[]{:S(2)}, u32[]{:S(2)}) async-start(f32[8,40,256]{2,1,0:T(8,128)} %broadcast_in_dim.13), calls=%async_computation.5 | async-start | bytes 655360 | tf_op jit(solution)/shard_map/all_to_all | solution.py:28
  149.3 4.0 %collective-permute-start.2 = (f32[256,256]{1,0:T(8,128)}, f32[256,256]{1,0:T(8,128)S(1)}, u32[]{:S(2)}, u32[]{:S(2)}) collective-permute-start(f32[256,256]{1,0:T(8,128)} %fusion.17), channel_id=1, source_target_pairs={{0,32},{32,0},{1,33},{33,1},{2,34},{34,2},{3,35},{35,3},{4,36},{36... | collective-permute-start | bytes 786440 | tf_op jit(solution)/shard_map/ppermute | solution.py:85
  164.6 15.7 %all-to-all-start.6 = ((f32[8,32,256]{2,1,0:T(8,128)}), f32[8,32,256]{2,1,0:T(8,128)S(1)}, u32[]{:S(2)}, u32[]{:S(2)}) async-start(f32[8,32,256]{2,1,0:T(8,128)} %bitcast.45), calls=%async_computation.6 | async-start | bytes 524288 | tf_op jit(solution)/shard_map/all_to_all | solution.py:21
  181.0 16.3 %all-to-all-start.7 = ((f32[8,32,256]{2,1,0:T(8,128)}), f32[8,32,256]{2,1,0:T(8,128)}, u32[]{:S(2)}, u32[]{:S(2)}) async-start(f32[8,32,256]{2,1,0:T(8,128)} %broadcast_in_dim.14), calls=%async_computation.7 | async-start | bytes 524288 | tf_op jit(solution)/shard_map/all_to_all | solution.py:28

commit v4 on v3

--- a/solution.py
+++ b/solution.py
@@ -28,12 +28,32 @@
     return lax.all_to_all(copies.reshape((-1,) + value.shape[1:]), axis, 0, 0, tiled=True)
 
 
+def edges_kernel(previous_ref, current_ref, last_ref, leading_ref, sems):
+    rows, depth = current_ref.shape[0], STEPS
+    copies = [
+        pltpu.make_async_copy(previous_ref.at[pl.ds(rows - depth + 1, depth - 1)], last_ref.at[pl.ds(0, depth - 1)], sems.at[0]),
+        pltpu.make_async_copy(current_ref.at[pl.ds(rows - depth, depth)], last_ref.at[pl.ds(depth - 1, depth)], sems.at[1]),
+        pltpu.make_async_copy(previous_ref.at[pl.ds(0, depth - 1)], leading_ref.at[pl.ds(0, depth - 1)], sems.at[2]),
+        pltpu.make_async_copy(current_ref.at[pl.ds(0, depth)], leading_ref.at[pl.ds(depth - 1, depth)], sems.at[3]),
+    ]
+    for copy in copies:
+        copy.start()
+    for copy in copies:
+        copy.wait()
+
+
 def halos(previous, current):
-    size, length = lax.axis_size(SITE), current.shape[0]
+    size = lax.axis_size(SITE)
     up = [(i, (i + 1) % size) for i in range(size)]
     down = [(j, i) for i, j in up]
-    last = jnp.concatenate([previous[length - STEPS + 1 :], current[length - STEPS :]], axis=0)
-    leading = jnp.concatenate([previous[: STEPS - 1], current[:STEPS]], axis=0)
+    edge = jax.ShapeDtypeStruct((2 * STEPS - 1,) + current.shape[1:], jnp.float32)
+    last, leading = pl.pallas_call(
+        edges_kernel,
+        out_shape=[edge, edge],
+        in_specs=[pl.BlockSpec(memory_space=pl.ANY)] * 2,
+        out_specs=[pl.BlockSpec(memory_space=pl.ANY)] * 2,
+        scratch_shapes=[pltpu.SemaphoreType.DMA((4,))],
+    )(previous, current)
     return lax.ppermute(last, SITE, up), lax.ppermute(leading, SITE, down)
 
 
@@ -260,13 +280,13 @@
     a_late, b_late, gram = lax.optimization_barrier((a, b, gram))
     inner = jnp.concatenate([product_t(a_late, flat), product_t(b_late, flat)], axis=0)
     gram = gather(exchange(gram, "z").sum(axis=0), "z")
-    inner = core_sum(inner)
-    inner, gram = lax.optimization_barrier((inner, lax.all_gather(gram, "core", axis=0, tiled=True)))
+    inner, gram = lax.optimization_barrier((core_sum(inner), gram))
+    gram = lax.all_gather(gram, "core", axis=0, tiled=True)
     inner = exchange(inner, "z").sum(axis=0)
     square, row = (PANEL, PANEL), (1, PANEL)
-    inverse_1, growth_1 = on_chip(first_kernel, 10_000_000_000, square, row)(gram)
+    inverse_1, growth_1 = on_chip(first_kernel, 1000, square, row)(gram)
     inner, inverse_1 = lax.optimization_barrier((inner, inverse_1))
-    inverse_2, growth_2, cross = on_chip(second_kernel, 11_000_000_000, square, row, square)(gram, inverse_1)
+    inverse_2, growth_2, cross = on_chip(second_kernel, 1000, square, row, square)(gram, inverse_1)
     inner, inverse_2 = lax.optimization_barrier((gather(inner, "z"), inverse_2))
     inner = lax.all_gather(inner, "core", axis=0, tiled=True)
     ax, bx = inner[:PANEL], inner[PANEL:]

time: 208 us -> 260 us (1.25)
  Pallas kernels: 25.3 us -> 82 us
  waiting for transfers between devices: 44.4 us -> 38.6 us
    pallas_call x0 -> x1, Pallas kernels: none -> 56.7 us  [halos(): pl.pallas_call(edges_kernel, out_shape=[edge, edge], in_specs=[pl.BlockSp...]
    all_to_all x3, waiting for transfers between devices: 26.7 us -> 23.2 us  [exchange(): out = lax.all_to_all(value, axis, 0, 0, tiled=True)]
  transfers between devices with their start and end apart: 8 -> 8, of which waited for: 7 -> 7; matrix products, arithmetic and copies ran while one was open for 6% -> 5% of each run, Pallas kernels for 9% -> 7%
where the time goes in v4:
time: 260 us; the launch traced here: 259 us
  Pallas kernels  82 us (32%)
  blocking collectives  60.2 us (23%)
  starting transfers between devices  49.6 us (19%)
  waiting for transfers between devices  38.6 us (15%)
  matrix products  13.2 us (5%)
  between operations  5.93 us (2%)
  local copies, waits for them, and re-layouts  5.32 us (2%)
  other arithmetic  4.18 us (2%)
    pallas_call x1, Pallas kernels, halos(): pl.pallas_call(edges_kernel, out_shape=[edge, edge], in_specs=[pl.BlockSp...  56.7 us
    all_to_all x2, blocking collectives, gather(): lax.all_to_all(copies.reshape((-1,) + value.shape[1:]), axis, 0, 0, tiled...  42.4 us
    all_to_all x3, starting transfers between devices, exchange(): out = lax.all_to_all(value, axis, 0, 0, tiled=True)  30.6 us
    all_to_all x3, waiting for transfers between devices, exchange(): out = lax.all_to_all(value, axis, 0, 0, tiled=True)  23.2 us
    pallas_call x3, Pallas kernels, on_chip(): pl.pallas_call(kernel, out_shape=[jax.ShapeDtypeStruct(shape, jnp.float32...  20.8 us
    all_to_all x1, blocking collectives, exchange(): out = lax.all_to_all(value, axis, 0, 0, tiled=True)  11.5 us
    all_to_all x2, starting transfers between devices, gather(): lax.all_to_all(copies.reshape((-1,) + value.shape[1:]), axis, 0, 0, tiled...  9.59 us
    all_to_all x2, waiting for transfers between devices, gather(): lax.all_to_all(copies.reshape((-1,) + value.shape[1:]), axis, 0, 0, tiled...  8.17 us
  transfers between devices with their start and end apart: 8, of which 7 were waited for; matrix products, arithmetic and copies ran while one was open for 5% of the time, Pallas kernels for 7%

profile of v4, /device:TPU:1, one launch (start us, length us, event | category | flops | bytes accessed | tf_op | source)
XLA Modules:
  0.0 259.0 jit_solution(17957443842565120200)
XLA Ops:
  0.6 56.7 %shard_map.59 = (f32[7,128,256]{2,1,0:T(8,128)}, f32[7,128,256]{2,1,0:T(8,128)}) custom-call(f32[8,128,256]{2,1,0:T(8,128)} %previous_ref.3, f32[8,128,256]{2,1,0:T(8,128)} %current_ref.3), custom_call_target="tpu_custom_call" | custom-call | tf_op jit(solution)/shard_map/pallas_call | solution.py:50
  57.4 3.5 %collective-permute-start = (f32[7,128,256]{2,1,0:T(8,128)}, f32[7,128,256]{2,1,0:T(8,128)S(1)}, u32[]{:S(2)}, u32[]{:S(2)}) collective-permute-start(f32[7,128,256]{2,1,0:T(8,128)} %get-tuple-element.18), channel_id=1, source_target_pairs={{0,32},{32,64},{64,96},{96,128},{128,160},{160,192},{192,224},{224... | collective-permute-start | bytes 2752520 | tf_op jit(solution)/shard_map/ppermute | solution.py:57
  60.9 3.4 %collective-permute-start.1 = (f32[7,128,256]{2,1,0:T(8,128)}, f32[7,128,256]{2,1,0:T(8,128)}, u32[]{:S(2)}, u32[]{:S(2)}) collective-permute-start(f32[7,128,256]{2,1,0:T(8,128)} %get-tuple-element.19), channel_id=1, source_target_pairs={{32,0},{64,32},{96,64},{128,96},{160,128},{192,160},{224,192},{256... | collective-permute-start | bytes 2752520 | tf_op jit(solution)/shard_map/ppermute | solution.py:57
  64.3 1.1 copy.10
  66.3 0.9 copy.9
  67.2 1.2 fusion.16.weight_ref
  68.4 3.1 %collective-permute-done.before_ref = f32[7,128,256]{2,1,0:T(8,128)S(1)} collective-permute-done((f32[7,128,256]{2,1,0:T(8,128)}, f32[7,128,256]{2,1,0:T(8,128)S(1)}, u32[]{:S(2)}, u32[]{:S(2)}) %collective-permute-start) | collective-permute-done | bytes 917536 | tf_op jit(solution)/shard_map/ppermute | solution.py:57
  71.5 2.7 %collective-permute-done.1.after_ref = f32[7,128,256]{2,1,0:T(8,128)} collective-permute-done((f32[7,128,256]{2,1,0:T(8,128)}, f32[7,128,256]{2,1,0:T(8,128)}, u32[]{:S(2)}, u32[]{:S(2)}) %collective-permute-start.1) | collective-permute-done | bytes 917536 | tf_op jit(solution)/shard_map/ppermute | solution.py:57
  74.2 4.5 %shard_map.60 = f32[8,128,256]{2,1,0:T(8,128)} custom-call(f32[8,128,256]{2,1,0:T(8,128)S(1)} %copy-done, f32[8,128,256]{2,1,0:T(8,128)S(1)} %copy-done.1, f32[7,128,256]{2,1,0:T(8,128)S(1)} %collective-permute-done.before_ref, f32[7,128,256]{2,1,0:T(8,128)} %collective-permute-done.1.after_ref, f32[4,128,16]{2,1,0:T(8,128)S(1)} %fusion.16.weight_ref), custom_call_target="tpu_custom_call" | custom-call | flops 12000000 | bytes 6000000 | tf_op jit(solution)/shard_map/pallas_call | solution.py:90
  78.8 9.8 %all-to-all-start = ((f32[32,32,256]{2,1,0:T(8,128)}), f32[32,32,256]{2,1,0:T(8,128)S(1)}, u32[]{:S(2)}, u32[]{:S(2)}) async-start(f32[32,32,256]{2,1,0:T(8,128)} %bitcast.4), calls=%async_computation | async-start | bytes 2097152 | tf_op jit(solution)/shard_map/all_to_all | solution.py:21
  93.0 15.2 %all-to-all-done = f32[32,32,256]{2,1,0:T(8,128)S(1)} async-done(((f32[32,32,256]{2,1,0:T(8,128)}), f32[32,32,256]{2,1,0:T(8,128)S(1)}, u32[]{:S(2)}, u32[]{:S(2)}) %all-to-all-start) | async-done | bytes 1048608 | tf_op jit(solution)/shard_map/all_to_all | solution.py:21
  108.2 19.4 %all_to_all.66 = f32[8,64,256]{2,1,0:T(8,128)S(1)} all-to-all(f32[8,64,256]{2,1,0:T(8,128)S(1)} %broadcast_in_dim.10), channel_id=1, replica_groups=mesh['z'=8,'core'=2,'x'=4,'y'=8] {'y'}, dimensions={0} | all-to-all | bytes 1048576 | tf_op jit(solution)/shard_map/all_to_all | solution.py:28
  127.8 23.0 %all_to_all.67 = f32[4,512,256]{2,1,0:T(8,128)S(1)} all-to-all(f32[4,512,256]{2,1,0:T(8,128)S(1)} %broadcast_in_dim.12), channel_id=1, replica_groups=mesh['z'=8,'core'=2,'x'=4,'y'=8] {'x'}, dimensions={0} | all-to-all | bytes 4194304 | tf_op jit(solution)/shard_map/all_to_all | solution.py:28
  151.0 3.0 %shard_map.61 = f32[640,256]{1,0:T(8,128)S(1)} custom-call(f32[32,2,32,256]{3,2,1,0:T(8,128)S(1)} %bitcast.36), custom_call_target="tpu_custom_call" | custom-call | flops 4000000000 | bytes 524288 | tf_op jit(solution)/shard_map/pallas_call | solution.py:261
  154.0 11.5 %all_to_all.68 = f32[2,320,256]{2,1,0:T(8,128)S(1)} all-to-all(f32[2,320,256]{2,1,0:T(8,128)S(1)} %bitcast.37), channel_id=1, replica_groups=mesh['z'=8,'core'=2,'x'=4,'y'=8] {'core'}, dimensions={0} | all-to-all | bytes 1310720 | tf_op jit(solution)/shard_map/all_to_all | solution.py:21
  166.2 17.4 %all-to-all-start.4 = ((f32[8,40,256]{2,1,0:T(8,128)}), f32[8,40,256]{2,1,0:T(8,128)S(1)}, u32[]{:S(2)}, u32[]{:S(2)}) async-start(f32[8,40,256]{2,1,0:T(8,128)} %bitcast.12), calls=%async_computation.4 | async-start | bytes 655360 | tf_op jit(solution)/shard_map/all_to_all | solution.py:21
  183.6 3.1 %fusion.27 = f32[256,256]{1,0:T(8,128)S(1)} fusion(f32[1024,256]{1,0:T(8,128)S(1)} %bitcast.40, f32[1024,256]{1,0:T(8,128)} %bitcast.1), kind=kOutput, calls=%fused_computation.40 | convolution fusion | flops 805306368 | bytes 2359296 | tf_op jit(solution)/shard_map/dot_general | solution.py:114
  186.7 3.1 %fusion.26 = f32[256,256]{1,0:T(8,128)S(1)} fusion(f32[1024,256]{1,0:T(8,128)S(1)} %bitcast.38, f32[1024,256]{1,0:T(8,128)} %bitcast.1), kind=kOutput, calls=%fused_computation.39 | convolution fusion | flops 805306368 | bytes 2359296 | tf_op jit(solution)/shard_map/dot_general | solution.py:114
  189.8 7.4 %all-to-all-done.4 = f32[8,40,256]{2,1,0:T(8,128)S(1)} async-done(((f32[8,40,256]{2,1,0:T(8,128)}), f32[8,40,256]{2,1,0:T(8,128)S(1)}, u32[]{:S(2)}, u32[]{:S(2)}) %all-to-all-start.4) | async-done | bytes 327712 | tf_op jit(solution)/shard_map/all_to_all | solution.py:21
  198.0 3.4 %all-to-all-start.5 = ((f32[8,40,256]{2,1,0:T(8,128)}), f32[8,40,256]{2,1,0:T(8,128)S(1)}, u32[]{:S(2)}, u32[]{:S(2)}) async-start(f32[8,40,256]{2,1,0:T(8,128)} %broadcast_in_dim.13), calls=%async_computation.5 | async-start | bytes 655360 | tf_op jit(solution)/shard_map/all_to_all | solution.py:28
  201.4 0.8 fusion.17
  202.2 2.5 collective-permute-start.2
  204.7 1.3 collective-permute-done.2
  206.1 0.8 fusion.19
  206.8 8.2 %all-to-all-done.5 = f32[8,40,256]{2,1,0:T(8,128)S(1)} async-done(((f32[8,40,256]{2,1,0:T(8,128)}), f32[8,40,256]{2,1,0:T(8,128)S(1)}, u32[]{:S(2)}, u32[]{:S(2)}) %all-to-all-start.5) | async-done | bytes 327712 | tf_op jit(solution)/shard_map/all_to_all | solution.py:28
  215.0 3.4 %all-to-all-start.6 = ((f32[8,32,256]{2,1,0:T(8,128)}), f32[8,32,256]{2,1,0:T(8,128)S(1)}, u32[]{:S(2)}, u32[]{:S(2)}) async-start(f32[8,32,256]{2,1,0:T(8,128)} %bitcast.45), calls=%async_computation.6 | async-start | bytes 524288 | tf_op jit(solution)/shard_map/all_to_all | solution.py:21
  218.4 2.6 %all_gather.6.gram_ref = f32[640,256]{1,0:T(8,128)S(1)} all-gather(f32[320,256]{1,0:T(8,128)S(1)} %bitcast.43), channel_id=1, replica_groups=mesh['z'=8,'core'=2,'x'=4,'y'=8] {'core'}, dimensions={0}, use_global_device_ids=true | all-gather | bytes 983040 | tf_op jit(solution)/shard_map/all_gather | solution.py:284
  221.1 8.3 %shard_map.62 = (f32[256,256]{1,0:T(8,128)S(1)}, f32[1,256]{1,0:T(1,128)S(1)}) custom-call(f32[640,256]{1,0:T(8,128)S(1)} %all_gather.6.gram_ref), custom_call_target="tpu_custom_call" | custom-call | flops 1000 | bytes 524288 | tf_op jit(solution)/shard_map/pallas_call | solution.py:261
  230.9 6.2 %all-to-all-start.7 = ((f32[8,32,256]{2,1,0:T(8,128)}), f32[8,32,256]{2,1,0:T(8,128)}, u32[]{:S(2)}, u32[]{:S(2)}) async-start(f32[8,32,256]{2,1,0:T(8,128)} %broadcast_in_dim.14), calls=%async_computation.7 | async-start | bytes 524288 | tf_op jit(solution)/shard_map/all_to_all | solution.py:28
  238.3 9.4 %shard_map.63 = (f32[256,256]{1,0:T(8,128)S(1)}, f32[1,256]{1,0:T(1,128)S(1)}, f32[256,256]{1,0:T(8,128)S(1)}) custom-call(f32[640,256]{1,0:T(8,128)S(1)} %all_gather.6.gram_ref, f32[256,256]{1,0:T(8,128)S(1)} %get-tuple-element.26.inverse_ref), custom_call_target="tpu_custom_call" | custom-call | flops 1000 | bytes 524288 | tf_op jit(solution)/shard_map/pallas_call | solution.py:261
  248.3 3.6 %all_gather.7 = f32[512,256]{1,0:T(8,128)S(1)} all-gather(f32[256,256]{1,0:T(8,128)} %bitcast.15), channel_id=1, replica_groups=mesh['z'=8,'core'=2,'x'=4,'y'=8] {'core'}, dimensions={0}, use_global_device_ids=true | all-gather | bytes 786432 | tf_op jit(solution)/shard_map/all_gather | solution.py:291
  255.0 4.0 %multiply_subtract_fusion = f32[1024,256]{1,0:T(8,128)} fusion(f32[1024,256]{1,0:T(8,128)} %bitcast.1, f32[1024,256]{1,0:T(8,128)S(1)} %bitcast.41, f32[1024,256]{1,0:T(8,128)S(1)} %bitcast.39, f32[256,256]{1,0:T(8,128)S(1)} %fusion.28, f32[256,256]{1,0:T(8,128)S(1)} %fusion.29, f32[]{:T(128)S(6)} %select_n.43), kind=kOutput, calls=%fused_computation.9 | convolution fusion | flops 1611792384 | bytes 4718596 | tf_op jit(solution)/shard_map/dot_general | solution.py:109
  (28 shorter events, 8.4 us)
Async XLA Ops:
  0.6 73.6 %copy-start = (f32[8,128,256]{2,1,0:T(8,128)S(1)}, f32[8,128,256]{2,1,0:T(8,128)}, u32[]{:S(2)}) copy-start(f32[8,128,256]{2,1,0:T(8,128)} %previous_ref.3) | copy-start | bytes 3145732
  0.6 73.6 %copy-start.1 = (f32[8,128,256]{2,1,0:T(8,128)S(1)}, f32[8,128,256]{2,1,0:T(8,128)}, u32[]{:S(2)}) copy-start(f32[8,128,256]{2,1,0:T(8,128)} %current_ref.3) | copy-start | bytes 3145732
  57.4 14.2 %collective-permute-start = (f32[7,128,256]{2,1,0:T(8,128)}, f32[7,128,256]{2,1,0:T(8,128)S(1)}, u32[]{:S(2)}, u32[]{:S(2)}) collective-permute-start(f32[7,128,256]{2,1,0:T(8,128)} %get-tuple-element.18), channel_id=1, source_target_pairs={{0,32},{32,64},{64,96},{96,128},{128,160},{160,192},{192,224},{224... | collective-permute-start | bytes 2752520 | tf_op jit(solution)/shard_map/ppermute | solution.py:57
  60.9 13.3 %collective-permute-start.1 = (f32[7,128,256]{2,1,0:T(8,128)}, f32[7,128,256]{2,1,0:T(8,128)}, u32[]{:S(2)}, u32[]{:S(2)}) collective-permute-start(f32[7,128,256]{2,1,0:T(8,128)} %get-tuple-element.19), channel_id=1, source_target_pairs={{32,0},{64,32},{96,64},{128,96},{160,128},{192,160},{224,192},{256... | collective-permute-start | bytes 2752520 | tf_op jit(solution)/shard_map/ppermute | solution.py:57
  78.7 9.8 %copy-start.2 = (s32[32]{0:T(128)S(1)}, s32[32]{0:T(128)}, u32[]{:S(2)}) copy-start(s32[32]{0:T(128)} %param.7) | copy-start | bytes 388
  78.8 29.4 %all-to-all-start = ((f32[32,32,256]{2,1,0:T(8,128)}), f32[32,32,256]{2,1,0:T(8,128)S(1)}, u32[]{:S(2)}, u32[]{:S(2)}) async-start(f32[32,32,256]{2,1,0:T(8,128)} %bitcast.4), calls=%async_computation | async-start | bytes 2097152 | tf_op jit(solution)/shard_map/all_to_all | solution.py:21
  166.2 31.0 %all-to-all-start.4 = ((f32[8,40,256]{2,1,0:T(8,128)}), f32[8,40,256]{2,1,0:T(8,128)S(1)}, u32[]{:S(2)}, u32[]{:S(2)}) async-start(f32[8,40,256]{2,1,0:T(8,128)} %bitcast.12), calls=%async_computation.4 | async-start | bytes 655360 | tf_op jit(solution)/shard_map/all_to_all | solution.py:21
  198.0 17.0 %all-to-all-start.5 = ((f32[8,40,256]{2,1,0:T(8,128)}), f32[8,40,256]{2,1,0:T(8,128)S(1)}, u32[]{:S(2)}, u32[]{:S(2)}) async-start(f32[8,40,256]{2,1,0:T(8,128)} %broadcast_in_dim.13), calls=%async_computation.5 | async-start | bytes 655360 | tf_op jit(solution)/shard_map/all_to_all | solution.py:28
  202.2 3.9 %collective-permute-start.2 = (f32[256,256]{1,0:T(8,128)}, f32[256,256]{1,0:T(8,128)S(1)}, u32[]{:S(2)}, u32[]{:S(2)}) collective-permute-start(f32[256,256]{1,0:T(8,128)} %fusion.17), channel_id=1, source_target_pairs={{0,32},{32,0},{1,33},{33,1},{2,34},{34,2},{3,35},{35,3},{4,36},{36... | collective-permute-start | bytes 786440 | tf_op jit(solution)/shard_map/ppermute | solution.py:105
  215.0 15.1 %all-to-all-start.6 = ((f32[8,32,256]{2,1,0:T(8,128)}), f32[8,32,256]{2,1,0:T(8,128)S(1)}, u32[]{:S(2)}, u32[]{:S(2)}) async-start(f32[8,32,256]{2,1,0:T(8,128)} %bitcast.45), calls=%async_computation.6 | async-start | bytes 524288 | tf_op jit(solution)/shard_map/all_to_all | solution.py:21
  230.9 17.5 %all-to-all-start.7 = ((f32[8,32,256]{2,1,0:T(8,128)}), f32[8,32,256]{2,1,0:T(8,128)}, u32[]{:S(2)}, u32[]{:S(2)}) async-start(f32[8,32,256]{2,1,0:T(8,128)} %broadcast_in_dim.14), calls=%async_computation.7 | async-start | bytes 524288 | tf_op jit(solution)/shard_map/all_to_all | solution.py:28

commit v5 on v4

--- a/solution.py
+++ b/solution.py
@@ -28,14 +28,15 @@
     return lax.all_to_all(copies.reshape((-1,) + value.shape[1:]), axis, 0, 0, tiled=True)
 
 
-def edges_kernel(previous_ref, current_ref, last_ref, leading_ref, sems):
+def edges_kernel(previous_ref, current_ref, far_ref, near_ref, sems):
     rows, depth = current_ref.shape[0], STEPS
-    copies = [
-        pltpu.make_async_copy(previous_ref.at[pl.ds(rows - depth + 1, depth - 1)], last_ref.at[pl.ds(0, depth - 1)], sems.at[0]),
-        pltpu.make_async_copy(current_ref.at[pl.ds(rows - depth, depth)], last_ref.at[pl.ds(depth - 1, depth)], sems.at[1]),
-        pltpu.make_async_copy(previous_ref.at[pl.ds(0, depth - 1)], leading_ref.at[pl.ds(0, depth - 1)], sems.at[2]),
-        pltpu.make_async_copy(current_ref.at[pl.ds(0, depth)], leading_ref.at[pl.ds(depth - 1, depth)], sems.at[3]),
-    ]
+    core = lax.axis_index("core")
+    copies = []
+    for n, (side, out_ref) in enumerate(((core, far_ref), (1 - core, near_ref))):
+        old = previous_ref.at[pl.ds(side * (rows - depth + 1), depth - 1)]
+        new = current_ref.at[pl.ds(side * (rows - depth), depth)]
+        copies.append(pltpu.make_async_copy(old, out_ref.at[pl.ds(0, depth - 1)], sems.at[2 * n]))
+        copies.append(pltpu.make_async_copy(new, out_ref.at[pl.ds(depth - 1, depth)], sems.at[2 * n + 1]))
     for copy in copies:
         copy.start()
     for copy in copies:
@@ -44,28 +45,33 @@
 
 def halos(previous, current):
     size = lax.axis_size(SITE)
-    up = [(i, (i + 1) % size) for i in range(size)]
-    down = [(j, i) for i, j in up]
     edge = jax.ShapeDtypeStruct((2 * STEPS - 1,) + current.shape[1:], jnp.float32)
-    last, leading = pl.pallas_call(
+    far, near = pl.pallas_call(
         edges_kernel,
         out_shape=[edge, edge],
         in_specs=[pl.BlockSpec(memory_space=pl.ANY)] * 2,
-        out_specs=[pl.BlockSpec(memory_space=pl.ANY)] * 2,
+        out_specs=[pl.BlockSpec(memory_space=pltpu.VMEM)] * 2,
         scratch_shapes=[pltpu.SemaphoreType.DMA((4,))],
     )(previous, current)
-    return lax.ppermute(last, SITE, up), lax.ppermute(leading, SITE, down)
-
-
-def window_kernel(previous_ref, current_ref, before_ref, after_ref, weight_ref, out_ref, even, odd):
+    swap = [(i, (i + 1 if i % 2 else i - 1) % size) for i in range(size)]
+    return lax.ppermute(far, SITE, swap), lax.ppermute(near, "core", [(0, 1), (1, 0)])
+
+
+def window_kernel(previous_ref, current_ref, far_ref, near_ref, weight_ref, out_ref, even, odd):
     rows = current_ref.shape[0]
     depth = STEPS
-    even[pl.ds(0, depth)] = before_ref[pl.ds(depth - 1, depth)]
+    core = lax.axis_index("core")
+
+    def place(before_ref, after_ref):
+        even[pl.ds(0, depth)] = before_ref[pl.ds(depth - 1, depth)]
+        even[pl.ds(depth + rows, depth)] = after_ref[pl.ds(depth - 1, depth)]
+        odd[pl.ds(1, depth - 1)] = before_ref[pl.ds(0, depth - 1)]
+        odd[pl.ds(depth + rows, depth - 1)] = after_ref[pl.ds(0, depth - 1)]
+
+    pl.when(core == 0)(lambda: place(far_ref, near_ref))
+    pl.when(core == 1)(lambda: place(near_ref, far_ref))
     even[pl.ds(depth, rows)] = current_ref[...]
-    even[pl.ds(depth + rows, depth)] = after_ref[pl.ds(depth - 1, depth)]
-    odd[pl.ds(1, depth - 1)] = before_ref[pl.ds(0, depth - 1)]
     odd[pl.ds(depth, rows)] = previous_ref[...]
-    odd[pl.ds(depth + rows, depth - 1)] = after_ref[pl.ds(0, depth - 1)]
     for turn in range(STEPS):
         current, previous = (even, odd) if turn % 2 == 0 else (odd, even)
         last = turn == STEPS - 1
@@ -82,7 +88,7 @@
 
 def window(previous, current, occupancy):
     rows, side, width = current.shape
-    before, after = halos(previous, current)
+    far, near = halos(previous, current)
     start = lax.axis_index(SITE) * rows
     around = jnp.concatenate([occupancy[:, side - STEPS :], occupancy, occupancy[:, :STEPS]], axis=1)
     weights = lax.dynamic_slice_in_dim(around, start, rows + 2 * STEPS, 1).astype(jnp.float32).transpose(0, 2, 1)
@@ -95,7 +101,7 @@
         scratch_shapes=[slab, slab],
         compiler_params=pltpu.CompilerParams(vmem_limit_bytes=32 * 1024 * 1024),
         cost_estimate=pl.CostEstimate(flops=12_000_000, bytes_accessed=6_000_000, transcendentals=0),
-    )(previous, current, before, after, weights)
+    )(previous, current, far, near, weights)
 
 
 def core_sum(value):

time: 260 us -> 208 us (0.80)
  Pallas kernels: 82 us -> 28.1 us
  starting transfers between devices: 49.6 us -> 57.7 us
  waiting for transfers between devices: 38.6 us -> 32.6 us
    pallas_call x1, Pallas kernels: 56.7 us -> 2.86 us  [halos(): pl.pallas_call(edges_kernel, out_shape=[edge, edge], in_specs=[pl.BlockSp...]
    ppermute x2, starting transfers between devices: 6.92 us -> 13.8 us  [the longest x1 8.41 us: halos(): lax.ppermute(near, 'core', [(0, 1), (1, 0)])]
    ppermute x2, waiting for transfers between devices: 5.81 us -> 0.01 us  [the longest x1 0.01 us: halos(): lax.ppermute(far, SITE, swap)]
  transfers between devices with their start and end apart: 8 -> 8, of which waited for: 7 -> 5; matrix products, arithmetic and copies ran while one was open for 5% -> 6% of each run, Pallas kernels for 7% -> 9%
where the time goes in v5:
time: 208 us; the launch traced here: 206 us
  blocking collectives  59.3 us (29%)
  starting transfers between devices  57.7 us (28%)
  waiting for transfers between devices  32.6 us (16%)
  Pallas kernels  28.1 us (14%)
  matrix products  13.2 us (6%)
  between operations  5.98 us (3%)
  local copies, waits for them, and re-layouts  5.32 us (3%)
  other arithmetic  4.18 us (2%)
    all_to_all x2, blocking collectives, gather(): lax.all_to_all(copies.reshape((-1,) + value.shape[1:]), axis, 0, 0, tiled...  40.9 us
    all_to_all x3, starting transfers between devices, exchange(): out = lax.all_to_all(value, axis, 0, 0, tiled=True)  31.8 us
    all_to_all x3, waiting for transfers between devices, exchange(): out = lax.all_to_all(value, axis, 0, 0, tiled=True)  23.3 us
    pallas_call x3, Pallas kernels, on_chip(): pl.pallas_call(kernel, out_shape=[jax.ShapeDtypeStruct(shape, jnp.float32...  20.8 us
    all_to_all x1, blocking collectives, exchange(): out = lax.all_to_all(value, axis, 0, 0, tiled=True)  12.3 us
    all_to_all x2, starting transfers between devices, gather(): lax.all_to_all(copies.reshape((-1,) + value.shape[1:]), axis, 0, 0, tiled...  9.41 us
    ppermute x1, starting transfers between devices, halos(): lax.ppermute(near, 'core', [(0, 1), (1, 0)])  8.41 us
    all_to_all x2, waiting for transfers between devices, gather(): lax.all_to_all(copies.reshape((-1,) + value.shape[1:]), axis, 0, 0, tiled...  8.17 us
  transfers between devices with their start and end apart: 8, of which 5 were waited for; matrix products, arithmetic and copies ran while one was open for 6% of the time, Pallas kernels for 9%

profile of v5, /device:TPU:1, one launch (start us, length us, event | category | flops | bytes accessed | tf_op | source)
XLA Modules:
  0.0 206.4 jit_solution(8701131990893602506)
XLA Ops:
  0.6 2.9 %shard_map.59 = (f32[7,128,256]{2,1,0:T(8,128)}, f32[7,128,256]{2,1,0:T(8,128)}) custom-call(f32[8,128,256]{2,1,0:T(8,128)} %previous_ref.3, f32[8,128,256]{2,1,0:T(8,128)} %current_ref.3), custom_call_target="tpu_custom_call" | custom-call | tf_op jit(solution)/shard_map/pallas_call | solution.py:49
  3.5 5.4 %collective-permute-start = (f32[7,128,256]{2,1,0:T(8,128)}, f32[7,128,256]{2,1,0:T(8,128)S(1)}, u32[]{:S(2)}, u32[]{:S(2)}) collective-permute-start(f32[7,128,256]{2,1,0:T(8,128)} %get-tuple-element.18), channel_id=1, source_target_pairs={{0,480},{32,64},{64,32},{96,128},{128,96},{160,192},{192,160},{224... | collective-permute-start | bytes 2752520 | tf_op jit(solution)/shard_map/ppermute | solution.py:57
  8.9 8.4 %collective-permute-start.1 = (f32[7,128,256]{2,1,0:T(8,128)}, f32[7,128,256]{2,1,0:T(8,128)}, u32[]{:S(2)}, u32[]{:S(2)}) collective-permute-start(f32[7,128,256]{2,1,0:T(8,128)} %get-tuple-element.19), channel_id=1, source_target_pairs={{0,32},{32,0},{1,33},{33,1},{2,34},{34,2},{3,35},{35,3},{4,36},{36... | collective-permute-start | bytes 2752520 | tf_op jit(solution)/shard_map/ppermute | solution.py:57
  17.3 1.1 copy.10
  19.3 0.9 copy.9
  20.2 1.2 fusion.16.weight_ref
  21.5 4.5 %shard_map.60 = f32[8,128,256]{2,1,0:T(8,128)} custom-call(f32[8,128,256]{2,1,0:T(8,128)S(1)} %copy-done, f32[8,128,256]{2,1,0:T(8,128)S(1)} %copy-done.1, f32[7,128,256]{2,1,0:T(8,128)S(1)} %collective-permute-done.far_ref, f32[7,128,256]{2,1,0:T(8,128)} %collective-permute-done.1.near_ref, f32[4,128,16]{2,1,0:T(8,128)S(1)} %fusion.16.weight_ref), custom_call_target="tpu_custom_call" | custom-call | flops 12000000 | bytes 6000000 | tf_op jit(solution)/shard_map/pallas_call | solution.py:96
  26.0 9.8 %all-to-all-start = ((f32[32,32,256]{2,1,0:T(8,128)}), f32[32,32,256]{2,1,0:T(8,128)S(1)}, u32[]{:S(2)}, u32[]{:S(2)}) async-start(f32[32,32,256]{2,1,0:T(8,128)} %bitcast.4), calls=%async_computation | async-start | bytes 2097152 | tf_op jit(solution)/shard_map/all_to_all | solution.py:21
  40.3 15.0 %all-to-all-done = f32[32,32,256]{2,1,0:T(8,128)S(1)} async-done(((f32[32,32,256]{2,1,0:T(8,128)}), f32[32,32,256]{2,1,0:T(8,128)S(1)}, u32[]{:S(2)}, u32[]{:S(2)}) %all-to-all-start) | async-done | bytes 1048608 | tf_op jit(solution)/shard_map/all_to_all | solution.py:21
  55.4 18.5 %all_to_all.66 = f32[8,64,256]{2,1,0:T(8,128)S(1)} all-to-all(f32[8,64,256]{2,1,0:T(8,128)S(1)} %broadcast_in_dim.10), channel_id=1, replica_groups=mesh['z'=8,'core'=2,'x'=4,'y'=8] {'y'}, dimensions={0} | all-to-all | bytes 1048576 | tf_op jit(solution)/shard_map/all_to_all | solution.py:28
  74.1 22.4 %all_to_all.67 = f32[4,512,256]{2,1,0:T(8,128)S(1)} all-to-all(f32[4,512,256]{2,1,0:T(8,128)S(1)} %broadcast_in_dim.12), channel_id=1, replica_groups=mesh['z'=8,'core'=2,'x'=4,'y'=8] {'x'}, dimensions={0} | all-to-all | bytes 4194304 | tf_op jit(solution)/shard_map/all_to_all | solution.py:28
  96.6 3.0 %shard_map.61 = f32[640,256]{1,0:T(8,128)S(1)} custom-call(f32[32,2,32,256]{3,2,1,0:T(8,128)S(1)} %bitcast.36), custom_call_target="tpu_custom_call" | custom-call | flops 4000000000 | bytes 524288 | tf_op jit(solution)/shard_map/pallas_call | solution.py:267
  99.6 12.3 %all_to_all.68 = f32[2,320,256]{2,1,0:T(8,128)S(1)} all-to-all(f32[2,320,256]{2,1,0:T(8,128)S(1)} %bitcast.37), channel_id=1, replica_groups=mesh['z'=8,'core'=2,'x'=4,'y'=8] {'core'}, dimensions={0} | all-to-all | bytes 1310720 | tf_op jit(solution)/shard_map/all_to_all | solution.py:21
  111.9 0.8 reduce_sum.27
  112.7 18.6 %all-to-all-start.4 = ((f32[8,40,256]{2,1,0:T(8,128)}), f32[8,40,256]{2,1,0:T(8,128)S(1)}, u32[]{:S(2)}, u32[]{:S(2)}) async-start(f32[8,40,256]{2,1,0:T(8,128)} %bitcast.12), calls=%async_computation.4 | async-start | bytes 655360 | tf_op jit(solution)/shard_map/all_to_all | solution.py:21
  131.3 3.1 %fusion.27 = f32[256,256]{1,0:T(8,128)S(1)} fusion(f32[1024,256]{1,0:T(8,128)S(1)} %bitcast.40, f32[1024,256]{1,0:T(8,128)} %bitcast.1), kind=kOutput, calls=%fused_computation.40 | convolution fusion | flops 805306368 | bytes 2359296 | tf_op jit(solution)/shard_map/dot_general | solution.py:120
  134.4 3.1 %fusion.26 = f32[256,256]{1,0:T(8,128)S(1)} fusion(f32[1024,256]{1,0:T(8,128)S(1)} %bitcast.38, f32[1024,256]{1,0:T(8,128)} %bitcast.1), kind=kOutput, calls=%fused_computation.39 | convolution fusion | flops 805306368 | bytes 2359296 | tf_op jit(solution)/shard_map/dot_general | solution.py:120
  137.5 7.4 %all-to-all-done.4 = f32[8,40,256]{2,1,0:T(8,128)S(1)} async-done(((f32[8,40,256]{2,1,0:T(8,128)}), f32[8,40,256]{2,1,0:T(8,128)S(1)}, u32[]{:S(2)}, u32[]{:S(2)}) %all-to-all-start.4) | async-done | bytes 327712 | tf_op jit(solution)/shard_map/all_to_all | solution.py:21
  145.7 3.4 %all-to-all-start.5 = ((f32[8,40,256]{2,1,0:T(8,128)}), f32[8,40,256]{2,1,0:T(8,128)S(1)}, u32[]{:S(2)}, u32[]{:S(2)}) async-start(f32[8,40,256]{2,1,0:T(8,128)} %broadcast_in_dim.13), calls=%async_computation.5 | async-start | bytes 655360 | tf_op jit(solution)/shard_map/all_to_all | solution.py:28
  149.1 0.8 fusion.17
  149.9 2.7 %collective-permute-start.2 = (f32[256,256]{1,0:T(8,128)}, f32[256,256]{1,0:T(8,128)S(1)}, u32[]{:S(2)}, u32[]{:S(2)}) collective-permute-start(f32[256,256]{1,0:T(8,128)} %fusion.17), channel_id=1, source_target_pairs={{0,32},{32,0},{1,33},{33,1},{2,34},{34,2},{3,35},{35,3},{4,36},{36... | collective-permute-start | bytes 786440 | tf_op jit(solution)/shard_map/ppermute | solution.py:111
  152.6 1.2 collective-permute-done.2
  153.7 0.8 fusion.19
  154.5 8.2 %all-to-all-done.5 = f32[8,40,256]{2,1,0:T(8,128)S(1)} async-done(((f32[8,40,256]{2,1,0:T(8,128)}), f32[8,40,256]{2,1,0:T(8,128)S(1)}, u32[]{:S(2)}, u32[]{:S(2)}) %all-to-all-start.5) | async-done | bytes 327712 | tf_op jit(solution)/shard_map/all_to_all | solution.py:28
  162.7 3.4 %all-to-all-start.6 = ((f32[8,32,256]{2,1,0:T(8,128)}), f32[8,32,256]{2,1,0:T(8,128)S(1)}, u32[]{:S(2)}, u32[]{:S(2)}) async-start(f32[8,32,256]{2,1,0:T(8,128)} %bitcast.45), calls=%async_computation.6 | async-start | bytes 524288 | tf_op jit(solution)/shard_map/all_to_all | solution.py:21
  166.1 2.5 %all_gather.6.gram_ref = f32[640,256]{1,0:T(8,128)S(1)} all-gather(f32[320,256]{1,0:T(8,128)S(1)} %bitcast.43), channel_id=1, replica_groups=mesh['z'=8,'core'=2,'x'=4,'y'=8] {'core'}, dimensions={0}, use_global_device_ids=true | all-gather | bytes 983040 | tf_op jit(solution)/shard_map/all_gather | solution.py:290
  168.6 8.3 %shard_map.62 = (f32[256,256]{1,0:T(8,128)S(1)}, f32[1,256]{1,0:T(1,128)S(1)}) custom-call(f32[640,256]{1,0:T(8,128)S(1)} %all_gather.6.gram_ref), custom_call_target="tpu_custom_call" | custom-call | flops 1000 | bytes 524288 | tf_op jit(solution)/shard_map/pallas_call | solution.py:267
  176.9 0.9 all-to-all-done.6
  178.5 6.0 %all-to-all-start.7 = ((f32[8,32,256]{2,1,0:T(8,128)}), f32[8,32,256]{2,1,0:T(8,128)}, u32[]{:S(2)}, u32[]{:S(2)}) async-start(f32[8,32,256]{2,1,0:T(8,128)} %broadcast_in_dim.14), calls=%async_computation.7 | async-start | bytes 524288 | tf_op jit(solution)/shard_map/all_to_all | solution.py:28
  185.8 9.4 %shard_map.63 = (f32[256,256]{1,0:T(8,128)S(1)}, f32[1,256]{1,0:T(1,128)S(1)}, f32[256,256]{1,0:T(8,128)S(1)}) custom-call(f32[640,256]{1,0:T(8,128)S(1)} %all_gather.6.gram_ref, f32[256,256]{1,0:T(8,128)S(1)} %get-tuple-element.26.inverse_ref), custom_call_target="tpu_custom_call" | custom-call | flops 1000 | bytes 524288 | tf_op jit(solution)/shard_map/pallas_call | solution.py:267
  195.8 3.6 %all_gather.7 = f32[512,256]{1,0:T(8,128)S(1)} all-gather(f32[256,256]{1,0:T(8,128)} %bitcast.15), channel_id=1, replica_groups=mesh['z'=8,'core'=2,'x'=4,'y'=8] {'core'}, dimensions={0}, use_global_device_ids=true | all-gather | bytes 786432 | tf_op jit(solution)/shard_map/all_gather | solution.py:297
  202.4 4.0 %multiply_subtract_fusion = f32[1024,256]{1,0:T(8,128)} fusion(f32[1024,256]{1,0:T(8,128)} %bitcast.1, f32[1024,256]{1,0:T(8,128)S(1)} %bitcast.41, f32[1024,256]{1,0:T(8,128)S(1)} %bitcast.39, f32[256,256]{1,0:T(8,128)S(1)} %fusion.28, f32[256,256]{1,0:T(8,128)S(1)} %fusion.29, f32[]{:T(128)S(6)} %select_n.43), kind=kOutput, calls=%fused_computation.9 | convolution fusion | flops 1611792384 | bytes 4718596 | tf_op jit(solution)/shard_map/dot_general | solution.py:115
  (28 shorter events, 6.9 us)
Async XLA Ops:
  0.6 20.8 %copy-start = (f32[8,128,256]{2,1,0:T(8,128)S(1)}, f32[8,128,256]{2,1,0:T(8,128)}, u32[]{:S(2)}) copy-start(f32[8,128,256]{2,1,0:T(8,128)} %previous_ref.3) | copy-start | bytes 3145732
  0.6 20.8 %copy-start.1 = (f32[8,128,256]{2,1,0:T(8,128)S(1)}, f32[8,128,256]{2,1,0:T(8,128)}, u32[]{:S(2)}) copy-start(f32[8,128,256]{2,1,0:T(8,128)} %current_ref.3) | copy-start | bytes 3145732
  3.5 17.9 %collective-permute-start = (f32[7,128,256]{2,1,0:T(8,128)}, f32[7,128,256]{2,1,0:T(8,128)S(1)}, u32[]{:S(2)}, u32[]{:S(2)}) collective-permute-start(f32[7,128,256]{2,1,0:T(8,128)} %get-tuple-element.18), channel_id=1, source_target_pairs={{0,480},{32,64},{64,32},{96,128},{128,96},{160,192},{192,160},{224... | collective-permute-start | bytes 2752520 | tf_op jit(solution)/shard_map/ppermute | solution.py:57
  8.9 12.5 %collective-permute-start.1 = (f32[7,128,256]{2,1,0:T(8,128)}, f32[7,128,256]{2,1,0:T(8,128)}, u32[]{:S(2)}, u32[]{:S(2)}) collective-permute-start(f32[7,128,256]{2,1,0:T(8,128)} %get-tuple-element.19), channel_id=1, source_target_pairs={{0,32},{32,0},{1,33},{33,1},{2,34},{34,2},{3,35},{35,3},{4,36},{36... | collective-permute-start | bytes 2752520 | tf_op jit(solution)/shard_map/ppermute | solution.py:57
  26.0 9.8 %copy-start.2 = (s32[32]{0:T(128)S(1)}, s32[32]{0:T(128)}, u32[]{:S(2)}) copy-start(s32[32]{0:T(128)} %param.7) | copy-start | bytes 388
  26.0 29.3 %all-to-all-start = ((f32[32,32,256]{2,1,0:T(8,128)}), f32[32,32,256]{2,1,0:T(8,128)S(1)}, u32[]{:S(2)}, u32[]{:S(2)}) async-start(f32[32,32,256]{2,1,0:T(8,128)} %bitcast.4), calls=%async_computation | async-start | bytes 2097152 | tf_op jit(solution)/shard_map/all_to_all | solution.py:21
  112.7 32.2 %all-to-all-start.4 = ((f32[8,40,256]{2,1,0:T(8,128)}), f32[8,40,256]{2,1,0:T(8,128)S(1)}, u32[]{:S(2)}, u32[]{:S(2)}) async-start(f32[8,40,256]{2,1,0:T(8,128)} %bitcast.12), calls=%async_computation.4 | async-start | bytes 655360 | tf_op jit(solution)/shard_map/all_to_all | solution.py:21
  145.7 17.0 %all-to-all-start.5 = ((f32[8,40,256]{2,1,0:T(8,128)}), f32[8,40,256]{2,1,0:T(8,128)S(1)}, u32[]{:S(2)}, u32[]{:S(2)}) async-start(f32[8,40,256]{2,1,0:T(8,128)} %broadcast_in_dim.13), calls=%async_computation.5 | async-start | bytes 655360 | tf_op jit(solution)/shard_map/all_to_all | solution.py:28
  149.9 3.9 %collective-permute-start.2 = (f32[256,256]{1,0:T(8,128)}, f32[256,256]{1,0:T(8,128)S(1)}, u32[]{:S(2)}, u32[]{:S(2)}) collective-permute-start(f32[256,256]{1,0:T(8,128)} %fusion.17), channel_id=1, source_target_pairs={{0,32},{32,0},{1,33},{33,1},{2,34},{34,2},{3,35},{35,3},{4,36},{36... | collective-permute-start | bytes 786440 | tf_op jit(solution)/shard_map/ppermute | solution.py:111
  162.7 15.1 %all-to-all-start.6 = ((f32[8,32,256]{2,1,0:T(8,128)}), f32[8,32,256]{2,1,0:T(8,128)S(1)}, u32[]{:S(2)}, u32[]{:S(2)}) async-start(f32[8,32,256]{2,1,0:T(8,128)} %bitcast.45), calls=%async_computation.6 | async-start | bytes 524288 | tf_op jit(solution)/shard_map/all_to_all | solution.py:21
  178.5 17.3 %all-to-all-start.7 = ((f32[8,32,256]{2,1,0:T(8,128)}), f32[8,32,256]{2,1,0:T(8,128)}, u32[]{:S(2)}, u32[]{:S(2)}) async-start(f32[8,32,256]{2,1,0:T(8,128)} %broadcast_in_dim.14), calls=%async_computation.7 | async-start | bytes 524288 | tf_op jit(solution)/shard_map/all_to_all | solution.py:28

commit v6 on v5

--- a/solution.py
+++ b/solution.py
@@ -1,3 +1,5 @@
+import functools
+
 import jax
 import jax.numpy as jnp
 from jax import lax
@@ -28,15 +30,13 @@
     return lax.all_to_all(copies.reshape((-1,) + value.shape[1:]), axis, 0, 0, tiled=True)
 
 
-def edges_kernel(previous_ref, current_ref, far_ref, near_ref, sems):
+def edge_kernel(far, previous_ref, current_ref, old_ref, new_ref, sems):
     rows, depth = current_ref.shape[0], STEPS
     core = lax.axis_index("core")
-    copies = []
-    for n, (side, out_ref) in enumerate(((core, far_ref), (1 - core, near_ref))):
-        old = previous_ref.at[pl.ds(side * (rows - depth + 1), depth - 1)]
-        new = current_ref.at[pl.ds(side * (rows - depth), depth)]
-        copies.append(pltpu.make_async_copy(old, out_ref.at[pl.ds(0, depth - 1)], sems.at[2 * n]))
-        copies.append(pltpu.make_async_copy(new, out_ref.at[pl.ds(depth - 1, depth)], sems.at[2 * n + 1]))
+    side = core if far else 1 - core
+    old = previous_ref.at[pl.ds(side * (rows - depth + 1), depth - 1)]
+    new = current_ref.at[pl.ds(side * (rows - depth), depth)]
+    copies = [pltpu.make_async_copy(new, new_ref, sems.at[0]), pltpu.make_async_copy(old, old_ref, sems.at[1])]
     for copy in copies:
         copy.start()
     for copy in copies:
@@ -45,31 +45,33 @@
 
 def halos(previous, current):
     size = lax.axis_size(SITE)
-    edge = jax.ShapeDtypeStruct((2 * STEPS - 1,) + current.shape[1:], jnp.float32)
-    far, near = pl.pallas_call(
-        edges_kernel,
-        out_shape=[edge, edge],
-        in_specs=[pl.BlockSpec(memory_space=pl.ANY)] * 2,
-        out_specs=[pl.BlockSpec(memory_space=pltpu.VMEM)] * 2,
-        scratch_shapes=[pltpu.SemaphoreType.DMA((4,))],
-    )(previous, current)
-    swap = [(i, (i + 1 if i % 2 else i - 1) % size) for i in range(size)]
-    return lax.ppermute(far, SITE, swap), lax.ppermute(near, "core", [(0, 1), (1, 0)])
-
-
-def window_kernel(previous_ref, current_ref, far_ref, near_ref, weight_ref, out_ref, even, odd):
+    out = []
+    for far in (True, False):
+        old, new = pl.pallas_call(
+            functools.partial(edge_kernel, far),
+            out_shape=[jax.ShapeDtypeStruct((n,) + current.shape[1:], jnp.float32) for n in (STEPS - 1, STEPS)],
+            in_specs=[pl.BlockSpec(memory_space=pl.ANY)] * 2,
+            out_specs=[pl.BlockSpec(memory_space=pltpu.VMEM)] * 2,
+            scratch_shapes=[pltpu.SemaphoreType.DMA((2,))],
+        )(previous, current)
+        swap = [(i, (i + 1 if i % 2 == far else i - 1) % size) for i in range(size)]
+        out += [lax.ppermute(old, SITE, swap), lax.ppermute(new, SITE, swap)]
+    return out
+
+
+def window_kernel(previous_ref, current_ref, far_old, far_new, near_old, near_new, weight_ref, out_ref, even, odd):
     rows = current_ref.shape[0]
     depth = STEPS
     core = lax.axis_index("core")
 
-    def place(before_ref, after_ref):
-        even[pl.ds(0, depth)] = before_ref[pl.ds(depth - 1, depth)]
-        even[pl.ds(depth + rows, depth)] = after_ref[pl.ds(depth - 1, depth)]
-        odd[pl.ds(1, depth - 1)] = before_ref[pl.ds(0, depth - 1)]
-        odd[pl.ds(depth + rows, depth - 1)] = after_ref[pl.ds(0, depth - 1)]
-
-    pl.when(core == 0)(lambda: place(far_ref, near_ref))
-    pl.when(core == 1)(lambda: place(near_ref, far_ref))
+    def place(before_old, before_new, after_old, after_new):
+        even[pl.ds(0, depth)] = before_new[...]
+        even[pl.ds(depth + rows, depth)] = after_new[...]
+        odd[pl.ds(1, depth - 1)] = before_old[...]
+        odd[pl.ds(depth + rows, depth - 1)] = after_old[...]
+
+    pl.when(core == 0)(lambda: place(far_old, far_new, near_old, near_new))
+    pl.when(core == 1)(lambda: place(near_old, near_new, far_old, far_new))
     even[pl.ds(depth, rows)] = current_ref[...]
     odd[pl.ds(depth, rows)] = previous_ref[...]
     for turn in range(STEPS):
@@ -88,7 +90,7 @@
 
 def window(previous, current, occupancy):
     rows, side, width = current.shape
-    far, near = halos(previous, current)
+    edges = halos(previous, current)
     start = lax.axis_index(SITE) * rows
     around = jnp.concatenate([occupancy[:, side - STEPS :], occupancy, occupancy[:, :STEPS]], axis=1)
     weights = lax.dynamic_slice_in_dim(around, start, rows + 2 * STEPS, 1).astype(jnp.float32).transpose(0, 2, 1)
@@ -96,12 +98,12 @@
     return pl.pallas_call(
         window_kernel,
         out_shape=jax.ShapeDtypeStruct(current.shape, jnp.float32),
-        in_specs=[pl.BlockSpec(memory_space=pltpu.VMEM)] * 5,
+        in_specs=[pl.BlockSpec(memory_space=pltpu.VMEM)] * 7,
         out_specs=pl.BlockSpec(memory_space=pltpu.VMEM),
         scratch_shapes=[slab, slab],
         compiler_params=pltpu.CompilerParams(vmem_limit_bytes=32 * 1024 * 1024),
         cost_estimate=pl.CostEstimate(flops=12_000_000, bytes_accessed=6_000_000, transcendentals=0),
-    )(previous, current, far, near, weights)
+    )(previous, current, *edges, weights)
 
 
 def core_sum(value):

time: 208 us -> 208 us (level)
  starting transfers between devices: 57.7 us -> 48.8 us
  waiting for transfers between devices: 32.6 us -> 37.3 us
  blocking collectives: 59.3 us -> 61.8 us
    all_to_all x3, starting transfers between devices: 31.8 us -> 17.4 us  [exchange(): out = lax.all_to_all(value, axis, 0, 0, tiled=True)]
    all_to_all x2, blocking collectives: 40.9 us -> 46.7 us  [gather(): lax.all_to_all(copies.reshape((-1,) + value.shape[1:]), axis, 0, 0, tiled...]
    all_to_all x3, waiting for transfers between devices: 23.3 us -> 28.4 us  [exchange(): out = lax.all_to_all(value, axis, 0, 0, tiled=True)]
    ppermute x2 -> x4, starting transfers between devices: 13.8 us -> 18.4 us  [halos(): out += [lax.ppermute(old, SITE, swap), lax.ppermute(new, SITE, swap)]]
    all_to_all x1, blocking collectives: 12.3 us -> 8.52 us  [exchange(): out = lax.all_to_all(value, axis, 0, 0, tiled=True)]
    pallas_call x1 -> x2, Pallas kernels: 2.86 us -> 4.2 us  [halos(): pl.pallas_call(functools.partial(edge_kernel, far), out_shape=[jax.ShapeD...]
  transfers between devices with their start and end apart: 8 -> 10, of which waited for: 5 -> 4; matrix products, arithmetic and copies ran while one was open for 6% -> 7% of each run, Pallas kernels for 9% -> 10%
where the time goes in v6:
time: 208 us; the launch traced here: 207 us
  blocking collectives  61.8 us (30%)
  starting transfers between devices  48.8 us (23%)
  waiting for transfers between devices  37.3 us (18%)
  Pallas kernels  29.3 us (14%)
  matrix products  13.2 us (6%)
  local copies, waits for them, and re-layouts  6.62 us (3%)
  between operations  5.76 us (3%)
  other arithmetic  4.32 us (2%)
    all_to_all x2, blocking collectives, gather(): lax.all_to_all(copies.reshape((-1,) + value.shape[1:]), axis, 0, 0, tiled...  46.7 us
    all_to_all x3, waiting for transfers between devices, exchange(): out = lax.all_to_all(value, axis, 0, 0, tiled=True)  28.4 us
    pallas_call x3, Pallas kernels, on_chip(): pl.pallas_call(kernel, out_shape=[jax.ShapeDtypeStruct(shape, jnp.float32...  20.8 us
    ppermute x4, starting transfers between devices, halos(): out += [lax.ppermute(old, SITE, swap), lax.ppermute(new, SITE, swap)]  18.4 us
    all_to_all x3, starting transfers between devices, exchange(): out = lax.all_to_all(value, axis, 0, 0, tiled=True)  17.4 us
    all_to_all x2, starting transfers between devices, gather(): lax.all_to_all(copies.reshape((-1,) + value.shape[1:]), axis, 0, 0, tiled...  10.4 us
    all_to_all x1, blocking collectives, exchange(): out = lax.all_to_all(value, axis, 0, 0, tiled=True)  8.52 us
    dot_general x5, matrix products, product_t(): lax.dot_general(left, right, dims, precision=lax.Precision.HIGHEST, prefe...  8.02 us
  transfers between devices with their start and end apart: 10, of which 4 were waited for; matrix products, arithmetic and copies ran while one was open for 7% of the time, Pallas kernels for 10%

profile of v6, /device:TPU:1, one launch (start us, length us, event | category | flops | bytes accessed | tf_op | source)
XLA Modules:
  0.0 207.1 jit_solution(6575121521724547037)
XLA Ops:
  0.6 2.1 %shard_map.59 = (f32[3,128,256]{2,1,0:T(8,128)}, f32[4,128,256]{2,1,0:T(8,128)}) custom-call(f32[8,128,256]{2,1,0:T(8,128)} %previous_ref.5, f32[8,128,256]{2,1,0:T(8,128)} %current_ref.5), custom_call_target="tpu_custom_call" | custom-call | tf_op jit(solution)/shard_map/pallas_call | solution.py:50
  2.8 5.5 %collective-permute-start.1 = (f32[4,128,256]{2,1,0:T(8,128)}, f32[4,128,256]{2,1,0:T(8,128)S(1)}, u32[]{:S(2)}, u32[]{:S(2)}) collective-permute-start(f32[4,128,256]{2,1,0:T(8,128)} %get-tuple-element.21), channel_id=1, source_target_pairs={{0,480},{32,64},{64,32},{96,128},{128,96},{160,192},{192,160},{224... | collective-permute-start | bytes 1572872 | tf_op jit(solution)/shard_map/ppermute | solution.py:58
  8.3 2.1 %shard_map.60 = (f32[3,128,256]{2,1,0:T(8,128)}, f32[4,128,256]{2,1,0:T(8,128)}) custom-call(f32[8,128,256]{2,1,0:T(8,128)} %previous_ref.5, f32[8,128,256]{2,1,0:T(8,128)} %current_ref.5), custom_call_target="tpu_custom_call" | custom-call | tf_op jit(solution)/shard_map/pallas_call | solution.py:50
  10.4 8.4 %collective-permute-start.3 = (f32[4,128,256]{2,1,0:T(8,128)}, f32[4,128,256]{2,1,0:T(8,128)S(1)}, u32[]{:S(2)}, u32[]{:S(2)}) collective-permute-start(f32[4,128,256]{2,1,0:T(8,128)} %get-tuple-element.23), channel_id=1, source_target_pairs={{0,32},{32,0},{64,96},{96,64},{128,160},{160,128},{192,224},{224,1... | collective-permute-start | bytes 1572872 | tf_op jit(solution)/shard_map/ppermute | solution.py:58
  18.8 1.9 collective-permute-start
  20.7 2.6 %collective-permute-start.2 = (f32[3,128,256]{2,1,0:T(8,128)}, f32[3,128,256]{2,1,0:T(8,128)}, u32[]{:S(2)}, u32[]{:S(2)}) collective-permute-start(f32[3,128,256]{2,1,0:T(8,128)} %get-tuple-element.22), channel_id=1, source_target_pairs={{0,32},{32,0},{64,96},{96,64},{128,160},{160,128},{192,224},{224,1... | collective-permute-start | bytes 1179656 | tf_op jit(solution)/shard_map/ppermute | solution.py:58
  23.3 1.8 copy.10
  25.9 0.9 copy.11
  26.7 0.9 copy.9
  27.6 1.4 fusion.16.weight_ref
  29.0 4.3 %shard_map.61 = f32[8,128,256]{2,1,0:T(8,128)} custom-call(f32[8,128,256]{2,1,0:T(8,128)S(1)} %copy-done, f32[8,128,256]{2,1,0:T(8,128)S(1)} %copy-done.1, f32[3,128,256]{2,1,0:T(8,128)S(1)} %collective-permute-done.far_old, f32[4,128,256]{2,1,0:T(8,128)S(1)} %collective-permute-done.1.far_new, f32[3,128,256]{2,1,0:T(8,128)} %collective-permute-done.2.near_old, ...), custom_call_target="tpu_custom_call" | custom-call | flops 12000000 | bytes 6000000 | tf_op jit(solution)/shard_map/pallas_call | solution.py:98
  33.4 9.8 %all-to-all-start = ((f32[32,32,256]{2,1,0:T(8,128)}), f32[32,32,256]{2,1,0:T(8,128)S(1)}, u32[]{:S(2)}, u32[]{:S(2)}) async-start(f32[32,32,256]{2,1,0:T(8,128)} %bitcast.4), calls=%async_computation | async-start | bytes 2097152 | tf_op jit(solution)/shard_map/all_to_all | solution.py:23
  47.4 21.0 %all-to-all-done = f32[32,32,256]{2,1,0:T(8,128)S(1)} async-done(((f32[32,32,256]{2,1,0:T(8,128)}), f32[32,32,256]{2,1,0:T(8,128)S(1)}, u32[]{:S(2)}, u32[]{:S(2)}) %all-to-all-start) | async-done | bytes 1048608 | tf_op jit(solution)/shard_map/all_to_all | solution.py:23
  68.4 19.9 %all_to_all.66 = f32[8,64,256]{2,1,0:T(8,128)S(1)} all-to-all(f32[8,64,256]{2,1,0:T(8,128)S(1)} %broadcast_in_dim.10), channel_id=1, replica_groups=mesh['z'=8,'core'=2,'x'=4,'y'=8] {'y'}, dimensions={0} | all-to-all | bytes 1048576 | tf_op jit(solution)/shard_map/all_to_all | solution.py:30
  88.5 26.8 %all_to_all.67 = f32[4,512,256]{2,1,0:T(8,128)S(1)} all-to-all(f32[4,512,256]{2,1,0:T(8,128)S(1)} %broadcast_in_dim.12), channel_id=1, replica_groups=mesh['z'=8,'core'=2,'x'=4,'y'=8] {'x'}, dimensions={0} | all-to-all | bytes 4194304 | tf_op jit(solution)/shard_map/all_to_all | solution.py:30
  115.4 3.0 %shard_map.62 = f32[640,256]{1,0:T(8,128)S(1)} custom-call(f32[32,2,32,256]{3,2,1,0:T(8,128)S(1)} %bitcast.36), custom_call_target="tpu_custom_call" | custom-call | flops 4000000000 | bytes 524288 | tf_op jit(solution)/shard_map/pallas_call | solution.py:269
  118.4 8.5 %all_to_all.68 = f32[2,320,256]{2,1,0:T(8,128)S(1)} all-to-all(f32[2,320,256]{2,1,0:T(8,128)S(1)} %bitcast.37), channel_id=1, replica_groups=mesh['z'=8,'core'=2,'x'=4,'y'=8] {'core'}, dimensions={0} | all-to-all | bytes 1310720 | tf_op jit(solution)/shard_map/all_to_all | solution.py:23
  127.7 4.2 %all-to-all-start.4 = ((f32[8,40,256]{2,1,0:T(8,128)}), f32[8,40,256]{2,1,0:T(8,128)S(1)}, u32[]{:S(2)}, u32[]{:S(2)}) async-start(f32[8,40,256]{2,1,0:T(8,128)} %bitcast.12), calls=%async_computation.4 | async-start | bytes 655360 | tf_op jit(solution)/shard_map/all_to_all | solution.py:23
  131.9 3.1 %fusion.27 = f32[256,256]{1,0:T(8,128)S(1)} fusion(f32[1024,256]{1,0:T(8,128)S(1)} %bitcast.40, f32[1024,256]{1,0:T(8,128)} %bitcast.1), kind=kOutput, calls=%fused_computation.40 | convolution fusion | flops 805306368 | bytes 2359296 | tf_op jit(solution)/shard_map/dot_general | solution.py:122
  135.0 3.1 %fusion.26 = f32[256,256]{1,0:T(8,128)S(1)} fusion(f32[1024,256]{1,0:T(8,128)S(1)} %bitcast.38, f32[1024,256]{1,0:T(8,128)} %bitcast.1), kind=kOutput, calls=%fused_computation.39 | convolution fusion | flops 805306368 | bytes 2359296 | tf_op jit(solution)/shard_map/dot_general | solution.py:122
  138.1 7.4 %all-to-all-done.4 = f32[8,40,256]{2,1,0:T(8,128)S(1)} async-done(((f32[8,40,256]{2,1,0:T(8,128)}), f32[8,40,256]{2,1,0:T(8,128)S(1)}, u32[]{:S(2)}, u32[]{:S(2)}) %all-to-all-start.4) | async-done | bytes 327712 | tf_op jit(solution)/shard_map/all_to_all | solution.py:23
  146.3 3.6 %all-to-all-start.5 = ((f32[8,40,256]{2,1,0:T(8,128)}), f32[8,40,256]{2,1,0:T(8,128)S(1)}, u32[]{:S(2)}, u32[]{:S(2)}) async-start(f32[8,40,256]{2,1,0:T(8,128)} %broadcast_in_dim.13), calls=%async_computation.5 | async-start | bytes 655360 | tf_op jit(solution)/shard_map/all_to_all | solution.py:30
  150.7 2.5 %collective-permute-start.4 = (f32[256,256]{1,0:T(8,128)}, f32[256,256]{1,0:T(8,128)S(1)}, u32[]{:S(2)}, u32[]{:S(2)}) collective-permute-start(f32[256,256]{1,0:T(8,128)} %fusion.17), channel_id=1, source_target_pairs={{0,32},{32,0},{1,33},{33,1},{2,34},{34,2},{3,35},{35,3},{4,36},{36... | collective-permute-start | bytes 786440 | tf_op jit(solution)/shard_map/ppermute | solution.py:113
  153.2 1.3 collective-permute-done.4
  155.3 7.6 %all-to-all-done.5 = f32[8,40,256]{2,1,0:T(8,128)S(1)} async-done(((f32[8,40,256]{2,1,0:T(8,128)}), f32[8,40,256]{2,1,0:T(8,128)S(1)}, u32[]{:S(2)}, u32[]{:S(2)}) %all-to-all-start.5) | async-done | bytes 327712 | tf_op jit(solution)/shard_map/all_to_all | solution.py:30
  162.9 3.4 %all-to-all-start.6 = ((f32[8,32,256]{2,1,0:T(8,128)}), f32[8,32,256]{2,1,0:T(8,128)S(1)}, u32[]{:S(2)}, u32[]{:S(2)}) async-start(f32[8,32,256]{2,1,0:T(8,128)} %bitcast.45), calls=%async_computation.6 | async-start | bytes 524288 | tf_op jit(solution)/shard_map/all_to_all | solution.py:23
  166.3 2.9 %all_gather.6.gram_ref = f32[640,256]{1,0:T(8,128)S(1)} all-gather(f32[320,256]{1,0:T(8,128)S(1)} %bitcast.43), channel_id=1, replica_groups=mesh['z'=8,'core'=2,'x'=4,'y'=8] {'core'}, dimensions={0}, use_global_device_ids=true | all-gather | bytes 983040 | tf_op jit(solution)/shard_map/all_gather | solution.py:292
  169.2 8.3 %shard_map.63 = (f32[256,256]{1,0:T(8,128)S(1)}, f32[1,256]{1,0:T(1,128)S(1)}) custom-call(f32[640,256]{1,0:T(8,128)S(1)} %all_gather.6.gram_ref), custom_call_target="tpu_custom_call" | custom-call | flops 1000 | bytes 524288 | tf_op jit(solution)/shard_map/pallas_call | solution.py:269
  178.3 6.8 %all-to-all-start.7 = ((f32[8,32,256]{2,1,0:T(8,128)}), f32[8,32,256]{2,1,0:T(8,128)}, u32[]{:S(2)}, u32[]{:S(2)}) async-start(f32[8,32,256]{2,1,0:T(8,128)} %broadcast_in_dim.14), calls=%async_computation.7 | async-start | bytes 524288 | tf_op jit(solution)/shard_map/all_to_all | solution.py:30
  186.3 9.4 %shard_map.64 = (f32[256,256]{1,0:T(8,128)S(1)}, f32[1,256]{1,0:T(1,128)S(1)}, f32[256,256]{1,0:T(8,128)S(1)}) custom-call(f32[640,256]{1,0:T(8,128)S(1)} %all_gather.6.gram_ref, f32[256,256]{1,0:T(8,128)S(1)} %get-tuple-element.30.inverse_ref), custom_call_target="tpu_custom_call" | custom-call | flops 1000 | bytes 524288 | tf_op jit(solution)/shard_map/pallas_call | solution.py:269
  196.4 3.7 %all_gather.7 = f32[512,256]{1,0:T(8,128)S(1)} all-gather(f32[256,256]{1,0:T(8,128)} %bitcast.15), channel_id=1, replica_groups=mesh['z'=8,'core'=2,'x'=4,'y'=8] {'core'}, dimensions={0}, use_global_device_ids=true | all-gather | bytes 786432 | tf_op jit(solution)/shard_map/all_gather | solution.py:299
  203.1 4.0 %multiply_subtract_fusion = f32[1024,256]{1,0:T(8,128)} fusion(f32[1024,256]{1,0:T(8,128)} %bitcast.1, f32[1024,256]{1,0:T(8,128)S(1)} %bitcast.41, f32[1024,256]{1,0:T(8,128)S(1)} %bitcast.39, f32[256,256]{1,0:T(8,128)S(1)} %fusion.28, f32[256,256]{1,0:T(8,128)S(1)} %fusion.29, f32[]{:T(128)S(6)} %select_n.43), kind=kOutput, calls=%fused_computation.9 | convolution fusion | flops 1611792384 | bytes 4718596 | tf_op jit(solution)/shard_map/dot_general | solution.py:117
  (33 shorter events, 9.0 us)
Async XLA Ops:
  2.7 26.3 %copy-start = (f32[8,128,256]{2,1,0:T(8,128)S(1)}, f32[8,128,256]{2,1,0:T(8,128)}, u32[]{:S(2)}) copy-start(f32[8,128,256]{2,1,0:T(8,128)} %previous_ref.5) | copy-start | bytes 3145732
  2.8 26.3 %copy-start.1 = (f32[8,128,256]{2,1,0:T(8,128)S(1)}, f32[8,128,256]{2,1,0:T(8,128)}, u32[]{:S(2)}) copy-start(f32[8,128,256]{2,1,0:T(8,128)} %current_ref.5) | copy-start | bytes 3145732
  2.8 26.2 %collective-permute-start.1 = (f32[4,128,256]{2,1,0:T(8,128)}, f32[4,128,256]{2,1,0:T(8,128)S(1)}, u32[]{:S(2)}, u32[]{:S(2)}) collective-permute-start(f32[4,128,256]{2,1,0:T(8,128)} %get-tuple-element.21), channel_id=1, source_target_pairs={{0,480},{32,64},{64,32},{96,128},{128,96},{160,192},{192,160},{224... | collective-permute-start | bytes 1572872 | tf_op jit(solution)/shard_map/ppermute | solution.py:58
  10.4 18.6 %collective-permute-start.3 = (f32[4,128,256]{2,1,0:T(8,128)}, f32[4,128,256]{2,1,0:T(8,128)S(1)}, u32[]{:S(2)}, u32[]{:S(2)}) collective-permute-start(f32[4,128,256]{2,1,0:T(8,128)} %get-tuple-element.23), channel_id=1, source_target_pairs={{0,32},{32,0},{64,96},{96,64},{128,160},{160,128},{192,224},{224,1... | collective-permute-start | bytes 1572872 | tf_op jit(solution)/shard_map/ppermute | solution.py:58
  18.8 10.2 %collective-permute-start = (f32[3,128,256]{2,1,0:T(8,128)}, f32[3,128,256]{2,1,0:T(8,128)S(1)}, u32[]{:S(2)}, u32[]{:S(2)}) collective-permute-start(f32[3,128,256]{2,1,0:T(8,128)} %get-tuple-element.20), channel_id=1, source_target_pairs={{0,480},{32,64},{64,32},{96,128},{128,96},{160,192},{192,160},{224... | collective-permute-start | bytes 1179656 | tf_op jit(solution)/shard_map/ppermute | solution.py:58
  20.7 8.2 %collective-permute-start.2 = (f32[3,128,256]{2,1,0:T(8,128)}, f32[3,128,256]{2,1,0:T(8,128)}, u32[]{:S(2)}, u32[]{:S(2)}) collective-permute-start(f32[3,128,256]{2,1,0:T(8,128)} %get-tuple-element.22), channel_id=1, source_target_pairs={{0,32},{32,0},{64,96},{96,64},{128,160},{160,128},{192,224},{224,1... | collective-permute-start | bytes 1179656 | tf_op jit(solution)/shard_map/ppermute | solution.py:58
  33.4 9.8 %copy-start.2 = (s32[32]{0:T(128)S(1)}, s32[32]{0:T(128)}, u32[]{:S(2)}) copy-start(s32[32]{0:T(128)} %param.7) | copy-start | bytes 388
  33.4 35.0 %all-to-all-start = ((f32[32,32,256]{2,1,0:T(8,128)}), f32[32,32,256]{2,1,0:T(8,128)S(1)}, u32[]{:S(2)}, u32[]{:S(2)}) async-start(f32[32,32,256]{2,1,0:T(8,128)} %bitcast.4), calls=%async_computation | async-start | bytes 2097152 | tf_op jit(solution)/shard_map/all_to_all | solution.py:23
  127.7 17.8 %all-to-all-start.4 = ((f32[8,40,256]{2,1,0:T(8,128)}), f32[8,40,256]{2,1,0:T(8,128)S(1)}, u32[]{:S(2)}, u32[]{:S(2)}) async-start(f32[8,40,256]{2,1,0:T(8,128)} %bitcast.12), calls=%async_computation.4 | async-start | bytes 655360 | tf_op jit(solution)/shard_map/all_to_all | solution.py:23
  146.3 16.6 %all-to-all-start.5 = ((f32[8,40,256]{2,1,0:T(8,128)}), f32[8,40,256]{2,1,0:T(8,128)S(1)}, u32[]{:S(2)}, u32[]{:S(2)}) async-start(f32[8,40,256]{2,1,0:T(8,128)} %broadcast_in_dim.13), calls=%async_computation.5 | async-start | bytes 655360 | tf_op jit(solution)/shard_map/all_to_all | solution.py:30
  150.7 3.9 %collective-permute-start.4 = (f32[256,256]{1,0:T(8,128)}, f32[256,256]{1,0:T(8,128)S(1)}, u32[]{:S(2)}, u32[]{:S(2)}) collective-permute-start(f32[256,256]{1,0:T(8,128)} %fusion.17), channel_id=1, source_target_pairs={{0,32},{32,0},{1,33},{33,1},{2,34},{34,2},{3,35},{35,3},{4,36},{36... | collective-permute-start | bytes 786440 | tf_op jit(solution)/shard_map/ppermute | solution.py:113
  162.9 14.6 %all-to-all-start.6 = ((f32[8,32,256]{2,1,0:T(8,128)}), f32[8,32,256]{2,1,0:T(8,128)S(1)}, u32[]{:S(2)}, u32[]{:S(2)}) async-start(f32[8,32,256]{2,1,0:T(8,128)} %bitcast.45), calls=%async_computation.6 | async-start | bytes 524288 | tf_op jit(solution)/shard_map/all_to_all | solution.py:23
  178.3 18.1 %all-to-all-start.7 = ((f32[8,32,256]{2,1,0:T(8,128)}), f32[8,32,256]{2,1,0:T(8,128)}, u32[]{:S(2)}, u32[]{:S(2)}) async-start(f32[8,32,256]{2,1,0:T(8,128)} %broadcast_in_dim.14), calls=%async_computation.7 | async-start | bytes 524288 | tf_op jit(solution)/shard_map/all_to_all | solution.py:30

commit v7 on v4

--- a/solution.py
+++ b/solution.py
@@ -28,13 +28,19 @@
     return lax.all_to_all(copies.reshape((-1,) + value.shape[1:]), axis, 0, 0, tiled=True)
 
 
-def edges_kernel(previous_ref, current_ref, last_ref, leading_ref, sems):
+def edges_kernel(previous_ref, current_ref, far_old, far_new, near_ref, sems):
     rows, depth = current_ref.shape[0], STEPS
+    core = lax.axis_index("core")
+
+    def edge(ref, count, side):
+        return ref.at[pl.ds(side * (rows - count), count)]
+
+    near_old, near_new = near_ref.at[pl.ds(0, depth - 1)], near_ref.at[pl.ds(depth - 1, depth)]
     copies = [
-        pltpu.make_async_copy(previous_ref.at[pl.ds(rows - depth + 1, depth - 1)], last_ref.at[pl.ds(0, depth - 1)], sems.at[0]),
-        pltpu.make_async_copy(current_ref.at[pl.ds(rows - depth, depth)], last_ref.at[pl.ds(depth - 1, depth)], sems.at[1]),
-        pltpu.make_async_copy(previous_ref.at[pl.ds(0, depth - 1)], leading_ref.at[pl.ds(0, depth - 1)], sems.at[2]),
-        pltpu.make_async_copy(current_ref.at[pl.ds(0, depth)], leading_ref.at[pl.ds(depth - 1, depth)], sems.at[3]),
+        pltpu.make_async_copy(edge(current_ref, depth, core), far_new, sems.at[0]),
+        pltpu.make_async_copy(edge(previous_ref, depth - 1, core), far_old, sems.at[1]),
+        pltpu.make_async_copy(edge(current_ref, depth, 1 - core), near_new, sems.at[2]),
+        pltpu.make_async_copy(edge(previous_ref, depth - 1, 1 - core), near_old, sems.at[3]),
     ]
     for copy in copies:
         copy.start()
@@ -44,37 +50,56 @@
 
 def halos(previous, current):
     size = lax.axis_size(SITE)
-    up = [(i, (i + 1) % size) for i in range(size)]
-    down = [(j, i) for i, j in up]
-    edge = jax.ShapeDtypeStruct((2 * STEPS - 1,) + current.shape[1:], jnp.float32)
-    last, leading = pl.pallas_call(
+    counts = (STEPS - 1, STEPS, 2 * STEPS - 1)
+    far_old, far_new, near = pl.pallas_call(
         edges_kernel,
-        out_shape=[edge, edge],
+        out_shape=[jax.ShapeDtypeStruct((n,) + current.shape[1:], jnp.float32) for n in counts],
         in_specs=[pl.BlockSpec(memory_space=pl.ANY)] * 2,
-        out_specs=[pl.BlockSpec(memory_space=pl.ANY)] * 2,
+        out_specs=[pl.BlockSpec(memory_space=pltpu.VMEM)] * 3,
         scratch_shapes=[pltpu.SemaphoreType.DMA((4,))],
     )(previous, current)
-    return lax.ppermute(last, SITE, up), lax.ppermute(leading, SITE, down)
-
-
-def window_kernel(previous_ref, current_ref, before_ref, after_ref, weight_ref, out_ref, even, odd):
-    rows = current_ref.shape[0]
+    swap = [(i, (i + 1 if i % 2 else i - 1) % size) for i in range(size)]
+    return [lax.ppermute(near, "core", [(0, 1), (1, 0)]), lax.ppermute(far_old, SITE, swap), lax.ppermute(far_new, SITE, swap)]
+
+
+def window_kernel(near_ref, far_old, far_new, occupancy_ref, previous_ref, current_ref, out_ref, even, odd):
+    rows, side = current_ref.shape[0], current_ref.shape[1]
     depth = STEPS
-    even[pl.ds(0, depth)] = before_ref[pl.ds(depth - 1, depth)]
-    even[pl.ds(depth, rows)] = current_ref[...]
-    even[pl.ds(depth + rows, depth)] = after_ref[pl.ds(depth - 1, depth)]
-    odd[pl.ds(1, depth - 1)] = before_ref[pl.ds(0, depth - 1)]
-    odd[pl.ds(depth, rows)] = previous_ref[...]
-    odd[pl.ds(depth + rows, depth - 1)] = after_ref[pl.ds(0, depth - 1)]
+    core, size = lax.axis_index("core"), lax.axis_size("z") * lax.axis_size("core")
+    site = lax.axis_index("z") * lax.axis_size("core") + core
+    near_old, near_new = near_ref.at[pl.ds(0, depth - 1)], near_ref.at[pl.ds(depth - 1, depth)]
+
+    def place(before_old, before_new, after_old, after_new):
+        even[pl.ds(0, depth)] = before_new[...]
+        even[pl.ds(depth + rows, depth)] = after_new[...]
+        odd[pl.ds(1, depth - 1)] = before_old[...]
+        odd[pl.ds(depth + rows, depth - 1)] = after_old[...]
+
+    pl.when(core == 0)(lambda: place(far_old, far_new, near_old, near_new))
+    pl.when(core == 1)(lambda: place(near_old, near_new, far_old, far_new))
+
+    slabs = [lax.rem(site + size - 1, size), site, lax.rem(site + 1, size)]
+    unread = jnp.zeros((side - len(slabs) * rows, side), jnp.float32)
+
     for turn in range(STEPS):
+        masks = [occupancy_ref[turn, pl.ds(pl.multiple_of(slab * rows, rows), rows), :].astype(jnp.float32) for slab in slabs]
+        weights = jnp.concatenate(masks + [unread], axis=0).T
         current, previous = (even, odd) if turn % 2 == 0 else (odd, even)
-        last = turn == STEPS - 1
+
+        def load(now, row):
+            own = depth <= row < depth + rows
+            if own and turn == 0:
+                return current_ref[row - depth] if now else previous_ref[row - depth]
+            if own and turn == 1 and not now:
+                return current_ref[row - depth]
+            return (current if now else previous)[row]
 
         for row in range(turn + 1, rows + 2 * depth - 1 - turn):
-            here = current[row]
-            neighbours = current[row + 1] + current[row - 1] + pltpu.roll(here, 1, 0) + pltpu.roll(here, here.shape[0] - 1, 0)
-            value = weight_ref[turn, :, row : row + 1] * (ENERGY * here - neighbours - previous[row])
-            if last:
+            here = load(True, row)
+            neighbours = load(True, row + 1) + load(True, row - 1) + pltpu.roll(here, 1, 0) + pltpu.roll(here, side - 1, 0)
+            column = row + rows - depth
+            value = weights[:, column : column + 1] * (ENERGY * here - neighbours - load(False, row))
+            if turn == STEPS - 1:
                 out_ref[row - depth] = value
             else:
                 previous[row] = value
@@ -82,20 +107,16 @@
 
 def window(previous, current, occupancy):
     rows, side, width = current.shape
-    before, after = halos(previous, current)
-    start = lax.axis_index(SITE) * rows
-    around = jnp.concatenate([occupancy[:, side - STEPS :], occupancy, occupancy[:, :STEPS]], axis=1)
-    weights = lax.dynamic_slice_in_dim(around, start, rows + 2 * STEPS, 1).astype(jnp.float32).transpose(0, 2, 1)
     slab = pltpu.VMEM((rows + 2 * STEPS, side, width), jnp.float32)
     return pl.pallas_call(
         window_kernel,
         out_shape=jax.ShapeDtypeStruct(current.shape, jnp.float32),
-        in_specs=[pl.BlockSpec(memory_space=pltpu.VMEM)] * 5,
+        in_specs=[pl.BlockSpec(memory_space=pltpu.VMEM)] * 6,
         out_specs=pl.BlockSpec(memory_space=pltpu.VMEM),
         scratch_shapes=[slab, slab],
         compiler_params=pltpu.CompilerParams(vmem_limit_bytes=32 * 1024 * 1024),
         cost_estimate=pl.CostEstimate(flops=12_000_000, bytes_accessed=6_000_000, transcendentals=0),
-    )(previous, current, before, after, weights)
+    )(*halos(previous, current), occupancy, previous, current)
 
 
 def core_sum(value):

time: 260 us -> 210 us (0.81)
  Pallas kernels: 82 us -> 27.2 us
  starting transfers between devices: 49.6 us -> 56.4 us
  waiting for transfers between devices: 38.6 us -> 41.5 us
    pallas_call x1, Pallas kernels: 56.7 us -> 2.84 us  [halos(): pl.pallas_call(edges_kernel, out_shape=[jax.ShapeDtypeStruct((n,) + curre...]
    ppermute x2 -> x3, starting transfers between devices: 6.92 us -> 14.3 us  [the longest x1 8.79 us: halos(): lax.ppermute(near, 'core', [(0, 1), (1, 0)])]
    all_to_all x2, blocking collectives: 42.4 us -> 38 us  [gather(): lax.all_to_all(copies.reshape((-1,) + value.shape[1:]), axis, 0, 0, tiled...]
    ppermute x2 -> x3, waiting for transfers between devices: 5.81 us -> 9.65 us  [the longest x1 9.64 us: halos(): lax.ppermute(far_old, SITE, swap)]
    all_to_all x1, blocking collectives: 11.5 us -> 14.2 us  [exchange(): out = lax.all_to_all(value, axis, 0, 0, tiled=True)]
  transfers between devices with their start and end apart: 8 -> 9, of which waited for: 7 -> 6; matrix products, arithmetic and copies ran while one was open for 5% -> 4% of each run, Pallas kernels for 7% -> 9%
where the time goes in v7:
time: 210 us; the launch traced here: 209 us
  blocking collectives  58.4 us (28%)
  starting transfers between devices  56.4 us (27%)
  waiting for transfers between devices  41.5 us (20%)
  Pallas kernels  27.2 us (13%)
  matrix products  13.2 us (6%)
  between operations  6 us (3%)
  local copies, waits for them, and re-layouts  3.36 us (2%)
  other arithmetic  2.95 us (1%)
    all_to_all x2, blocking collectives, gather(): lax.all_to_all(copies.reshape((-1,) + value.shape[1:]), axis, 0, 0, tiled...  38 us
    all_to_all x3, starting transfers between devices, exchange(): out = lax.all_to_all(value, axis, 0, 0, tiled=True)  29.9 us
    all_to_all x3, waiting for transfers between devices, exchange(): out = lax.all_to_all(value, axis, 0, 0, tiled=True)  22.4 us
    pallas_call x3, Pallas kernels, on_chip(): pl.pallas_call(kernel, out_shape=[jax.ShapeDtypeStruct(shape, jnp.float32...  20.8 us
    all_to_all x1, blocking collectives, exchange(): out = lax.all_to_all(value, axis, 0, 0, tiled=True)  14.2 us
    ppermute x1, waiting for transfers between devices, halos(): lax.ppermute(far_old, SITE, swap)  9.64 us
    all_to_all x2, starting transfers between devices, gather(): lax.all_to_all(copies.reshape((-1,) + value.shape[1:]), axis, 0, 0, tiled...  9.59 us
    ppermute x1, starting transfers between devices, halos(): lax.ppermute(near, 'core', [(0, 1), (1, 0)])  8.79 us
  transfers between devices with their start and end apart: 9, of which 6 were waited for; matrix products, arithmetic and copies ran while one was open for 4% of the time, Pallas kernels for 9%

profile of v7, /device:TPU:1, one launch (start us, length us, event | category | flops | bytes accessed | tf_op | source)
XLA Modules:
  0.0 209.0 jit_solution(10637784529983074769)
XLA Ops:
  0.6 2.8 %shard_map.59 = (f32[3,128,256]{2,1,0:T(8,128)}, f32[4,128,256]{2,1,0:T(8,128)}, f32[7,128,256]{2,1,0:T(8,128)}) custom-call(f32[8,128,256]{2,1,0:T(8,128)} %previous_ref.3, f32[8,128,256]{2,1,0:T(8,128)} %current_ref.3), custom_call_target="tpu_custom_call" | custom-call | tf_op jit(solution)/shard_map/pallas_call | solution.py:54
  3.5 8.8 %collective-permute-start = (f32[7,128,256]{2,1,0:T(8,128)}, f32[7,128,256]{2,1,0:T(8,128)S(1)}, u32[]{:S(2)}, u32[]{:S(2)}) collective-permute-start(f32[7,128,256]{2,1,0:T(8,128)} %get-tuple-element.19), channel_id=1, source_target_pairs={{0,32},{32,0},{1,33},{33,1},{2,34},{34,2},{3,35},{35,3},{4,36},{36... | collective-permute-start | bytes 2752520 | tf_op jit(solution)/shard_map/ppermute | solution.py:62
  12.3 1.9 collective-permute-start.2
  14.2 3.6 %collective-permute-start.1 = (f32[3,128,256]{2,1,0:T(8,128)}, f32[3,128,256]{2,1,0:T(8,128)S(1)}, u32[]{:S(2)}, u32[]{:S(2)}) collective-permute-start(f32[3,128,256]{2,1,0:T(8,128)} %get-tuple-element.20), channel_id=1, source_target_pairs={{0,480},{32,64},{64,32},{96,128},{128,96},{160,192},{192,160},{224... | collective-permute-start | bytes 1179656 | tf_op jit(solution)/shard_map/ppermute | solution.py:62
  17.9 9.6 %collective-permute-done.1.far_old = f32[3,128,256]{2,1,0:T(8,128)S(1)} collective-permute-done((f32[3,128,256]{2,1,0:T(8,128)}, f32[3,128,256]{2,1,0:T(8,128)S(1)}, u32[]{:S(2)}, u32[]{:S(2)}) %collective-permute-start.1) | collective-permute-done | bytes 393248 | tf_op jit(solution)/shard_map/ppermute | solution.py:62
  27.5 0.9 copy-done.2
  28.5 3.5 %shard_map.60 = f32[8,128,256]{2,1,0:T(8,128)} custom-call(f32[7,128,256]{2,1,0:T(8,128)S(1)} %collective-permute-done.near_ref, f32[3,128,256]{2,1,0:T(8,128)S(1)} %collective-permute-done.1.far_old, f32[4,128,256]{2,1,0:T(8,128)S(1)} %collective-permute-done.2.far_new, s32[4,128,128]{2,1,0:T(8,128)S(1)} %copy-done.2, f32[8,128,256]{2,1,0:T(8,128)S(1)} %copy-done, ...), custom_call_target="tpu_custom_call" | custom-call | flops 12000000 | bytes 6000000 | tf_op jit(solution)/shard_map/pallas_call | solution.py:111
  32.0 4.7 %all-to-all-start = ((f32[32,32,256]{2,1,0:T(8,128)}), f32[32,32,256]{2,1,0:T(8,128)S(1)}, u32[]{:S(2)}, u32[]{:S(2)}) async-start(f32[32,32,256]{2,1,0:T(8,128)} %bitcast.3), calls=%async_computation | async-start | bytes 2097152 | tf_op jit(solution)/shard_map/all_to_all | solution.py:21
  41.2 14.3 %all-to-all-done = f32[32,32,256]{2,1,0:T(8,128)S(1)} async-done(((f32[32,32,256]{2,1,0:T(8,128)}), f32[32,32,256]{2,1,0:T(8,128)S(1)}, u32[]{:S(2)}, u32[]{:S(2)}) %all-to-all-start) | async-done | bytes 1048608 | tf_op jit(solution)/shard_map/all_to_all | solution.py:21
  55.5 17.4 %all_to_all.66 = f32[8,64,256]{2,1,0:T(8,128)S(1)} all-to-all(f32[8,64,256]{2,1,0:T(8,128)S(1)} %broadcast_in_dim.10), channel_id=1, replica_groups=mesh['z'=8,'core'=2,'x'=4,'y'=8] {'y'}, dimensions={0} | all-to-all | bytes 1048576 | tf_op jit(solution)/shard_map/all_to_all | solution.py:28
  73.1 20.6 %all_to_all.67 = f32[4,512,256]{2,1,0:T(8,128)S(1)} all-to-all(f32[4,512,256]{2,1,0:T(8,128)S(1)} %broadcast_in_dim.12), channel_id=1, replica_groups=mesh['z'=8,'core'=2,'x'=4,'y'=8] {'x'}, dimensions={0} | all-to-all | bytes 4194304 | tf_op jit(solution)/shard_map/all_to_all | solution.py:28
  93.8 3.0 %shard_map.61 = f32[640,256]{1,0:T(8,128)S(1)} custom-call(f32[32,2,32,256]{3,2,1,0:T(8,128)S(1)} %bitcast.34), custom_call_target="tpu_custom_call" | custom-call | flops 4000000000 | bytes 524288 | tf_op jit(solution)/shard_map/pallas_call | solution.py:282
  96.8 14.2 %all_to_all.68 = f32[2,320,256]{2,1,0:T(8,128)S(1)} all-to-all(f32[2,320,256]{2,1,0:T(8,128)S(1)} %bitcast.35), channel_id=1, replica_groups=mesh['z'=8,'core'=2,'x'=4,'y'=8] {'core'}, dimensions={0} | all-to-all | bytes 1310720 | tf_op jit(solution)/shard_map/all_to_all | solution.py:21
  111.0 0.8 reduce_sum.27
  111.8 21.9 %all-to-all-start.4 = ((f32[8,40,256]{2,1,0:T(8,128)}), f32[8,40,256]{2,1,0:T(8,128)S(1)}, u32[]{:S(2)}, u32[]{:S(2)}) async-start(f32[8,40,256]{2,1,0:T(8,128)} %bitcast.11), calls=%async_computation.4 | async-start | bytes 655360 | tf_op jit(solution)/shard_map/all_to_all | solution.py:21
  133.6 3.1 %fusion.22 = f32[256,256]{1,0:T(8,128)S(1)} fusion(f32[1024,256]{1,0:T(8,128)S(1)} %bitcast.38, f32[1024,256]{1,0:T(8,128)} %bitcast), kind=kOutput, calls=%fused_computation.32 | convolution fusion | flops 805306368 | bytes 2359296 | tf_op jit(solution)/shard_map/dot_general | solution.py:135
  136.7 3.1 %fusion.21 = f32[256,256]{1,0:T(8,128)S(1)} fusion(f32[1024,256]{1,0:T(8,128)S(1)} %bitcast.36, f32[1024,256]{1,0:T(8,128)} %bitcast), kind=kOutput, calls=%fused_computation.31 | convolution fusion | flops 805306368 | bytes 2359296 | tf_op jit(solution)/shard_map/dot_general | solution.py:135
  139.9 7.4 %all-to-all-done.4 = f32[8,40,256]{2,1,0:T(8,128)S(1)} async-done(((f32[8,40,256]{2,1,0:T(8,128)}), f32[8,40,256]{2,1,0:T(8,128)S(1)}, u32[]{:S(2)}, u32[]{:S(2)}) %all-to-all-start.4) | async-done | bytes 327712 | tf_op jit(solution)/shard_map/all_to_all | solution.py:21
  147.3 0.7 broadcast_in_dim.13
  148.0 3.4 %all-to-all-start.5 = ((f32[8,40,256]{2,1,0:T(8,128)}), f32[8,40,256]{2,1,0:T(8,128)S(1)}, u32[]{:S(2)}, u32[]{:S(2)}) async-start(f32[8,40,256]{2,1,0:T(8,128)} %broadcast_in_dim.13), calls=%async_computation.5 | async-start | bytes 655360 | tf_op jit(solution)/shard_map/all_to_all | solution.py:28
  151.5 0.8 fusion.13
  152.2 2.5 %collective-permute-start.3 = (f32[256,256]{1,0:T(8,128)}, f32[256,256]{1,0:T(8,128)S(1)}, u32[]{:S(2)}, u32[]{:S(2)}) collective-permute-start(f32[256,256]{1,0:T(8,128)} %fusion.13), channel_id=1, source_target_pairs={{0,32},{32,0},{1,33},{33,1},{2,34},{34,2},{3,35},{35,3},{4,36},{36... | collective-permute-start | bytes 786440 | tf_op jit(solution)/shard_map/ppermute | solution.py:126
  154.8 1.3 collective-permute-done.3
  156.1 0.8 fusion.15
  156.9 8.2 %all-to-all-done.5 = f32[8,40,256]{2,1,0:T(8,128)S(1)} async-done(((f32[8,40,256]{2,1,0:T(8,128)}), f32[8,40,256]{2,1,0:T(8,128)S(1)}, u32[]{:S(2)}, u32[]{:S(2)}) %all-to-all-start.5) | async-done | bytes 327712 | tf_op jit(solution)/shard_map/all_to_all | solution.py:28
  165.1 3.4 %all-to-all-start.6 = ((f32[8,32,256]{2,1,0:T(8,128)}), f32[8,32,256]{2,1,0:T(8,128)S(1)}, u32[]{:S(2)}, u32[]{:S(2)}) async-start(f32[8,32,256]{2,1,0:T(8,128)} %bitcast.43), calls=%async_computation.6 | async-start | bytes 524288 | tf_op jit(solution)/shard_map/all_to_all | solution.py:21
  168.5 2.6 %all_gather.6.gram_ref = f32[640,256]{1,0:T(8,128)S(1)} all-gather(f32[320,256]{1,0:T(8,128)S(1)} %bitcast.41), channel_id=1, replica_groups=mesh['z'=8,'core'=2,'x'=4,'y'=8] {'core'}, dimensions={0}, use_global_device_ids=true | all-gather | bytes 983040 | tf_op jit(solution)/shard_map/all_gather | solution.py:305
  171.1 8.3 %shard_map.62 = (f32[256,256]{1,0:T(8,128)S(1)}, f32[1,256]{1,0:T(1,128)S(1)}) custom-call(f32[640,256]{1,0:T(8,128)S(1)} %all_gather.6.gram_ref), custom_call_target="tpu_custom_call" | custom-call | flops 1000 | bytes 524288 | tf_op jit(solution)/shard_map/pallas_call | solution.py:282
  180.9 6.2 %all-to-all-start.7 = ((f32[8,32,256]{2,1,0:T(8,128)}), f32[8,32,256]{2,1,0:T(8,128)}, u32[]{:S(2)}, u32[]{:S(2)}) async-start(f32[8,32,256]{2,1,0:T(8,128)} %broadcast_in_dim.14), calls=%async_computation.7 | async-start | bytes 524288 | tf_op jit(solution)/shard_map/all_to_all | solution.py:28
  188.3 9.4 %shard_map.63 = (f32[256,256]{1,0:T(8,128)S(1)}, f32[1,256]{1,0:T(1,128)S(1)}, f32[256,256]{1,0:T(8,128)S(1)}) custom-call(f32[640,256]{1,0:T(8,128)S(1)} %all_gather.6.gram_ref, f32[256,256]{1,0:T(8,128)S(1)} %get-tuple-element.28.inverse_ref), custom_call_target="tpu_custom_call" | custom-call | flops 1000 | bytes 524288 | tf_op jit(solution)/shard_map/pallas_call | solution.py:282
  198.4 3.6 %all_gather.7 = f32[512,256]{1,0:T(8,128)S(1)} all-gather(f32[256,256]{1,0:T(8,128)} %bitcast.14), channel_id=1, replica_groups=mesh['z'=8,'core'=2,'x'=4,'y'=8] {'core'}, dimensions={0}, use_global_device_ids=true | all-gather | bytes 786432 | tf_op jit(solution)/shard_map/all_gather | solution.py:312
  205.0 4.0 %multiply_subtract_fusion = f32[1024,256]{1,0:T(8,128)} fusion(f32[1024,256]{1,0:T(8,128)} %bitcast, f32[1024,256]{1,0:T(8,128)S(1)} %bitcast.39, f32[1024,256]{1,0:T(8,128)S(1)} %bitcast.37, f32[256,256]{1,0:T(8,128)S(1)} %fusion.23, f32[256,256]{1,0:T(8,128)S(1)} %fusion.24, f32[]{:T(128)S(6)} %select_n.39), kind=kOutput, calls=%fused_computation.9 | convolution fusion | flops 1611792384 | bytes 4718596 | tf_op jit(solution)/shard_map/dot_general | solution.py:130
  (27 shorter events, 6.0 us)
Async XLA Ops:
  0.6 26.9 %copy-start = (f32[8,128,256]{2,1,0:T(8,128)S(1)}, f32[8,128,256]{2,1,0:T(8,128)}, u32[]{:S(2)}) copy-start(f32[8,128,256]{2,1,0:T(8,128)} %previous_ref.3) | copy-start | bytes 3145732
  0.6 26.9 %copy-start.1 = (f32[8,128,256]{2,1,0:T(8,128)S(1)}, f32[8,128,256]{2,1,0:T(8,128)}, u32[]{:S(2)}) copy-start(f32[8,128,256]{2,1,0:T(8,128)} %current_ref.3) | copy-start | bytes 3145732
  3.5 24.0 %collective-permute-start = (f32[7,128,256]{2,1,0:T(8,128)}, f32[7,128,256]{2,1,0:T(8,128)S(1)}, u32[]{:S(2)}, u32[]{:S(2)}) collective-permute-start(f32[7,128,256]{2,1,0:T(8,128)} %get-tuple-element.19), channel_id=1, source_target_pairs={{0,32},{32,0},{1,33},{33,1},{2,34},{34,2},{3,35},{35,3},{4,36},{36... | collective-permute-start | bytes 2752520 | tf_op jit(solution)/shard_map/ppermute | solution.py:62
  12.3 15.2 %collective-permute-start.2 = (f32[4,128,256]{2,1,0:T(8,128)}, f32[4,128,256]{2,1,0:T(8,128)S(1)}, u32[]{:S(2)}, u32[]{:S(2)}) collective-permute-start(f32[4,128,256]{2,1,0:T(8,128)} %get-tuple-element.21), channel_id=1, source_target_pairs={{0,480},{32,64},{64,32},{96,128},{128,96},{160,192},{192,160},{224... | collective-permute-start | bytes 1572872 | tf_op jit(solution)/shard_map/ppermute | solution.py:62
  14.2 13.3 %collective-permute-start.1 = (f32[3,128,256]{2,1,0:T(8,128)}, f32[3,128,256]{2,1,0:T(8,128)S(1)}, u32[]{:S(2)}, u32[]{:S(2)}) collective-permute-start(f32[3,128,256]{2,1,0:T(8,128)} %get-tuple-element.20), channel_id=1, source_target_pairs={{0,480},{32,64},{64,32},{96,128},{128,96},{160,192},{192,160},{224... | collective-permute-start | bytes 1179656 | tf_op jit(solution)/shard_map/ppermute | solution.py:62
  27.5 1.0 copy-start.2
  32.0 4.7 %copy-start.3 = (s32[32]{0:T(128)S(1)}, s32[32]{0:T(128)}, u32[]{:S(2)}) copy-start(s32[32]{0:T(128)} %param.7) | copy-start | bytes 388
  32.0 23.4 %all-to-all-start = ((f32[32,32,256]{2,1,0:T(8,128)}), f32[32,32,256]{2,1,0:T(8,128)S(1)}, u32[]{:S(2)}, u32[]{:S(2)}) async-start(f32[32,32,256]{2,1,0:T(8,128)} %bitcast.3), calls=%async_computation | async-start | bytes 2097152 | tf_op jit(solution)/shard_map/all_to_all | solution.py:21
  111.8 35.5 %all-to-all-start.4 = ((f32[8,40,256]{2,1,0:T(8,128)}), f32[8,40,256]{2,1,0:T(8,128)S(1)}, u32[]{:S(2)}, u32[]{:S(2)}) async-start(f32[8,40,256]{2,1,0:T(8,128)} %bitcast.11), calls=%async_computation.4 | async-start | bytes 655360 | tf_op jit(solution)/shard_map/all_to_all | solution.py:21
  148.0 17.0 %all-to-all-start.5 = ((f32[8,40,256]{2,1,0:T(8,128)}), f32[8,40,256]{2,1,0:T(8,128)S(1)}, u32[]{:S(2)}, u32[]{:S(2)}) async-start(f32[8,40,256]{2,1,0:T(8,128)} %broadcast_in_dim.13), calls=%async_computation.5 | async-start | bytes 655360 | tf_op jit(solution)/shard_map/all_to_all | solution.py:28
  152.2 3.9 %collective-permute-start.3 = (f32[256,256]{1,0:T(8,128)}, f32[256,256]{1,0:T(8,128)S(1)}, u32[]{:S(2)}, u32[]{:S(2)}) collective-permute-start(f32[256,256]{1,0:T(8,128)} %fusion.13), channel_id=1, source_target_pairs={{0,32},{32,0},{1,33},{33,1},{2,34},{34,2},{3,35},{35,3},{4,36},{36... | collective-permute-start | bytes 786440 | tf_op jit(solution)/shard_map/ppermute | solution.py:126
  165.1 15.1 %all-to-all-start.6 = ((f32[8,32,256]{2,1,0:T(8,128)}), f32[8,32,256]{2,1,0:T(8,128)S(1)}, u32[]{:S(2)}, u32[]{:S(2)}) async-start(f32[8,32,256]{2,1,0:T(8,128)} %bitcast.43), calls=%async_computation.6 | async-start | bytes 524288 | tf_op jit(solution)/shard_map/all_to_all | solution.py:21
  180.9 17.5 %all-to-all-start.7 = ((f32[8,32,256]{2,1,0:T(8,128)}), f32[8,32,256]{2,1,0:T(8,128)}, u32[]{:S(2)}, u32[]{:S(2)}) async-start(f32[8,32,256]{2,1,0:T(8,128)} %broadcast_in_dim.14), calls=%async_computation.7 | async-start | bytes 524288 | tf_op jit(solution)/shard_map/all_to_all | solution.py:28

commit v8 on v7

--- a/solution.py
+++ b/solution.py
@@ -1,3 +1,5 @@
+import functools
+
 import jax
 import jax.numpy as jnp
 from jax import lax
@@ -28,19 +30,15 @@
     return lax.all_to_all(copies.reshape((-1,) + value.shape[1:]), axis, 0, 0, tiled=True)
 
 
-def edges_kernel(previous_ref, current_ref, far_old, far_new, near_ref, sems):
+def edge_kernel(far, previous_ref, current_ref, out_ref, sems):
     rows, depth = current_ref.shape[0], STEPS
     core = lax.axis_index("core")
-
-    def edge(ref, count, side):
-        return ref.at[pl.ds(side * (rows - count), count)]
-
-    near_old, near_new = near_ref.at[pl.ds(0, depth - 1)], near_ref.at[pl.ds(depth - 1, depth)]
+    side = core if far else 1 - core
+    old = previous_ref.at[pl.ds(side * (rows - depth + 1), depth - 1)]
+    new = current_ref.at[pl.ds(side * (rows - depth), depth)]
     copies = [
-        pltpu.make_async_copy(edge(current_ref, depth, core), far_new, sems.at[0]),
-        pltpu.make_async_copy(edge(previous_ref, depth - 1, core), far_old, sems.at[1]),
-        pltpu.make_async_copy(edge(current_ref, depth, 1 - core), near_new, sems.at[2]),
-        pltpu.make_async_copy(edge(previous_ref, depth - 1, 1 - core), near_old, sems.at[3]),
+        pltpu.make_async_copy(old, out_ref.at[pl.ds(0, depth - 1)], sems.at[0]),
+        pltpu.make_async_copy(new, out_ref.at[pl.ds(depth - 1, depth)], sems.at[1]),
     ]
     for copy in copies:
         copy.start()
@@ -50,39 +48,43 @@
 
 def halos(previous, current):
     size = lax.axis_size(SITE)
-    counts = (STEPS - 1, STEPS, 2 * STEPS - 1)
-    far_old, far_new, near = pl.pallas_call(
-        edges_kernel,
-        out_shape=[jax.ShapeDtypeStruct((n,) + current.shape[1:], jnp.float32) for n in counts],
-        in_specs=[pl.BlockSpec(memory_space=pl.ANY)] * 2,
-        out_specs=[pl.BlockSpec(memory_space=pltpu.VMEM)] * 3,
-        scratch_shapes=[pltpu.SemaphoreType.DMA((4,))],
-    )(previous, current)
-    swap = [(i, (i + 1 if i % 2 else i - 1) % size) for i in range(size)]
-    return [lax.ppermute(near, "core", [(0, 1), (1, 0)]), lax.ppermute(far_old, SITE, swap), lax.ppermute(far_new, SITE, swap)]
-
-
-def window_kernel(near_ref, far_old, far_new, occupancy_ref, previous_ref, current_ref, out_ref, even, odd):
+    out = []
+    for far in (True, False):
+        edge = pl.pallas_call(
+            functools.partial(edge_kernel, far),
+            out_shape=jax.ShapeDtypeStruct((2 * STEPS - 1,) + current.shape[1:], jnp.float32),
+            in_specs=[pl.BlockSpec(memory_space=pl.ANY)] * 2,
+            out_specs=pl.BlockSpec(memory_space=pltpu.VMEM),
+            scratch_shapes=[pltpu.SemaphoreType.DMA((2,))],
+        )(previous, current)
+        swap = [(i, (i + 1 if i % 2 == far else i - 1) % size) for i in range(size)]
+        out.append(lax.ppermute(edge, SITE, swap))
+    return out
+
+
+def window_kernel(previous_ref, current_ref, far_ref, near_ref, occupancy_ref, out_ref, even, odd, masks_ref, sem):
     rows, side = current_ref.shape[0], current_ref.shape[1]
     depth = STEPS
     core, size = lax.axis_index("core"), lax.axis_size("z") * lax.axis_size("core")
     site = lax.axis_index("z") * lax.axis_size("core") + core
-    near_old, near_new = near_ref.at[pl.ds(0, depth - 1)], near_ref.at[pl.ds(depth - 1, depth)]
-
-    def place(before_old, before_new, after_old, after_new):
-        even[pl.ds(0, depth)] = before_new[...]
-        even[pl.ds(depth + rows, depth)] = after_new[...]
-        odd[pl.ds(1, depth - 1)] = before_old[...]
-        odd[pl.ds(depth + rows, depth - 1)] = after_old[...]
-
-    pl.when(core == 0)(lambda: place(far_old, far_new, near_old, near_new))
-    pl.when(core == 1)(lambda: place(near_old, near_new, far_old, far_new))
+    fetch = pltpu.make_async_copy(occupancy_ref, masks_ref, sem)
+    fetch.start()
+
+    def place(before_ref, after_ref):
+        even[pl.ds(0, depth)] = before_ref[pl.ds(depth - 1, depth)]
+        even[pl.ds(depth + rows, depth)] = after_ref[pl.ds(depth - 1, depth)]
+        odd[pl.ds(1, depth - 1)] = before_ref[pl.ds(0, depth - 1)]
+        odd[pl.ds(depth + rows, depth - 1)] = after_ref[pl.ds(0, depth - 1)]
+
+    pl.when(core == 0)(lambda: place(far_ref, near_ref))
+    pl.when(core == 1)(lambda: place(near_ref, far_ref))
+    fetch.wait()
 
     slabs = [lax.rem(site + size - 1, size), site, lax.rem(site + 1, size)]
     unread = jnp.zeros((side - len(slabs) * rows, side), jnp.float32)
 
     for turn in range(STEPS):
-        masks = [occupancy_ref[turn, pl.ds(pl.multiple_of(slab * rows, rows), rows), :].astype(jnp.float32) for slab in slabs]
+        masks = [masks_ref[turn, pl.ds(pl.multiple_of(slab * rows, rows), rows), :].astype(jnp.float32) for slab in slabs]
         weights = jnp.concatenate(masks + [unread], axis=0).T
         current, previous = (even, odd) if turn % 2 == 0 else (odd, even)
 
@@ -111,12 +113,12 @@
     return pl.pallas_call(
         window_kernel,
         out_shape=jax.ShapeDtypeStruct(current.shape, jnp.float32),
-        in_specs=[pl.BlockSpec(memory_space=pltpu.VMEM)] * 6,
+        in_specs=[pl.BlockSpec(memory_space=pltpu.VMEM)] * 4 + [pl.BlockSpec(memory_space=pl.ANY)],
         out_specs=pl.BlockSpec(memory_space=pltpu.VMEM),
-        scratch_shapes=[slab, slab],
+        scratch_shapes=[slab, slab, pltpu.VMEM(occupancy.shape, jnp.int32), pltpu.SemaphoreType.DMA],
         compiler_params=pltpu.CompilerParams(vmem_limit_bytes=32 * 1024 * 1024),
         cost_estimate=pl.CostEstimate(flops=12_000_000, bytes_accessed=6_000_000, transcendentals=0),
-    )(*halos(previous, current), occupancy, previous, current)
+    )(previous, current, *halos(previous, current), occupancy)
 
 
 def core_sum(value):

time: 210 us -> 206 us (0.981)
  waiting for transfers between devices: 41.5 us -> 34.7 us
    ppermute x3 -> x2, waiting for transfers between devices: 9.65 us -> 2.29 us  [halos(): out.append(lax.ppermute(edge, SITE, swap))]
    all_to_all x2, blocking collectives: 38 us -> 41.4 us  [gather(): lax.all_to_all(copies.reshape((-1,) + value.shape[1:]), axis, 0, 0, tiled...]
    pallas_call x1 -> x2, Pallas kernels: 2.84 us -> 4.22 us  [halos(): pl.pallas_call(functools.partial(edge_kernel, far), out_shape=jax.ShapeDt...]
    ppermute x3 -> x2, starting transfers between devices: 14.3 us -> 13.9 us  [halos(): out.append(lax.ppermute(edge, SITE, swap))]
  transfers between devices with their start and end apart: 9 -> 8, of which waited for: 6 -> 7; matrix products, arithmetic and copies ran while one was open for 4% -> 4% of each run, Pallas kernels for 9% -> 10%
where the time goes in v8:
time: 206 us; the launch traced here: 205 us
  blocking collectives  59.8 us (29%)
  starting transfers between devices  57.4 us (28%)
  waiting for transfers between devices  34.7 us (17%)
  Pallas kernels  28.6 us (14%)
  matrix products  13.2 us (6%)
  between operations  6.01 us (3%)
  other arithmetic  2.94 us (1%)
  local copies, waits for them, and re-layouts  2.43 us (1%)
    all_to_all x2, blocking collectives, gather(): lax.all_to_all(copies.reshape((-1,) + value.shape[1:]), axis, 0, 0, tiled...  41.4 us
    all_to_all x3, starting transfers between devices, exchange(): out = lax.all_to_all(value, axis, 0, 0, tiled=True)  31.3 us
    all_to_all x3, waiting for transfers between devices, exchange(): out = lax.all_to_all(value, axis, 0, 0, tiled=True)  22.9 us
    pallas_call x3, Pallas kernels, on_chip(): pl.pallas_call(kernel, out_shape=[jax.ShapeDtypeStruct(shape, jnp.float32...  20.8 us
    ppermute x2, starting transfers between devices, halos(): out.append(lax.ppermute(edge, SITE, swap))  13.9 us
    all_to_all x1, blocking collectives, exchange(): out = lax.all_to_all(value, axis, 0, 0, tiled=True)  12.1 us
    all_to_all x2, starting transfers between devices, gather(): lax.all_to_all(copies.reshape((-1,) + value.shape[1:]), axis, 0, 0, tiled...  9.59 us
    all_to_all x2, waiting for transfers between devices, gather(): lax.all_to_all(copies.reshape((-1,) + value.shape[1:]), axis, 0, 0, tiled...  8.18 us
  transfers between devices with their start and end apart: 8, of which 7 were waited for; matrix products, arithmetic and copies ran while one was open for 4% of the time, Pallas kernels for 10%

profile of v8, /device:TPU:1, one launch (start us, length us, event | category | flops | bytes accessed | tf_op | source)
XLA Modules:
  0.0 205.0 jit_solution(12238978378808720718)
XLA Ops:
  0.6 2.1 %shard_map.59 = f32[7,128,256]{2,1,0:T(8,128)} custom-call(f32[8,128,256]{2,1,0:T(8,128)} %previous_ref.5, f32[8,128,256]{2,1,0:T(8,128)} %current_ref.5), custom_call_target="tpu_custom_call" | custom-call | tf_op jit(solution)/shard_map/pallas_call | solution.py:53
  2.8 5.5 %collective-permute-start = (f32[7,128,256]{2,1,0:T(8,128)}, f32[7,128,256]{2,1,0:T(8,128)S(1)}, u32[]{:S(2)}, u32[]{:S(2)}) collective-permute-start(f32[7,128,256]{2,1,0:T(8,128)} %shard_map.59), channel_id=1, source_target_pairs={{0,480},{32,64},{64,32},{96,128},{128,96},{160,192},{192,160},{224... | collective-permute-start | bytes 2752520 | tf_op jit(solution)/shard_map/ppermute | solution.py:61
  8.3 2.1 %shard_map.60 = f32[7,128,256]{2,1,0:T(8,128)} custom-call(f32[8,128,256]{2,1,0:T(8,128)} %previous_ref.5, f32[8,128,256]{2,1,0:T(8,128)} %current_ref.5), custom_call_target="tpu_custom_call" | custom-call | tf_op jit(solution)/shard_map/pallas_call | solution.py:53
  10.4 8.4 %collective-permute-start.1 = (f32[7,128,256]{2,1,0:T(8,128)}, f32[7,128,256]{2,1,0:T(8,128)S(1)}, u32[]{:S(2)}, u32[]{:S(2)}) collective-permute-start(f32[7,128,256]{2,1,0:T(8,128)} %shard_map.60), channel_id=1, source_target_pairs={{0,32},{32,0},{64,96},{96,64},{128,160},{160,128},{192,224},{224,1... | collective-permute-start | bytes 2752520 | tf_op jit(solution)/shard_map/ppermute | solution.py:61
  18.8 1.0 collective-permute-done.far_ref
  19.9 1.3 collective-permute-done.1.near_ref
  21.1 3.6 %shard_map.61 = f32[8,128,256]{2,1,0:T(8,128)} custom-call(f32[8,128,256]{2,1,0:T(8,128)S(1)} %copy-done, f32[8,128,256]{2,1,0:T(8,128)S(1)} %copy-done.1, f32[7,128,256]{2,1,0:T(8,128)S(1)} %collective-permute-done.far_ref, f32[7,128,256]{2,1,0:T(8,128)S(1)} %collective-permute-done.1.near_ref, s32[4,128,128]{2,1,0:T(8,128)S(1)} %copy-done.2), custom_call_target="tpu_custom_call" | custom-call | flops 12000000 | bytes 6000000 | tf_op jit(solution)/shard_map/pallas_call | solution.py:113
  24.8 9.7 %all-to-all-start = ((f32[32,32,256]{2,1,0:T(8,128)}), f32[32,32,256]{2,1,0:T(8,128)S(1)}, u32[]{:S(2)}, u32[]{:S(2)}) async-start(f32[32,32,256]{2,1,0:T(8,128)} %bitcast.3), calls=%async_computation | async-start | bytes 2097152 | tf_op jit(solution)/shard_map/all_to_all | solution.py:23
  38.9 14.8 %all-to-all-done = f32[32,32,256]{2,1,0:T(8,128)S(1)} async-done(((f32[32,32,256]{2,1,0:T(8,128)}), f32[32,32,256]{2,1,0:T(8,128)S(1)}, u32[]{:S(2)}, u32[]{:S(2)}) %all-to-all-start) | async-done | bytes 1048608 | tf_op jit(solution)/shard_map/all_to_all | solution.py:23
  53.8 19.5 %all_to_all.66 = f32[8,64,256]{2,1,0:T(8,128)S(1)} all-to-all(f32[8,64,256]{2,1,0:T(8,128)S(1)} %broadcast_in_dim.10), channel_id=1, replica_groups=mesh['z'=8,'core'=2,'x'=4,'y'=8] {'y'}, dimensions={0} | all-to-all | bytes 1048576 | tf_op jit(solution)/shard_map/all_to_all | solution.py:30
  73.4 22.0 %all_to_all.67 = f32[4,512,256]{2,1,0:T(8,128)S(1)} all-to-all(f32[4,512,256]{2,1,0:T(8,128)S(1)} %broadcast_in_dim.12), channel_id=1, replica_groups=mesh['z'=8,'core'=2,'x'=4,'y'=8] {'x'}, dimensions={0} | all-to-all | bytes 4194304 | tf_op jit(solution)/shard_map/all_to_all | solution.py:30
  95.5 3.0 %shard_map.62 = f32[640,256]{1,0:T(8,128)S(1)} custom-call(f32[32,2,32,256]{3,2,1,0:T(8,128)S(1)} %bitcast.34), custom_call_target="tpu_custom_call" | custom-call | flops 4000000000 | bytes 524288 | tf_op jit(solution)/shard_map/pallas_call | solution.py:284
  98.5 12.1 %all_to_all.68 = f32[2,320,256]{2,1,0:T(8,128)S(1)} all-to-all(f32[2,320,256]{2,1,0:T(8,128)S(1)} %bitcast.35), channel_id=1, replica_groups=mesh['z'=8,'core'=2,'x'=4,'y'=8] {'core'}, dimensions={0} | all-to-all | bytes 1310720 | tf_op jit(solution)/shard_map/all_to_all | solution.py:23
  110.7 0.8 reduce_sum.27
  111.4 18.2 %all-to-all-start.4 = ((f32[8,40,256]{2,1,0:T(8,128)}), f32[8,40,256]{2,1,0:T(8,128)S(1)}, u32[]{:S(2)}, u32[]{:S(2)}) async-start(f32[8,40,256]{2,1,0:T(8,128)} %bitcast.11), calls=%async_computation.4 | async-start | bytes 655360 | tf_op jit(solution)/shard_map/all_to_all | solution.py:23
  129.7 3.1 %fusion.22 = f32[256,256]{1,0:T(8,128)S(1)} fusion(f32[1024,256]{1,0:T(8,128)S(1)} %bitcast.38, f32[1024,256]{1,0:T(8,128)} %bitcast), kind=kOutput, calls=%fused_computation.32 | convolution fusion | flops 805306368 | bytes 2359296 | tf_op jit(solution)/shard_map/dot_general | solution.py:137
  132.8 3.1 %fusion.21 = f32[256,256]{1,0:T(8,128)S(1)} fusion(f32[1024,256]{1,0:T(8,128)S(1)} %bitcast.36, f32[1024,256]{1,0:T(8,128)} %bitcast), kind=kOutput, calls=%fused_computation.31 | convolution fusion | flops 805306368 | bytes 2359296 | tf_op jit(solution)/shard_map/dot_general | solution.py:137
  135.9 7.4 %all-to-all-done.4 = f32[8,40,256]{2,1,0:T(8,128)S(1)} async-done(((f32[8,40,256]{2,1,0:T(8,128)}), f32[8,40,256]{2,1,0:T(8,128)S(1)}, u32[]{:S(2)}, u32[]{:S(2)}) %all-to-all-start.4) | async-done | bytes 327712 | tf_op jit(solution)/shard_map/all_to_all | solution.py:23
  143.3 0.7 broadcast_in_dim.13
  144.0 3.4 %all-to-all-start.5 = ((f32[8,40,256]{2,1,0:T(8,128)}), f32[8,40,256]{2,1,0:T(8,128)S(1)}, u32[]{:S(2)}, u32[]{:S(2)}) async-start(f32[8,40,256]{2,1,0:T(8,128)} %broadcast_in_dim.13), calls=%async_computation.5 | async-start | bytes 655360 | tf_op jit(solution)/shard_map/all_to_all | solution.py:30
  147.5 0.8 fusion.13
  148.3 2.5 %collective-permute-start.2 = (f32[256,256]{1,0:T(8,128)}, f32[256,256]{1,0:T(8,128)S(1)}, u32[]{:S(2)}, u32[]{:S(2)}) collective-permute-start(f32[256,256]{1,0:T(8,128)} %fusion.13), channel_id=1, source_target_pairs={{0,32},{32,0},{1,33},{33,1},{2,34},{34,2},{3,35},{35,3},{4,36},{36... | collective-permute-start | bytes 786440 | tf_op jit(solution)/shard_map/ppermute | solution.py:128
  150.8 1.3 collective-permute-done.2
  152.1 0.8 fusion.15
  152.9 8.2 %all-to-all-done.5 = f32[8,40,256]{2,1,0:T(8,128)S(1)} async-done(((f32[8,40,256]{2,1,0:T(8,128)}), f32[8,40,256]{2,1,0:T(8,128)S(1)}, u32[]{:S(2)}, u32[]{:S(2)}) %all-to-all-start.5) | async-done | bytes 327712 | tf_op jit(solution)/shard_map/all_to_all | solution.py:30
  161.1 3.4 %all-to-all-start.6 = ((f32[8,32,256]{2,1,0:T(8,128)}), f32[8,32,256]{2,1,0:T(8,128)S(1)}, u32[]{:S(2)}, u32[]{:S(2)}) async-start(f32[8,32,256]{2,1,0:T(8,128)} %bitcast.43), calls=%async_computation.6 | async-start | bytes 524288 | tf_op jit(solution)/shard_map/all_to_all | solution.py:23
  164.5 2.6 %all_gather.6.gram_ref = f32[640,256]{1,0:T(8,128)S(1)} all-gather(f32[320,256]{1,0:T(8,128)S(1)} %bitcast.41), channel_id=1, replica_groups=mesh['z'=8,'core'=2,'x'=4,'y'=8] {'core'}, dimensions={0}, use_global_device_ids=true | all-gather | bytes 983040 | tf_op jit(solution)/shard_map/all_gather | solution.py:307
  167.1 8.3 %shard_map.63 = (f32[256,256]{1,0:T(8,128)S(1)}, f32[1,256]{1,0:T(1,128)S(1)}) custom-call(f32[640,256]{1,0:T(8,128)S(1)} %all_gather.6.gram_ref), custom_call_target="tpu_custom_call" | custom-call | flops 1000 | bytes 524288 | tf_op jit(solution)/shard_map/pallas_call | solution.py:284
  176.9 6.2 %all-to-all-start.7 = ((f32[8,32,256]{2,1,0:T(8,128)}), f32[8,32,256]{2,1,0:T(8,128)}, u32[]{:S(2)}, u32[]{:S(2)}) async-start(f32[8,32,256]{2,1,0:T(8,128)} %broadcast_in_dim.14), calls=%async_computation.7 | async-start | bytes 524288 | tf_op jit(solution)/shard_map/all_to_all | solution.py:30
  184.4 9.4 %shard_map.64 = (f32[256,256]{1,0:T(8,128)S(1)}, f32[1,256]{1,0:T(1,128)S(1)}, f32[256,256]{1,0:T(8,128)S(1)}) custom-call(f32[640,256]{1,0:T(8,128)S(1)} %all_gather.6.gram_ref, f32[256,256]{1,0:T(8,128)S(1)} %get-tuple-element.22.inverse_ref), custom_call_target="tpu_custom_call" | custom-call | flops 1000 | bytes 524288 | tf_op jit(solution)/shard_map/pallas_call | solution.py:284
  194.4 3.6 %all_gather.7 = f32[512,256]{1,0:T(8,128)S(1)} all-gather(f32[256,256]{1,0:T(8,128)} %bitcast.14), channel_id=1, replica_groups=mesh['z'=8,'core'=2,'x'=4,'y'=8] {'core'}, dimensions={0}, use_global_device_ids=true | all-gather | bytes 786432 | tf_op jit(solution)/shard_map/all_gather | solution.py:314
  201.0 4.0 %multiply_subtract_fusion = f32[1024,256]{1,0:T(8,128)} fusion(f32[1024,256]{1,0:T(8,128)} %bitcast, f32[1024,256]{1,0:T(8,128)S(1)} %bitcast.39, f32[1024,256]{1,0:T(8,128)S(1)} %bitcast.37, f32[256,256]{1,0:T(8,128)S(1)} %fusion.23, f32[256,256]{1,0:T(8,128)S(1)} %fusion.24, f32[]{:T(128)S(6)} %select_n.39), kind=kOutput, calls=%fused_computation.9 | convolution fusion | flops 1611792384 | bytes 4718596 | tf_op jit(solution)/shard_map/dot_general | solution.py:132
  (26 shorter events, 6.0 us)
Async XLA Ops:
  2.7 18.4 %copy-start = (f32[8,128,256]{2,1,0:T(8,128)S(1)}, f32[8,128,256]{2,1,0:T(8,128)}, u32[]{:S(2)}) copy-start(f32[8,128,256]{2,1,0:T(8,128)} %previous_ref.5) | copy-start | bytes 3145732
  2.8 18.4 %copy-start.1 = (f32[8,128,256]{2,1,0:T(8,128)S(1)}, f32[8,128,256]{2,1,0:T(8,128)}, u32[]{:S(2)}) copy-start(f32[8,128,256]{2,1,0:T(8,128)} %current_ref.5) | copy-start | bytes 3145732
  2.8 18.4 %copy-start.2 = (s32[4,128,128]{2,1,0:T(8,128)S(1)}, s32[4,128,128]{2,1,0:T(8,128)}, u32[]{:S(2)}) copy-start(s32[4,128,128]{2,1,0:T(8,128)} %occupancy_ref.1) | copy-start | bytes 786436
  2.8 17.1 %collective-permute-start = (f32[7,128,256]{2,1,0:T(8,128)}, f32[7,128,256]{2,1,0:T(8,128)S(1)}, u32[]{:S(2)}, u32[]{:S(2)}) collective-permute-start(f32[7,128,256]{2,1,0:T(8,128)} %shard_map.59), channel_id=1, source_target_pairs={{0,480},{32,64},{64,32},{96,128},{128,96},{160,192},{192,160},{224... | collective-permute-start | bytes 2752520 | tf_op jit(solution)/shard_map/ppermute | solution.py:61
  10.4 10.7 %collective-permute-start.1 = (f32[7,128,256]{2,1,0:T(8,128)}, f32[7,128,256]{2,1,0:T(8,128)S(1)}, u32[]{:S(2)}, u32[]{:S(2)}) collective-permute-start(f32[7,128,256]{2,1,0:T(8,128)} %shard_map.60), channel_id=1, source_target_pairs={{0,32},{32,0},{64,96},{96,64},{128,160},{160,128},{192,224},{224,1... | collective-permute-start | bytes 2752520 | tf_op jit(solution)/shard_map/ppermute | solution.py:61
  24.7 9.7 %copy-start.3 = (s32[32]{0:T(128)S(1)}, s32[32]{0:T(128)}, u32[]{:S(2)}) copy-start(s32[32]{0:T(128)} %param.7) | copy-start | bytes 388
  24.8 28.9 %all-to-all-start = ((f32[32,32,256]{2,1,0:T(8,128)}), f32[32,32,256]{2,1,0:T(8,128)S(1)}, u32[]{:S(2)}, u32[]{:S(2)}) async-start(f32[32,32,256]{2,1,0:T(8,128)} %bitcast.3), calls=%async_computation | async-start | bytes 2097152 | tf_op jit(solution)/shard_map/all_to_all | solution.py:23
  111.4 31.9 %all-to-all-start.4 = ((f32[8,40,256]{2,1,0:T(8,128)}), f32[8,40,256]{2,1,0:T(8,128)S(1)}, u32[]{:S(2)}, u32[]{:S(2)}) async-start(f32[8,40,256]{2,1,0:T(8,128)} %bitcast.11), calls=%async_computation.4 | async-start | bytes 655360 | tf_op jit(solution)/shard_map/all_to_all | solution.py:23
  144.0 17.0 %all-to-all-start.5 = ((f32[8,40,256]{2,1,0:T(8,128)}), f32[8,40,256]{2,1,0:T(8,128)S(1)}, u32[]{:S(2)}, u32[]{:S(2)}) async-start(f32[8,40,256]{2,1,0:T(8,128)} %broadcast_in_dim.13), calls=%async_computation.5 | async-start | bytes 655360 | tf_op jit(solution)/shard_map/all_to_all | solution.py:30
  148.3 3.9 %collective-permute-start.2 = (f32[256,256]{1,0:T(8,128)}, f32[256,256]{1,0:T(8,128)S(1)}, u32[]{:S(2)}, u32[]{:S(2)}) collective-permute-start(f32[256,256]{1,0:T(8,128)} %fusion.13), channel_id=1, source_target_pairs={{0,32},{32,0},{1,33},{33,1},{2,34},{34,2},{3,35},{35,3},{4,36},{36... | collective-permute-start | bytes 786440 | tf_op jit(solution)/shard_map/ppermute | solution.py:128
  161.1 15.1 %all-to-all-start.6 = ((f32[8,32,256]{2,1,0:T(8,128)}), f32[8,32,256]{2,1,0:T(8,128)S(1)}, u32[]{:S(2)}, u32[]{:S(2)}) async-start(f32[8,32,256]{2,1,0:T(8,128)} %bitcast.43), calls=%async_computation.6 | async-start | bytes 524288 | tf_op jit(solution)/shard_map/all_to_all | solution.py:23
  176.9 17.5 %all-to-all-start.7 = ((f32[8,32,256]{2,1,0:T(8,128)}), f32[8,32,256]{2,1,0:T(8,128)}, u32[]{:S(2)}, u32[]{:S(2)}) async-start(f32[8,32,256]{2,1,0:T(8,128)} %broadcast_in_dim.14), calls=%async_computation.7 | async-start | bytes 524288 | tf_op jit(solution)/shard_map/all_to_all | solution.py:30

commit v9 on v8

--- a/solution.py
+++ b/solution.py
@@ -140,7 +140,7 @@
 def fetch_panels(flat, panels):
     received = exchange(flat, COL)
     mine = jnp.concatenate([lax.dynamic_index_in_dim(received, panel, 0, False) for panel in panels], axis=0)
-    both = gather(gather(mine, "y"), "x")
+    both = gather(mine, COL)
     return both.reshape(-1, len(panels), received.shape[1], PANEL)
 
 

time: 206 us -> 213 us (1.034)
  blocking collectives: 59.8 us -> 70.6 us
  starting transfers between devices: 57.4 us -> 53.8 us
    all_to_all x2 -> x1, blocking collectives: 41.4 us -> 51.3 us  [gather(): lax.all_to_all(copies.reshape((-1,) + value.shape[1:]), axis, 0, 0, tiled...]
    all_to_all x3, starting transfers between devices: 31.3 us -> 27.9 us  [exchange(): out = lax.all_to_all(value, axis, 0, 0, tiled=True)]
  transfers between devices with their start and end apart: 8 -> 8, of which waited for: 7 -> 7; matrix products, arithmetic and copies ran while one was open for 4% -> 4% of each run, Pallas kernels for 10% -> 9%
where the time goes in v9:
time: 213 us; the launch traced here: 212 us
  blocking collectives  70.6 us (33%)
  starting transfers between devices  53.8 us (25%)
  waiting for transfers between devices  34.9 us (16%)
  Pallas kernels  28.6 us (13%)
  matrix products  13.2 us (6%)
  between operations  6 us (3%)
  other arithmetic  2.94 us (1%)
  local copies, waits for them, and re-layouts  2.46 us (1%)
    all_to_all x1, blocking collectives, gather(): lax.all_to_all(copies.reshape((-1,) + value.shape[1:]), axis, 0, 0, tiled...  51.3 us
    all_to_all x3, starting transfers between devices, exchange(): out = lax.all_to_all(value, axis, 0, 0, tiled=True)  27.9 us
    all_to_all x3, waiting for transfers between devices, exchange(): out = lax.all_to_all(value, axis, 0, 0, tiled=True)  23 us
    pallas_call x3, Pallas kernels, on_chip(): pl.pallas_call(kernel, out_shape=[jax.ShapeDtypeStruct(shape, jnp.float32...  20.8 us
    ppermute x2, starting transfers between devices, halos(): out.append(lax.ppermute(edge, SITE, swap))  13.9 us
    all_to_all x1, blocking collectives, exchange(): out = lax.all_to_all(value, axis, 0, 0, tiled=True)  13.3 us
    all_to_all x2, starting transfers between devices, gather(): lax.all_to_all(copies.reshape((-1,) + value.shape[1:]), axis, 0, 0, tiled...  9.41 us
    all_to_all x2, waiting for transfers between devices, gather(): lax.all_to_all(copies.reshape((-1,) + value.shape[1:]), axis, 0, 0, tiled...  8.18 us
  transfers between devices with their start and end apart: 8, of which 7 were waited for; matrix products, arithmetic and copies ran while one was open for 4% of the time, Pallas kernels for 9%

profile of v9, /device:TPU:1, one launch (start us, length us, event | category | flops | bytes accessed | tf_op | source)
XLA Modules:
  0.0 212.4 jit_solution(2502041309405261853)
XLA Ops:
  0.6 2.1 shard_map.59
  2.8 5.5 %collective-permute-start = (f32[7,128,256]{2,1,0:T(8,128)}, f32[7,128,256]{2,1,0:T(8,128)S(1)}, u32[]{:S(2)}, u32[]{:S(2)}) collective-permute-start(f32[7,128,256]{2,1,0:T(8,128)} %shard_map.59), channel_id=1, source_target_pairs={{0,480},{32,64},{64,32},{96,128},{128,96},{160,192},{192,160},{224... | collective-permute-start | bytes 2752520 | tf_op jit(solution)/shard_map/ppermute | solution.py:61
  8.3 2.1 shard_map.60
  10.4 8.4 %collective-permute-start.1 = (f32[7,128,256]{2,1,0:T(8,128)}, f32[7,128,256]{2,1,0:T(8,128)S(1)}, u32[]{:S(2)}, u32[]{:S(2)}) collective-permute-start(f32[7,128,256]{2,1,0:T(8,128)} %shard_map.60), channel_id=1, source_target_pairs={{0,32},{32,0},{64,96},{96,64},{128,160},{160,128},{192,224},{224,1... | collective-permute-start | bytes 2752520 | tf_op jit(solution)/shard_map/ppermute | solution.py:61
  18.8 1.0 collective-permute-done.far_ref
  19.9 1.3 collective-permute-done.1.near_ref
  21.1 3.6 %shard_map.61 = f32[8,128,256]{2,1,0:T(8,128)} custom-call(f32[8,128,256]{2,1,0:T(8,128)S(1)} %copy-done, f32[8,128,256]{2,1,0:T(8,128)S(1)} %copy-done.1, f32[7,128,256]{2,1,0:T(8,128)S(1)} %collective-permute-done.far_ref, f32[7,128,256]{2,1,0:T(8,128)S(1)} %collective-permute-done.1.near_ref, s32[4,128,128]{2,1,0:T(8,128)S(1)} %copy-done.2), custom_call_target="tpu_custom_call" | custom-call | flops 12000000 | bytes 6000000 | tf_op jit(solution)/shard_map/pallas_call | solution.py:113
  24.8 9.7 %all-to-all-start = ((f32[32,32,256]{2,1,0:T(8,128)}), f32[32,32,256]{2,1,0:T(8,128)S(1)}, u32[]{:S(2)}, u32[]{:S(2)}) async-start(f32[32,32,256]{2,1,0:T(8,128)} %bitcast.3), calls=%async_computation | async-start | bytes 2097152 | tf_op jit(solution)/shard_map/all_to_all | solution.py:23
  38.9 14.8 %all-to-all-done = f32[32,32,256]{2,1,0:T(8,128)S(1)} async-done(((f32[32,32,256]{2,1,0:T(8,128)}), f32[32,32,256]{2,1,0:T(8,128)S(1)}, u32[]{:S(2)}, u32[]{:S(2)}) %all-to-all-start) | async-done | bytes 1048608 | tf_op jit(solution)/shard_map/all_to_all | solution.py:23
  54.0 51.3 %all_to_all.60 = f32[32,64,256]{2,1,0:T(8,128)S(1)} all-to-all(f32[32,64,256]{2,1,0:T(8,128)S(1)} %broadcast_in_dim.6), channel_id=1, replica_groups=mesh['z'=8,'core'=2,'x'=4,'y'=8] {'x','y'}, dimensions={0} | all-to-all | bytes 4194304 | tf_op jit(solution)/shard_map/all_to_all | solution.py:30
  105.4 3.0 %shard_map.62 = f32[640,256]{1,0:T(8,128)S(1)} custom-call(f32[32,2,32,256]{3,2,1,0:T(8,128)S(1)} %bitcast.33), custom_call_target="tpu_custom_call" | custom-call | flops 4000000000 | bytes 524288 | tf_op jit(solution)/shard_map/pallas_call | solution.py:284
  108.4 13.3 %all_to_all.61 = f32[2,320,256]{2,1,0:T(8,128)S(1)} all-to-all(f32[2,320,256]{2,1,0:T(8,128)S(1)} %bitcast.34), channel_id=1, replica_groups=mesh['z'=8,'core'=2,'x'=4,'y'=8] {'core'}, dimensions={0} | all-to-all | bytes 1310720 | tf_op jit(solution)/shard_map/all_to_all | solution.py:23
  121.7 0.8 reduce_sum.27
  122.4 14.6 %all-to-all-start.3 = ((f32[8,40,256]{2,1,0:T(8,128)}), f32[8,40,256]{2,1,0:T(8,128)S(1)}, u32[]{:S(2)}, u32[]{:S(2)}) async-start(f32[8,40,256]{2,1,0:T(8,128)} %bitcast.10), calls=%async_computation.3 | async-start | bytes 655360 | tf_op jit(solution)/shard_map/all_to_all | solution.py:23
  137.1 3.1 %fusion.22 = f32[256,256]{1,0:T(8,128)S(1)} fusion(f32[1024,256]{1,0:T(8,128)S(1)} %bitcast.37, f32[1024,256]{1,0:T(8,128)} %bitcast), kind=kOutput, calls=%fused_computation.32 | convolution fusion | flops 805306368 | bytes 2359296 | tf_op jit(solution)/shard_map/dot_general | solution.py:137
  140.2 3.1 %fusion.21 = f32[256,256]{1,0:T(8,128)S(1)} fusion(f32[1024,256]{1,0:T(8,128)S(1)} %bitcast.35, f32[1024,256]{1,0:T(8,128)} %bitcast), kind=kOutput, calls=%fused_computation.31 | convolution fusion | flops 805306368 | bytes 2359296 | tf_op jit(solution)/shard_map/dot_general | solution.py:137
  143.3 7.4 %all-to-all-done.3 = f32[8,40,256]{2,1,0:T(8,128)S(1)} async-done(((f32[8,40,256]{2,1,0:T(8,128)}), f32[8,40,256]{2,1,0:T(8,128)S(1)}, u32[]{:S(2)}, u32[]{:S(2)}) %all-to-all-start.3) | async-done | bytes 327712 | tf_op jit(solution)/shard_map/all_to_all | solution.py:23
  150.7 0.7 broadcast_in_dim.7
  151.4 3.4 %all-to-all-start.4 = ((f32[8,40,256]{2,1,0:T(8,128)}), f32[8,40,256]{2,1,0:T(8,128)S(1)}, u32[]{:S(2)}, u32[]{:S(2)}) async-start(f32[8,40,256]{2,1,0:T(8,128)} %broadcast_in_dim.7), calls=%async_computation.4 | async-start | bytes 655360 | tf_op jit(solution)/shard_map/all_to_all | solution.py:30
  154.9 0.8 fusion.13
  155.7 2.5 %collective-permute-start.2 = (f32[256,256]{1,0:T(8,128)}, f32[256,256]{1,0:T(8,128)S(1)}, u32[]{:S(2)}, u32[]{:S(2)}) collective-permute-start(f32[256,256]{1,0:T(8,128)} %fusion.13), channel_id=1, source_target_pairs={{0,32},{32,0},{1,33},{33,1},{2,34},{34,2},{3,35},{35,3},{4,36},{36... | collective-permute-start | bytes 786440 | tf_op jit(solution)/shard_map/ppermute | solution.py:128
  158.2 1.3 collective-permute-done.2
  159.5 0.8 fusion.15
  160.3 8.2 %all-to-all-done.4 = f32[8,40,256]{2,1,0:T(8,128)S(1)} async-done(((f32[8,40,256]{2,1,0:T(8,128)}), f32[8,40,256]{2,1,0:T(8,128)S(1)}, u32[]{:S(2)}, u32[]{:S(2)}) %all-to-all-start.4) | async-done | bytes 327712 | tf_op jit(solution)/shard_map/all_to_all | solution.py:30
  168.5 3.6 %all-to-all-start.5 = ((f32[8,32,256]{2,1,0:T(8,128)}), f32[8,32,256]{2,1,0:T(8,128)S(1)}, u32[]{:S(2)}, u32[]{:S(2)}) async-start(f32[8,32,256]{2,1,0:T(8,128)} %bitcast.41), calls=%async_computation.5 | async-start | bytes 524288 | tf_op jit(solution)/shard_map/all_to_all | solution.py:23
  172.1 2.5 %all_gather.6.gram_ref = f32[640,256]{1,0:T(8,128)S(1)} all-gather(f32[320,256]{1,0:T(8,128)S(1)} %bitcast.39), channel_id=1, replica_groups=mesh['z'=8,'core'=2,'x'=4,'y'=8] {'core'}, dimensions={0}, use_global_device_ids=true | all-gather | bytes 983040 | tf_op jit(solution)/shard_map/all_gather | solution.py:307
  174.5 8.3 %shard_map.63 = (f32[256,256]{1,0:T(8,128)S(1)}, f32[1,256]{1,0:T(1,128)S(1)}) custom-call(f32[640,256]{1,0:T(8,128)S(1)} %all_gather.6.gram_ref), custom_call_target="tpu_custom_call" | custom-call | flops 1000 | bytes 524288 | tf_op jit(solution)/shard_map/pallas_call | solution.py:284
  182.9 0.9 all-to-all-done.5
  184.5 6.0 %all-to-all-start.6 = ((f32[8,32,256]{2,1,0:T(8,128)}), f32[8,32,256]{2,1,0:T(8,128)}, u32[]{:S(2)}, u32[]{:S(2)}) async-start(f32[8,32,256]{2,1,0:T(8,128)} %broadcast_in_dim.8), calls=%async_computation.6 | async-start | bytes 524288 | tf_op jit(solution)/shard_map/all_to_all | solution.py:30
  191.8 9.4 %shard_map.64 = (f32[256,256]{1,0:T(8,128)S(1)}, f32[1,256]{1,0:T(1,128)S(1)}, f32[256,256]{1,0:T(8,128)S(1)}) custom-call(f32[640,256]{1,0:T(8,128)S(1)} %all_gather.6.gram_ref, f32[256,256]{1,0:T(8,128)S(1)} %get-tuple-element.22.inverse_ref), custom_call_target="tpu_custom_call" | custom-call | flops 1000 | bytes 524288 | tf_op jit(solution)/shard_map/pallas_call | solution.py:284
  201.8 3.6 %all_gather.7 = f32[512,256]{1,0:T(8,128)S(1)} all-gather(f32[256,256]{1,0:T(8,128)} %bitcast.13), channel_id=1, replica_groups=mesh['z'=8,'core'=2,'x'=4,'y'=8] {'core'}, dimensions={0}, use_global_device_ids=true | all-gather | bytes 786432 | tf_op jit(solution)/shard_map/all_gather | solution.py:314
  208.4 4.0 %multiply_subtract_fusion = f32[1024,256]{1,0:T(8,128)} fusion(f32[1024,256]{1,0:T(8,128)} %bitcast, f32[1024,256]{1,0:T(8,128)S(1)} %bitcast.38, f32[1024,256]{1,0:T(8,128)S(1)} %bitcast.36, f32[256,256]{1,0:T(8,128)S(1)} %fusion.23, f32[256,256]{1,0:T(8,128)S(1)} %fusion.24, f32[]{:T(128)S(6)} %select_n.39), kind=kOutput, calls=%fused_computation.9 | convolution fusion | flops 1611792384 | bytes 4718596 | tf_op jit(solution)/shard_map/dot_general | solution.py:132
  (24 shorter events, 5.3 us)
Async XLA Ops:
  2.7 18.4 %copy-start = (f32[8,128,256]{2,1,0:T(8,128)S(1)}, f32[8,128,256]{2,1,0:T(8,128)}, u32[]{:S(2)}) copy-start(f32[8,128,256]{2,1,0:T(8,128)} %previous_ref.5) | copy-start | bytes 3145732
  2.8 18.4 %copy-start.1 = (f32[8,128,256]{2,1,0:T(8,128)S(1)}, f32[8,128,256]{2,1,0:T(8,128)}, u32[]{:S(2)}) copy-start(f32[8,128,256]{2,1,0:T(8,128)} %current_ref.5) | copy-start | bytes 3145732
  2.8 18.4 %copy-start.2 = (s32[4,128,128]{2,1,0:T(8,128)S(1)}, s32[4,128,128]{2,1,0:T(8,128)}, u32[]{:S(2)}) copy-start(s32[4,128,128]{2,1,0:T(8,128)} %occupancy_ref.1) | copy-start | bytes 786436
  2.8 17.1 %collective-permute-start = (f32[7,128,256]{2,1,0:T(8,128)}, f32[7,128,256]{2,1,0:T(8,128)S(1)}, u32[]{:S(2)}, u32[]{:S(2)}) collective-permute-start(f32[7,128,256]{2,1,0:T(8,128)} %shard_map.59), channel_id=1, source_target_pairs={{0,480},{32,64},{64,32},{96,128},{128,96},{160,192},{192,160},{224... | collective-permute-start | bytes 2752520 | tf_op jit(solution)/shard_map/ppermute | solution.py:61
  10.4 10.7 %collective-permute-start.1 = (f32[7,128,256]{2,1,0:T(8,128)}, f32[7,128,256]{2,1,0:T(8,128)S(1)}, u32[]{:S(2)}, u32[]{:S(2)}) collective-permute-start(f32[7,128,256]{2,1,0:T(8,128)} %shard_map.60), channel_id=1, source_target_pairs={{0,32},{32,0},{64,96},{96,64},{128,160},{160,128},{192,224},{224,1... | collective-permute-start | bytes 2752520 | tf_op jit(solution)/shard_map/ppermute | solution.py:61
  24.7 9.7 %copy-start.3 = (s32[32]{0:T(128)S(1)}, s32[32]{0:T(128)}, u32[]{:S(2)}) copy-start(s32[32]{0:T(128)} %param.7) | copy-start | bytes 388
  24.8 28.9 %all-to-all-start = ((f32[32,32,256]{2,1,0:T(8,128)}), f32[32,32,256]{2,1,0:T(8,128)S(1)}, u32[]{:S(2)}, u32[]{:S(2)}) async-start(f32[32,32,256]{2,1,0:T(8,128)} %bitcast.3), calls=%async_computation | async-start | bytes 2097152 | tf_op jit(solution)/shard_map/all_to_all | solution.py:23
  122.4 28.3 %all-to-all-start.3 = ((f32[8,40,256]{2,1,0:T(8,128)}), f32[8,40,256]{2,1,0:T(8,128)S(1)}, u32[]{:S(2)}, u32[]{:S(2)}) async-start(f32[8,40,256]{2,1,0:T(8,128)} %bitcast.10), calls=%async_computation.3 | async-start | bytes 655360 | tf_op jit(solution)/shard_map/all_to_all | solution.py:23
  151.4 17.0 %all-to-all-start.4 = ((f32[8,40,256]{2,1,0:T(8,128)}), f32[8,40,256]{2,1,0:T(8,128)S(1)}, u32[]{:S(2)}, u32[]{:S(2)}) async-start(f32[8,40,256]{2,1,0:T(8,128)} %broadcast_in_dim.7), calls=%async_computation.4 | async-start | bytes 655360 | tf_op jit(solution)/shard_map/all_to_all | solution.py:30
  155.7 3.9 %collective-permute-start.2 = (f32[256,256]{1,0:T(8,128)}, f32[256,256]{1,0:T(8,128)S(1)}, u32[]{:S(2)}, u32[]{:S(2)}) collective-permute-start(f32[256,256]{1,0:T(8,128)} %fusion.13), channel_id=1, source_target_pairs={{0,32},{32,0},{1,33},{33,1},{2,34},{34,2},{3,35},{35,3},{4,36},{36... | collective-permute-start | bytes 786440 | tf_op jit(solution)/shard_map/ppermute | solution.py:128
  168.5 15.3 %all-to-all-start.5 = ((f32[8,32,256]{2,1,0:T(8,128)}), f32[8,32,256]{2,1,0:T(8,128)S(1)}, u32[]{:S(2)}, u32[]{:S(2)}) async-start(f32[8,32,256]{2,1,0:T(8,128)} %bitcast.41), calls=%async_computation.5 | async-start | bytes 524288 | tf_op jit(solution)/shard_map/all_to_all | solution.py:23
  184.5 17.3 %all-to-all-start.6 = ((f32[8,32,256]{2,1,0:T(8,128)}), f32[8,32,256]{2,1,0:T(8,128)}, u32[]{:S(2)}, u32[]{:S(2)}) async-start(f32[8,32,256]{2,1,0:T(8,128)} %broadcast_in_dim.8), calls=%async_computation.6 | async-start | bytes 524288 | tf_op jit(solution)/shard_map/all_to_all | solution.py:30

commit v10 on v8

--- a/solution.py
+++ b/solution.py
@@ -260,6 +260,14 @@
     out_ref[pl.ds(PANEL + half, PANEL), :] = product_t(a, b)
 
 
+def sum_copies_kernel(parts_ref, out_ref):
+    total = parts_ref[0]
+    for n in range(1, parts_ref.shape[0]):
+        total = total + parts_ref[n]
+    for n in range(out_ref.shape[0]):
+        out_ref[n] = total
+
+
 def first_kernel(gram_ref, out_ref, growth_ref):
     half = PANEL // 2
     out_ref[pl.ds(0, half), :] = gram_ref[pl.ds(0, half), :]
@@ -289,6 +297,11 @@
         compiler_params=pltpu.CompilerParams(vmem_limit_bytes=32 * 1024 * 1024),
         cost_estimate=pl.CostEstimate(flops=flops, bytes_accessed=524288, transcendentals=PANEL),
     )(*args)
+
+
+def sum_and_gather(parts, axis):
+    (copies,) = on_chip(sum_copies_kernel, 1000, parts.shape)(parts)
+    return lax.all_to_all(copies.reshape(-1, PANEL), axis, 0, 0, tiled=True)
 
 
 def on_device(state_prev, state_cur, occupancy, panel_order):
@@ -302,15 +315,15 @@
     gram = exchange(gram, "core").sum(axis=0)
     a_late, b_late, gram = lax.optimization_barrier((a, b, gram))
     inner = jnp.concatenate([product_t(a_late, flat), product_t(b_late, flat)], axis=0)
-    gram = gather(exchange(gram, "z").sum(axis=0), "z")
+    gram = sum_and_gather(exchange(gram, "z"), "z")
     inner, gram = lax.optimization_barrier((core_sum(inner), gram))
     gram = lax.all_gather(gram, "core", axis=0, tiled=True)
-    inner = exchange(inner, "z").sum(axis=0)
+    inner = exchange(inner, "z")
     square, row = (PANEL, PANEL), (1, PANEL)
     inverse_1, growth_1 = on_chip(first_kernel, 1000, square, row)(gram)
     inner, inverse_1 = lax.optimization_barrier((inner, inverse_1))
     inverse_2, growth_2, cross = on_chip(second_kernel, 1000, square, row, square)(gram, inverse_1)
-    inner, inverse_2 = lax.optimization_barrier((gather(inner, "z"), inverse_2))
+    inner, inverse_2 = lax.optimization_barrier((sum_and_gather(inner, "z"), inverse_2))
     inner = lax.all_gather(inner, "core", axis=0, tiled=True)
     ax, bx = inner[:PANEL], inner[PANEL:]
     inner_1 = product(inverse_1, ax)

time: 206 us -> 207 us (level)
    pallas_call x3 -> x5, Pallas kernels: 20.8 us -> 22.3 us  [on_chip(): pl.pallas_call(kernel, out_shape=[jax.ShapeDtypeStruct(shape, jnp.float32...]
where the time goes in v10:
time: 207 us; the launch traced here: 206 us
  blocking collectives  60 us (29%)
  starting transfers between devices  57.6 us (28%)
  waiting for transfers between devices  35.1 us (17%)
  Pallas kernels  30.1 us (15%)
  matrix products  13 us (6%)
  between operations  6.16 us (3%)
  other arithmetic  2.25 us (1%)
    all_to_all x2, blocking collectives, gather(): lax.all_to_all(copies.reshape((-1,) + value.shape[1:]), axis, 0, 0, tiled...  41.4 us
    all_to_all x3, starting transfers between devices, exchange(): out = lax.all_to_all(value, axis, 0, 0, tiled=True)  31.3 us
    all_to_all x3, waiting for transfers between devices, exchange(): out = lax.all_to_all(value, axis, 0, 0, tiled=True)  22.6 us
    pallas_call x5, Pallas kernels, on_chip(): pl.pallas_call(kernel, out_shape=[jax.ShapeDtypeStruct(shape, jnp.float32...  22.3 us
    ppermute x2, starting transfers between devices, halos(): out.append(lax.ppermute(edge, SITE, swap))  13.9 us
    all_to_all x1, blocking collectives, exchange(): out = lax.all_to_all(value, axis, 0, 0, tiled=True)  12.1 us
    all_to_all x2, starting transfers between devices, sum_and_gather(): return lax.all_to_all(copies.reshape(-1, PANEL), axis, 0, 0, tiled=True)  9.8 us
    all_to_all x2, waiting for transfers between devices, sum_and_gather(): return lax.all_to_all(copies.reshape(-1, PANEL), axis, 0, 0, tiled=True)  9.04 us
  transfers between devices with their start and end apart: 8, of which 7 were waited for; matrix products, arithmetic and copies ran while one was open for 4% of the time, Pallas kernels for 10%

profile of v10, /device:TPU:1, one launch (start us, length us, event | category | flops | bytes accessed | tf_op | source)
XLA Modules:
  0.0 206.1 jit_solution(5833603133379663858)
XLA Ops:
  0.6 2.1 %shard_map.59 = f32[7,128,256]{2,1,0:T(8,128)} custom-call(f32[8,128,256]{2,1,0:T(8,128)} %previous_ref.5, f32[8,128,256]{2,1,0:T(8,128)} %current_ref.5), custom_call_target="tpu_custom_call" | custom-call | tf_op jit(solution)/shard_map/pallas_call | solution.py:53
  2.8 5.5 %collective-permute-start = (f32[7,128,256]{2,1,0:T(8,128)}, f32[7,128,256]{2,1,0:T(8,128)S(1)}, u32[]{:S(2)}, u32[]{:S(2)}) collective-permute-start(f32[7,128,256]{2,1,0:T(8,128)} %shard_map.59), channel_id=1, source_target_pairs={{0,480},{32,64},{64,32},{96,128},{128,96},{160,192},{192,160},{224... | collective-permute-start | bytes 2752520 | tf_op jit(solution)/shard_map/ppermute | solution.py:61
  8.3 2.1 %shard_map.60 = f32[7,128,256]{2,1,0:T(8,128)} custom-call(f32[8,128,256]{2,1,0:T(8,128)} %previous_ref.5, f32[8,128,256]{2,1,0:T(8,128)} %current_ref.5), custom_call_target="tpu_custom_call" | custom-call | tf_op jit(solution)/shard_map/pallas_call | solution.py:53
  10.4 8.4 %collective-permute-start.1 = (f32[7,128,256]{2,1,0:T(8,128)}, f32[7,128,256]{2,1,0:T(8,128)S(1)}, u32[]{:S(2)}, u32[]{:S(2)}) collective-permute-start(f32[7,128,256]{2,1,0:T(8,128)} %shard_map.60), channel_id=1, source_target_pairs={{0,32},{32,0},{64,96},{96,64},{128,160},{160,128},{192,224},{224,1... | collective-permute-start | bytes 2752520 | tf_op jit(solution)/shard_map/ppermute | solution.py:61
  18.9 1.0 collective-permute-done.far_ref
  19.9 1.3 collective-permute-done.1.near_ref
  21.2 3.6 %shard_map.61 = f32[8,128,256]{2,1,0:T(8,128)} custom-call(f32[8,128,256]{2,1,0:T(8,128)S(1)} %copy-done, f32[8,128,256]{2,1,0:T(8,128)S(1)} %copy-done.1, f32[7,128,256]{2,1,0:T(8,128)S(1)} %collective-permute-done.far_ref, f32[7,128,256]{2,1,0:T(8,128)S(1)} %collective-permute-done.1.near_ref, s32[4,128,128]{2,1,0:T(8,128)S(1)} %copy-done.2), custom_call_target="tpu_custom_call" | custom-call | flops 12000000 | bytes 6000000 | tf_op jit(solution)/shard_map/pallas_call | solution.py:113
  24.8 9.7 %all-to-all-start = ((f32[32,32,256]{2,1,0:T(8,128)}), f32[32,32,256]{2,1,0:T(8,128)S(1)}, u32[]{:S(2)}, u32[]{:S(2)}) async-start(f32[32,32,256]{2,1,0:T(8,128)} %bitcast.3), calls=%async_computation | async-start | bytes 2097152 | tf_op jit(solution)/shard_map/all_to_all | solution.py:23
  39.1 14.6 %all-to-all-done = f32[32,32,256]{2,1,0:T(8,128)S(1)} async-done(((f32[32,32,256]{2,1,0:T(8,128)}), f32[32,32,256]{2,1,0:T(8,128)S(1)}, u32[]{:S(2)}, u32[]{:S(2)}) %all-to-all-start) | async-done | bytes 1048608 | tf_op jit(solution)/shard_map/all_to_all | solution.py:23
  53.8 19.5 %all_to_all.66 = f32[8,64,256]{2,1,0:T(8,128)S(1)} all-to-all(f32[8,64,256]{2,1,0:T(8,128)S(1)} %broadcast_in_dim.6), channel_id=1, replica_groups=mesh['z'=8,'core'=2,'x'=4,'y'=8] {'y'}, dimensions={0} | all-to-all | bytes 1048576 | tf_op jit(solution)/shard_map/all_to_all | solution.py:30
  73.4 21.9 %all_to_all.67 = f32[4,512,256]{2,1,0:T(8,128)S(1)} all-to-all(f32[4,512,256]{2,1,0:T(8,128)S(1)} %broadcast_in_dim.8), channel_id=1, replica_groups=mesh['z'=8,'core'=2,'x'=4,'y'=8] {'x'}, dimensions={0} | all-to-all | bytes 4194304 | tf_op jit(solution)/shard_map/all_to_all | solution.py:30
  95.6 3.0 %shard_map.62 = f32[640,256]{1,0:T(8,128)S(1)} custom-call(f32[32,2,32,256]{3,2,1,0:T(8,128)S(1)} %bitcast.34), custom_call_target="tpu_custom_call" | custom-call | flops 4000000000 | bytes 524288 | tf_op jit(solution)/shard_map/pallas_call | solution.py:292
  98.6 12.1 %all_to_all.68 = f32[2,320,256]{2,1,0:T(8,128)S(1)} all-to-all(f32[2,320,256]{2,1,0:T(8,128)S(1)} %bitcast.35), channel_id=1, replica_groups=mesh['z'=8,'core'=2,'x'=4,'y'=8] {'core'}, dimensions={0} | all-to-all | bytes 1310720 | tf_op jit(solution)/shard_map/all_to_all | solution.py:23
  110.8 0.8 reduce_sum.9
  111.6 18.2 %all-to-all-start.4 = ((f32[8,40,256]{2,1,0:T(8,128)}), f32[8,40,256]{2,1,0:T(8,128)S(1)}, u32[]{:S(2)}, u32[]{:S(2)}) async-start(f32[8,40,256]{2,1,0:T(8,128)} %bitcast.11), calls=%async_computation.4 | async-start | bytes 655360 | tf_op jit(solution)/shard_map/all_to_all | solution.py:23
  129.8 3.0 %fusion.22 = f32[256,256]{1,0:T(8,128)S(1)} fusion(f32[1024,256]{1,0:T(8,128)S(1)} %bitcast.38, f32[1024,256]{1,0:T(8,128)} %bitcast), kind=kOutput, calls=%fused_computation.32 | convolution fusion | flops 805306368 | bytes 2359296 | tf_op jit(solution)/shard_map/dot_general | solution.py:137
  132.8 3.0 %fusion.21 = f32[256,256]{1,0:T(8,128)S(1)} fusion(f32[1024,256]{1,0:T(8,128)S(1)} %bitcast.36, f32[1024,256]{1,0:T(8,128)} %bitcast), kind=kOutput, calls=%fused_computation.31 | convolution fusion | flops 805306368 | bytes 2359296 | tf_op jit(solution)/shard_map/dot_general | solution.py:137
  135.9 7.5 %all-to-all-done.4.parts_ref = f32[8,40,256]{2,1,0:T(8,128)S(1)} async-done(((f32[8,40,256]{2,1,0:T(8,128)}), f32[8,40,256]{2,1,0:T(8,128)S(1)}, u32[]{:S(2)}, u32[]{:S(2)}) %all-to-all-start.4) | async-done | bytes 327712 | tf_op jit(solution)/shard_map/all_to_all | solution.py:23
  143.4 0.8 shard_map.63
  144.2 3.4 %all-to-all-start.5 = ((f32[8,40,256]{2,1,0:T(8,128)}), f32[8,40,256]{2,1,0:T(8,128)S(1)}, u32[]{:S(2)}, u32[]{:S(2)}) async-start(f32[8,40,256]{2,1,0:T(8,128)} %shard_map.63), calls=%async_computation.5 | async-start | bytes 655360 | tf_op jit(solution)/shard_map/all_to_all | solution.py:304
  147.7 2.5 %collective-permute-start.2 = (f32[256,256]{1,0:T(8,128)S(1)}, f32[256,256]{1,0:T(8,128)S(1)}, u32[]{:S(2)}, u32[]{:S(2)}) collective-permute-start(f32[256,256]{1,0:T(8,128)S(1)} %fusion.13), channel_id=1, source_target_pairs={{0,32},{32,0},{1,33},{33,1},{2,34},{34,2},{3,35},{35,3},{4,36},{36... | collective-permute-start | bytes 786440 | tf_op jit(solution)/shard_map/ppermute | solution.py:128
  150.2 1.1 collective-permute-done.2
  151.4 0.8 fusion.15
  152.2 9.0 %all-to-all-done.5 = f32[8,40,256]{2,1,0:T(8,128)S(1)} async-done(((f32[8,40,256]{2,1,0:T(8,128)}), f32[8,40,256]{2,1,0:T(8,128)S(1)}, u32[]{:S(2)}, u32[]{:S(2)}) %all-to-all-start.5) | async-done | bytes 327712 | tf_op jit(solution)/shard_map/all_to_all | solution.py:304
  161.2 0.7 copy-done.3
  161.9 3.4 %all-to-all-start.6 = ((f32[8,32,256]{2,1,0:T(8,128)}), f32[8,32,256]{2,1,0:T(8,128)S(1)}, u32[]{:S(2)}, u32[]{:S(2)}) async-start(f32[8,32,256]{2,1,0:T(8,128)} %bitcast.13), calls=%async_computation.6 | async-start | bytes 524288 | tf_op jit(solution)/shard_map/all_to_all | solution.py:23
  165.4 2.8 %all_gather.6.gram_ref = f32[640,256]{1,0:T(8,128)S(1)} all-gather(f32[320,256]{1,0:T(8,128)} %bitcast.41), channel_id=1, replica_groups=mesh['z'=8,'core'=2,'x'=4,'y'=8] {'core'}, dimensions={0}, use_global_device_ids=true | all-gather | bytes 983040 | tf_op jit(solution)/shard_map/all_gather | solution.py:320
  168.2 8.3 %shard_map.64 = (f32[256,256]{1,0:T(8,128)S(1)}, f32[1,256]{1,0:T(1,128)S(1)}) custom-call(f32[640,256]{1,0:T(8,128)S(1)} %all_gather.6.gram_ref), custom_call_target="tpu_custom_call" | custom-call | flops 1000 | bytes 524288 | tf_op jit(solution)/shard_map/pallas_call | solution.py:292
  177.8 6.4 %all-to-all-start.7 = ((f32[8,32,256]{2,1,0:T(8,128)}), f32[8,32,256]{2,1,0:T(8,128)}, u32[]{:S(2)}, u32[]{:S(2)}) async-start(f32[8,32,256]{2,1,0:T(8,128)} %shard_map.65), calls=%async_computation.7 | async-start | bytes 524288 | tf_op jit(solution)/shard_map/all_to_all | solution.py:304
  185.4 9.4 %shard_map.66 = (f32[256,256]{1,0:T(8,128)S(1)}, f32[1,256]{1,0:T(1,128)S(1)}, f32[256,256]{1,0:T(8,128)S(1)}) custom-call(f32[640,256]{1,0:T(8,128)S(1)} %all_gather.6.gram_ref, f32[256,256]{1,0:T(8,128)S(1)} %get-tuple-element.22.inverse_ref), custom_call_target="tpu_custom_call" | custom-call | flops 1000 | bytes 524288 | tf_op jit(solution)/shard_map/pallas_call | solution.py:292
  195.5 3.6 %all_gather.7 = f32[512,256]{1,0:T(8,128)S(1)} all-gather(f32[256,256]{1,0:T(8,128)} %bitcast.14), channel_id=1, replica_groups=mesh['z'=8,'core'=2,'x'=4,'y'=8] {'core'}, dimensions={0}, use_global_device_ids=true | all-gather | bytes 786432 | tf_op jit(solution)/shard_map/all_gather | solution.py:327
  202.1 4.0 %multiply_subtract_fusion = f32[1024,256]{1,0:T(8,128)} fusion(f32[1024,256]{1,0:T(8,128)} %bitcast, f32[1024,256]{1,0:T(8,128)S(1)} %bitcast.39, f32[1024,256]{1,0:T(8,128)S(1)} %bitcast.37, f32[256,256]{1,0:T(8,128)S(1)} %fusion.23, f32[256,256]{1,0:T(8,128)S(1)} %fusion.24, f32[]{:T(128)S(6)} %select_n.39), kind=kOutput, calls=%fused_computation.9 | convolution fusion | flops 1611792384 | bytes 4718596 | tf_op jit(solution)/shard_map/dot_general | solution.py:132
  (26 shorter events, 5.9 us)
Async XLA Ops:
  2.7 18.4 %copy-start = (f32[8,128,256]{2,1,0:T(8,128)S(1)}, f32[8,128,256]{2,1,0:T(8,128)}, u32[]{:S(2)}) copy-start(f32[8,128,256]{2,1,0:T(8,128)} %previous_ref.5) | copy-start | bytes 3145732
  2.8 18.4 %copy-start.1 = (f32[8,128,256]{2,1,0:T(8,128)S(1)}, f32[8,128,256]{2,1,0:T(8,128)}, u32[]{:S(2)}) copy-start(f32[8,128,256]{2,1,0:T(8,128)} %current_ref.5) | copy-start | bytes 3145732
  2.8 18.4 %copy-start.2 = (s32[4,128,128]{2,1,0:T(8,128)S(1)}, s32[4,128,128]{2,1,0:T(8,128)}, u32[]{:S(2)}) copy-start(s32[4,128,128]{2,1,0:T(8,128)} %occupancy_ref.1) | copy-start | bytes 786436
  2.8 17.1 %collective-permute-start = (f32[7,128,256]{2,1,0:T(8,128)}, f32[7,128,256]{2,1,0:T(8,128)S(1)}, u32[]{:S(2)}, u32[]{:S(2)}) collective-permute-start(f32[7,128,256]{2,1,0:T(8,128)} %shard_map.59), channel_id=1, source_target_pairs={{0,480},{32,64},{64,32},{96,128},{128,96},{160,192},{192,160},{224... | collective-permute-start | bytes 2752520 | tf_op jit(solution)/shard_map/ppermute | solution.py:61
  10.4 10.7 %collective-permute-start.1 = (f32[7,128,256]{2,1,0:T(8,128)}, f32[7,128,256]{2,1,0:T(8,128)S(1)}, u32[]{:S(2)}, u32[]{:S(2)}) collective-permute-start(f32[7,128,256]{2,1,0:T(8,128)} %shard_map.60), channel_id=1, source_target_pairs={{0,32},{32,0},{64,96},{96,64},{128,160},{160,128},{192,224},{224,1... | collective-permute-start | bytes 2752520 | tf_op jit(solution)/shard_map/ppermute | solution.py:61
  24.8 9.7 %copy-start.4 = (s32[32]{0:T(128)S(1)}, s32[32]{0:T(128)}, u32[]{:S(2)}) copy-start(s32[32]{0:T(128)} %param.7) | copy-start | bytes 388
  24.8 28.9 %all-to-all-start = ((f32[32,32,256]{2,1,0:T(8,128)}), f32[32,32,256]{2,1,0:T(8,128)S(1)}, u32[]{:S(2)}, u32[]{:S(2)}) async-start(f32[32,32,256]{2,1,0:T(8,128)} %bitcast.3), calls=%async_computation | async-start | bytes 2097152 | tf_op jit(solution)/shard_map/all_to_all | solution.py:23
  111.6 31.8 %all-to-all-start.4 = ((f32[8,40,256]{2,1,0:T(8,128)}), f32[8,40,256]{2,1,0:T(8,128)S(1)}, u32[]{:S(2)}, u32[]{:S(2)}) async-start(f32[8,40,256]{2,1,0:T(8,128)} %bitcast.11), calls=%async_computation.4 | async-start | bytes 655360 | tf_op jit(solution)/shard_map/all_to_all | solution.py:23
  144.2 17.0 %all-to-all-start.5 = ((f32[8,40,256]{2,1,0:T(8,128)}), f32[8,40,256]{2,1,0:T(8,128)S(1)}, u32[]{:S(2)}, u32[]{:S(2)}) async-start(f32[8,40,256]{2,1,0:T(8,128)} %shard_map.63), calls=%async_computation.5 | async-start | bytes 655360 | tf_op jit(solution)/shard_map/all_to_all | solution.py:304
  147.7 3.7 %collective-permute-start.2 = (f32[256,256]{1,0:T(8,128)S(1)}, f32[256,256]{1,0:T(8,128)S(1)}, u32[]{:S(2)}, u32[]{:S(2)}) collective-permute-start(f32[256,256]{1,0:T(8,128)S(1)} %fusion.13), channel_id=1, source_target_pairs={{0,32},{32,0},{1,33},{33,1},{2,34},{34,2},{3,35},{35,3},{4,36},{36... | collective-permute-start | bytes 786440 | tf_op jit(solution)/shard_map/ppermute | solution.py:128
  161.2 0.7 copy-start.3
  161.9 15.1 %all-to-all-start.6 = ((f32[8,32,256]{2,1,0:T(8,128)}), f32[8,32,256]{2,1,0:T(8,128)S(1)}, u32[]{:S(2)}, u32[]{:S(2)}) async-start(f32[8,32,256]{2,1,0:T(8,128)} %bitcast.13), calls=%async_computation.6 | async-start | bytes 524288 | tf_op jit(solution)/shard_map/all_to_all | solution.py:23
  177.8 17.7 %all-to-all-start.7 = ((f32[8,32,256]{2,1,0:T(8,128)}), f32[8,32,256]{2,1,0:T(8,128)}, u32[]{:S(2)}, u32[]{:S(2)}) async-start(f32[8,32,256]{2,1,0:T(8,128)} %shard_map.65), calls=%async_computation.7 | async-start | bytes 524288 | tf_op jit(solution)/shard_map/all_to_all | solution.py:304
